TPU v7x, 32 devices: a whole 2x2x4 slice. The times are simulated.
32 devices in a mesh: row: 8 (over z, y), col: 4 (over x, core).
Axes of the slice: x: 2, y: 2, z: 4, core: 2. Of those that a mesh axis runs over, the one named last changes fastest.
Arguments:
- amplitude: float32 [128, 256, 256], P(('row', 'col')), may hold values from 0.1 to 3
- patches: float32 [128, 2, 256, 256], P(('row', 'col')), may hold values from -5 to 5
- dual: float32 [128, 3, 2, 256, 256], P(('row', 'col')), may hold values from -3 to 3
- probe: float32 [3, 2, 256, 256], replicated, may hold values from -6 to 6
- obj: float32 [2, 6144, 3072], P(None, 'row', 'col'), may hold values from -5 to 5
- positions: int32 [128, 2], P(('row', 'col')), may hold values from 0 to 5888, as said below
Outputs:
- dual_new: float32 [128, 3, 2, 256, 256], P(('row', 'col'))
- object_new: float32 [2, 6144, 3072], P(None, 'row', 'col')
- probe_new: float32 [3, 2, 256, 256], replicated
- patches_new: float32 [128, 2, 256, 256], P(('row', 'col'))
Inputs may be any that keep to these rules, and one draw needn't show every extreme that they name: `positions`: both entries of each row are multiples of 128. A frame held by the device at index i of row and j of col has its row offset between i * 768 and (i + 1) * 768 - 128 and its column offset between j * 768 and (j + 1) * 768 - 128; every frame lies inside the object.
All inputs are finite; a program needn't handle non-finite values.
Results may differ from a plain program's by a relative error of at most 0.0003.
Values sent between devices are 32-bit elements; how exact they have to be, the bound alone decides.
No kernel may reach another device: no remote copies, remote signals or barrier semaphores. Data moves between devices by JAX's collectives and lax.ppermute only.
A program may use at most 192 MiB of HBM per device.

v0:
```python
import functools
import math

import jax
import jax.numpy as jnp
import numpy as np
from jax import lax
from jax.experimental import pallas as pl
from jax.experimental.pallas import tpu as pltpu
from jax.sharding import PartitionSpec as P

SWEEPS = 4
HALO = 8

amp_floor = 1.0
obj_weight = 0.5
smooth_weight = 16.0
probe_weight = 1.0

VMEM_SPEC = pl.BlockSpec(memory_space=pltpu.VMEM)
VMEM_LIMIT = 60 * 1024 * 1024


def shift(block, axis, distance):
    count = lax.axis_size(axis)
    route = [(i, i + distance) for i in range(count) if 0 <= i + distance < count]
    return lax.ppermute(block, axis, route)


def split_two(value):
    high = value.astype(jnp.bfloat16)
    low = (value - high.astype(jnp.float32)).astype(jnp.bfloat16)
    return high, low


def dft_weights(width):
    half = width // 2
    k = np.arange(half)[:, None]
    j = np.arange(half)[None, :]
    mats = []
    for parity in range(2):
        angle = 2.0 * math.pi * ((k * (2 * j + parity)) % width) / width
        re = np.cos(angle) / math.sqrt(width)
        im = -np.sin(angle) / math.sqrt(width)
        mats.append(np.block([[re, im], [-im, re]]))
    mats = mats + [m.T for m in mats]
    right, left = [], []
    for m in mats:
        high = m.astype(np.float32).astype(jnp.bfloat16)
        low = (m - high.astype(np.float64)).astype(np.float32).astype(jnp.bfloat16)
        right.append(np.concatenate([high, high, low], axis=0))
        left.append(np.concatenate([high, low, high], axis=1))
    order = np.concatenate([np.arange(0, width, 2), np.arange(1, width, 2)])
    perm = np.zeros((width, width), np.float32)
    perm[order, np.arange(width)] = 1.0
    right = np.stack(right)
    left = np.stack([left[2], left[3], left[0], left[1]])
    return right, left, perm.astype(jnp.bfloat16)


def frames_kernel(
    place_ref, amp_low_ref, amp_high_ref, patch_ref, dual_ref, probe_ref, right_ref, left_ref, perm_ref,
    new_ref, num_ref, canvas_ref, even_ref, odd_ref,
):
    frame = pl.program_id(0)
    modes = probe_ref.shape[0]
    width = probe_ref.shape[-1]
    half = width // 2

    @pl.when(frame == 0)
    def _():
        canvas_ref[...] = jnp.zeros_like(canvas_ref)
        num_ref[...] = jnp.zeros_like(num_ref)

    def dot(a, b):
        return jnp.dot(a, b, preferred_element_type=jnp.float32)

    def times_right(value, which):
        high, low = split_two(value)
        return dot(jnp.concatenate([high, low, high], axis=1), right_ref[which])

    def times_left(which, value):
        high, low = split_two(value)
        return dot(left_ref[which], jnp.concatenate([high, high, low], axis=0))

    patch_re = patch_ref[0, 0]
    patch_im = patch_ref[0, 1]

    def exit_wave(m):
        probe_re = probe_ref[m, 0]
        probe_im = probe_ref[m, 1]
        return probe_re * patch_re - probe_im * patch_im, probe_re * patch_im + probe_im * patch_re

    amps = []
    for parity in range(2):
        every = pl.ds(parity, half, stride=2)
        rows = jnp.concatenate([amp_low_ref[0, every, :], amp_high_ref[0, every, :]], axis=1)
        first = rows.astype(jnp.bfloat16)
        rest = rows - first.astype(jnp.float32)
        second, third = split_two(rest)
        amps.append(dot(first, perm_ref[...]) + (dot(second, perm_ref[...]) + dot(third, perm_ref[...])))

    power = [None, None]
    for m in range(modes):
        exit_re, exit_im = exit_wave(m)
        wave_re = exit_re + dual_ref[0, m, 0]
        wave_im = exit_im + dual_ref[0, m, 1]
        sums = jnp.concatenate(
            [wave_re[:, :half] + wave_re[:, half:], wave_im[:, :half] + wave_im[:, half:]], axis=1
        )
        diffs = jnp.concatenate(
            [wave_re[:, :half] - wave_re[:, half:], wave_im[:, :half] - wave_im[:, half:]], axis=1
        )
        even = times_right(sums, 0)
        odd = times_right(diffs, 1)

        def stack(op):
            return jnp.concatenate(
                [
                    jnp.concatenate([op(x[:half, part], x[half:, part]) for x in (even, odd)], axis=1)
                    for part in (slice(0, half), slice(half, width))
                ],
                axis=0,
            )

        far_even = times_left(0, stack(lambda a, b: a + b))
        far_odd = times_left(1, stack(lambda a, b: a - b))
        even_ref[m] = far_even
        odd_ref[m] = far_odd
        for parity, far in enumerate((far_even, far_odd)):
            term = far[:half] * far[:half] + far[half:] * far[half:]
            power[parity] = term if m == 0 else power[parity] + term

    ratios = []
    for parity in range(2):
        ratio = amps[parity] / jnp.sqrt(power[parity] + amp_floor)
        ratios.append(jnp.concatenate([ratio, ratio], axis=0))

    start_row = pl.multiple_of(place_ref[frame, 0], half)
    start_col = pl.multiple_of(place_ref[frame, 1], half)
    obj_re = jnp.zeros((width, width), jnp.float32)
    obj_im = jnp.zeros((width, width), jnp.float32)
    for m in range(modes):
        even = times_left(2, even_ref[m] * ratios[0])
        odd = times_left(3, odd_ref[m] * ratios[1])
        top = even + odd
        bottom = even - odd

        def rows_of(part):
            return jnp.concatenate(
                [
                    jnp.concatenate([x[:half, part], x[half:, part]], axis=1)
                    for x in (top, bottom)
                ],
                axis=0,
            )

        even = times_right(rows_of(slice(0, half)), 2)
        odd = times_right(rows_of(slice(half, width)), 3)
        low = even + odd
        high = even - odd
        near_re = jnp.concatenate([low[:, :half], high[:, :half]], axis=1)
        near_im = jnp.concatenate([low[:, half:], high[:, half:]], axis=1)
        exit_re, exit_im = exit_wave(m)
        new_re = dual_ref[0, m, 0] + exit_re - near_re
        new_im = dual_ref[0, m, 1] + exit_im - near_im
        new_ref[0, m, 0] = new_re
        new_ref[0, m, 1] = new_im
        target_re = near_re - new_re
        target_im = near_im - new_im
        num_ref[2 * m] += patch_re * target_re + patch_im * target_im
        num_ref[2 * m + 1] += patch_re * target_im - patch_im * target_re
        probe_re = probe_ref[m, 0]
        probe_im = probe_ref[m, 1]
        obj_re += probe_re * target_re + probe_im * target_im
        obj_im += probe_re * target_im - probe_im * target_re
    num_ref[2 * modes] += patch_re * patch_re + patch_im * patch_im
    canvas_ref[0, pl.ds(start_row, width), pl.ds(start_col, width)] += obj_re
    canvas_ref[1, pl.ds(start_row, width), pl.ds(start_col, width)] += obj_im


def frames_update(amplitude, patches, dual, probe, places, tile):
    count, modes = dual.shape[:2]
    width = amplitude.shape[-1]
    right, left, perm = dft_weights(width)
    grow = tile + width // 2

    def whole(shape):
        return pl.BlockSpec(shape, lambda f, *_: (0,) * len(shape))

    return pl.pallas_call(
        frames_kernel,
        out_shape=(
            jax.ShapeDtypeStruct(dual.shape, jnp.float32),
            jax.ShapeDtypeStruct((2 * modes + 1, width, width), jnp.float32),
            jax.ShapeDtypeStruct((2, grow, grow), jnp.float32),
        ),
        grid_spec=pltpu.PrefetchScalarGridSpec(
            num_scalar_prefetch=1,
            grid=(count,),
            in_specs=[
                pl.BlockSpec((1, width, width // 2), lambda f, *_: (f, 0, 0)),
                pl.BlockSpec((1, width, width // 2), lambda f, *_: (f, 0, 1)),
                pl.BlockSpec((1, 2, width, width), lambda f, *_: (f, 0, 0, 0)),
                pl.BlockSpec((1, modes, 2, width, width), lambda f, *_: (f, 0, 0, 0, 0)),
                whole(probe.shape),
                whole(right.shape),
                whole(left.shape),
                whole(perm.shape),
            ],
            out_specs=[
                pl.BlockSpec((1, modes, 2, width, width), lambda f, *_: (f, 0, 0, 0, 0)),
                whole((2 * modes + 1, width, width)),
                whole((2, grow, grow)),
            ],
            scratch_shapes=[
                pltpu.VMEM((modes, width, width), jnp.float32),
                pltpu.VMEM((modes, width, width), jnp.float32),
            ],
        ),
        compiler_params=pltpu.CompilerParams(vmem_limit_bytes=VMEM_LIMIT),
        cost_estimate=pl.CostEstimate(
            flops=count * modes * 24 * 2 * width**3, bytes_accessed=20 << 20, transcendentals=0
        ),
        name="frames",
    )(places, amplitude, amplitude, patches, dual, probe, jnp.asarray(right), jnp.asarray(left), jnp.asarray(perm))


def lane_of(shape):
    return lax.broadcasted_iota(jnp.int32, shape, len(shape) - 1)


def edge_block(right_part, left_part):
    lane = lane_of(right_part.shape)
    width = right_part.shape[-1]
    return jnp.where(lane < HALO, right_part, jnp.where(lane >= width - HALO, left_part, 0.0))


def weights_kernel(place_ref, bound_ref, probe_ref, out_ref, sums_ref):
    modes = probe_ref.shape[0]
    width = probe_ref.shape[-1]
    half = width // 2
    rows = out_ref.shape[0]
    tile = rows - 2 * HALO
    power = jnp.zeros((width, width), jnp.float32)
    for m in range(modes):
        power += probe_ref[m, 0] * probe_ref[m, 0] + probe_ref[m, 1] * probe_ref[m, 1]
    sums_ref[...] = jnp.zeros_like(sums_ref)

    def place(frame, carry):
        row = place_ref[frame, 0]
        col = place_ref[frame, 1]

        @pl.when((row >= -width) & (row <= tile) & (col >= -width) & (col <= tile))
        def _():
            at_row = pl.ds(pl.multiple_of(row + width, half), width)
            at_col = pl.ds(pl.multiple_of(col + width, half), width)
            sums_ref[at_row, at_col] += power

        return carry

    lax.fori_loop(0, place_ref.shape[0], place, 0)
    low_row, high_row, low_col, high_col = (bound_ref[n] for n in range(4))

    chunk = 56

    def finish(step, carry):
        base = pl.multiple_of(step * chunk, 8)
        at = pl.ds(pl.multiple_of(base + width - HALO, 8), chunk)
        den = jnp.concatenate(
            [
                sums_ref[at, width : width + tile],
                edge_block(sums_ref[at, width + tile : width + tile + half], sums_ref[at, half:width]),
            ],
            axis=1,
        )
        row = lax.broadcasted_iota(jnp.int32, den.shape, 0) + (base - HALO)
        lane = lane_of(den.shape)
        col = jnp.where(lane >= tile + half - HALO, lane - (tile + half), lane)
        inside = (row >= low_row) & (row < high_row) & (col >= low_col) & (col < high_col)
        out_ref[pl.ds(base, chunk), :] = jnp.where(
            inside, 1.0 / (den + (obj_weight + 4.0 * smooth_weight)), 0.0
        )
        return carry

    lax.fori_loop(0, rows // chunk, finish, 0)


def object_weights(places, bounds, probe, tile):
    width = probe.shape[-1]
    smem = pl.BlockSpec(memory_space=pltpu.SMEM)
    return pl.pallas_call(
        weights_kernel,
        out_shape=jax.ShapeDtypeStruct((tile + 2 * HALO, tile + width // 2), jnp.float32),
        in_specs=[smem, smem, VMEM_SPEC],
        out_specs=VMEM_SPEC,
        scratch_shapes=[pltpu.VMEM((tile + 2 * width, tile + 2 * width), jnp.float32)],
        compiler_params=pltpu.CompilerParams(vmem_limit_bytes=VMEM_LIMIT),
        name="weights",
    )(places, bounds, probe)


def columns_kernel(
    lead_ref, trail_ref, last_ref, beyond_ref, head_ref, left_ref, right_ref, lead_out, trail_out, down_out, up_out
):
    half = lead_ref.shape[-1]
    tile = lead_ref.shape[1] - half
    for part in range(2):
        lead_out[part] = lead_ref[part] + left_ref[part, :, half:]
        trail_out[part] = edge_block(
            trail_ref[part] + right_ref[part], left_ref[part, :, :half]
        )
        down_out[part, :, :half] = lead_out[part, tile - HALO :, :]
        down_out[part, :HALO, half:tile] = last_ref[part, half - HALO :, half:tile]
        down_out[part, HALO:, half:tile] = beyond_ref[part, :, half:tile]
        down_out[part, :, tile:] = trail_out[part, tile - HALO :, :]
        up_out[part, :, :half] = lead_out[part, :HALO, :]
        up_out[part, :, half:tile] = head_ref[part, :, half:tile]
        up_out[part, :, tile:] = trail_out[part, :HALO, :]


def columns_sum(canvas, from_left, from_right):
    grow = canvas.shape[1]
    half = from_right.shape[-1]
    tile = grow - half
    strip = jax.ShapeDtypeStruct((2, grow, half), jnp.float32)
    return pl.pallas_call(
        columns_kernel,
        out_shape=(
            strip,
            strip,
            jax.ShapeDtypeStruct((2, half + HALO, grow), jnp.float32),
            jax.ShapeDtypeStruct((2, HALO, grow), jnp.float32),
        ),
        grid=(1,),
        in_specs=[
            pl.BlockSpec((2, grow, half), lambda g: (0, 0, 0)),
            pl.BlockSpec((2, grow, half), lambda g: (0, 0, tile // half)),
            pl.BlockSpec((2, half, grow), lambda g: (0, tile // half - 1, 0)),
            pl.BlockSpec((2, half, grow), lambda g: (0, tile // half, 0)),
            pl.BlockSpec((2, HALO, grow), lambda g: (0, 0, 0)),
            pl.BlockSpec((2, grow, 2 * half), lambda g: (0, 0, 0)),
            pl.BlockSpec((2, grow, half), lambda g: (0, 0, 0)),
        ],
        out_specs=[
            pl.BlockSpec((2, grow, half), lambda g: (0, 0, 0)),
            pl.BlockSpec((2, grow, half), lambda g: (0, 0, 0)),
            pl.BlockSpec((2, half + HALO, grow), lambda g: (0, 0, 0)),
            pl.BlockSpec((2, HALO, grow), lambda g: (0, 0, 0)),
        ],
        compiler_params=pltpu.CompilerParams(vmem_limit_bytes=VMEM_LIMIT),
        name="columns",
    )(canvas, canvas, canvas, canvas, canvas, from_left, from_right)


def sweeps_kernel(
    canvas_ref, lead_ref, trail_ref, above_ref, below_ref, obj_ref, top_ref, bottom_ref,
    left_ref, right_ref, weight_ref, field_ref, edge_ref, rhs_ref, first_ref, second_ref,
):
    tile = obj_ref.shape[1]
    half = lead_ref.shape[-1]
    rows = tile + 2 * HALO
    grow = tile + half
    chunk = 56
    for part in range(2):
        first_ref[part, :HALO, :tile] = top_ref[part]
        first_ref[part, HALO : HALO + tile, :tile] = obj_ref[part]
        first_ref[part, HALO + tile :, :tile] = bottom_ref[part]
        first_ref[part, :, tile:] = edge_block(right_ref[part], left_ref[part])
        rhs_ref[part, :HALO, :] = above_ref[part, :HALO, :]
        rhs_ref[part, HALO : HALO + tile, half:tile] = canvas_ref[part, :tile, half:tile]
        rhs_ref[part, HALO : HALO + tile, :half] = lead_ref[part, :tile, :]
        rhs_ref[part, HALO : HALO + tile, tile:] = trail_ref[part, :tile, :]
        rhs_ref[part, HALO + tile :, half:tile] = canvas_ref[part, tile : tile + HALO, half:tile]
        rhs_ref[part, HALO + tile :, :half] = lead_ref[part, tile : tile + HALO, :]
        rhs_ref[part, HALO + tile :, tile:] = trail_ref[part, tile : tile + HALO, :]
        rhs_ref[part, HALO + tile :, :] += below_ref[part]
        rhs_ref[part, HALO : HALO + half, :] += above_ref[part, HALO:, :]

        def prepare(step, carry):
            at = pl.ds(pl.multiple_of(step * chunk, 8), chunk)
            rhs_ref[part, at, :] = (
                rhs_ref[part, at, :] + obj_weight * first_ref[part, at, :]
            ) * weight_ref[at, :]
            return carry

        lax.fori_loop(0, rows // chunk, prepare, 0)

    def sweep(source, target, part):
        def step_rows(step, carry):
            base = pl.multiple_of(step * 8, 8)
            at = pl.ds(base, 8)
            before = pl.ds(pl.multiple_of(jnp.maximum(base - 8, 0), 8), 8)
            after = pl.ds(pl.multiple_of(jnp.minimum(base + 8, rows - 8), 8), 8)
            here = source[part, at, :]
            row = lax.broadcasted_iota(jnp.int32, here.shape, 0)
            up = jnp.where(row == 0, pltpu.roll(source[part, before, :], 1, 0), pltpu.roll(here, 1, 0))
            down = jnp.where(row == 7, pltpu.roll(source[part, after, :], 7, 0), pltpu.roll(here, 7, 0))
            sides = pltpu.roll(here, 1, 1) + pltpu.roll(here, grow - 1, 1)
            target[part, at, :] = rhs_ref[part, at, :] + (smooth_weight * weight_ref[at, :]) * (
                up + down + sides
            )
            return carry

        lax.fori_loop(0, rows // 8, step_rows, 0, unroll=2)

    for part in range(2):
        source, target = first_ref, second_ref
        for _ in range(SWEEPS):
            sweep(source, target, part)
            source, target = target, source
        field_ref[part] = source[part, HALO : HALO + tile, :tile]
        edge_ref[part] = source[part, HALO : HALO + tile, :half]


def object_sweeps(canvas, lead, trail, above, below, obj, top, bottom, left, right, weight):
    tile = obj.shape[1]
    grow = canvas.shape[1]
    rows = tile + 2 * HALO
    work = pltpu.VMEM((2, rows, grow), jnp.float32)
    return pl.pallas_call(
        sweeps_kernel,
        out_shape=(
            jax.ShapeDtypeStruct(obj.shape, jnp.float32),
            jax.ShapeDtypeStruct((2, tile, grow - tile), jnp.float32),
        ),
        in_specs=[VMEM_SPEC] * 11,
        out_specs=[VMEM_SPEC] * 2,
        scratch_shapes=[work, work, work],
        compiler_params=pltpu.CompilerParams(vmem_limit_bytes=VMEM_LIMIT),
        name="sweeps",
    )(canvas, lead, trail, above, below, obj, top, bottom, left, right, weight)


def windows_kernel(place_ref, field_ref, right_ref, below_ref, out_ref, whole_ref, load_sem, store_sem):
    tile = field_ref.shape[1]
    width = out_ref.shape[-1]
    half = width // 2
    loads = [
        pltpu.make_async_copy(field_ref, whole_ref.at[:, :tile, :tile], load_sem.at[0]),
        pltpu.make_async_copy(right_ref, whole_ref.at[:, :tile, tile:], load_sem.at[1]),
        pltpu.make_async_copy(below_ref, whole_ref.at[:, tile:, :], load_sem.at[2]),
    ]
    for copy in loads:
        copy.start()
    for copy in loads:
        copy.wait()
    stores = []
    for frame in range(out_ref.shape[0]):
        row = pl.multiple_of(place_ref[frame, 0], half)
        col = pl.multiple_of(place_ref[frame, 1], half)
        stores.append(
            pltpu.make_async_copy(
                whole_ref.at[:, pl.ds(row, width), pl.ds(col, width)], out_ref.at[frame], store_sem.at[frame]
            )
        )
    for copy in stores:
        copy.start()
    for copy in stores:
        copy.wait()


def windows(places, field, from_right, from_below, width):
    count = places.shape[0]
    grow = from_below.shape[-1]
    anywhere = pl.BlockSpec(memory_space=pl.ANY)
    return pl.pallas_call(
        windows_kernel,
        out_shape=jax.ShapeDtypeStruct((count, 2, width, width), jnp.float32),
        in_specs=[pl.BlockSpec(memory_space=pltpu.SMEM), anywhere, anywhere, anywhere],
        out_specs=anywhere,
        scratch_shapes=[
            pltpu.VMEM((2, grow, grow), jnp.float32),
            pltpu.SemaphoreType.DMA((3,)),
            pltpu.SemaphoreType.DMA((count,)),
        ],
        compiler_params=pltpu.CompilerParams(vmem_limit_bytes=VMEM_LIMIT),
        name="windows",
    )(places, field, from_right, from_below)


def halve(data, axis, mask):
    rows = data.shape[1] // 2
    upper = (lax.axis_index(axis) & mask) != 0
    keep = jnp.where(upper, rows, 0)
    give = jnp.where(upper, 0, rows)
    route = [(i, i ^ mask) for i in range(lax.axis_size(axis))]
    got = lax.ppermute(lax.dynamic_slice_in_dim(data, give, rows, axis=1), axis, route)
    return lax.dynamic_slice_in_dim(data, keep, rows, axis=1) + got


def double(data, axis, mask):
    upper = (lax.axis_index(axis) & mask) != 0
    route = [(i, i ^ mask) for i in range(lax.axis_size(axis))]
    got = lax.ppermute(data, axis, route)
    return jnp.concatenate([jnp.where(upper, got, data), jnp.where(upper, data, got)], axis=1)


def scatter_rows(data, axis):
    count = lax.axis_size(axis)
    rows = data.shape[1] // count
    me = lax.axis_index(axis)
    total = lax.dynamic_slice_in_dim(data, me * rows, rows, axis=1)
    for mask in range(1, count):
        route = [(i, i ^ mask) for i in range(count)]
        piece = lax.dynamic_slice_in_dim(data, (me ^ mask) * rows, rows, axis=1)
        total = total + lax.ppermute(piece, axis, route)
    return total


def gather_rows(data, axis):
    count = lax.axis_size(axis)
    rows = data.shape[1]
    me = lax.axis_index(axis)
    out = jnp.zeros((data.shape[0], rows * count) + data.shape[2:], data.dtype)
    out = lax.dynamic_update_slice_in_dim(out, data, me * rows, axis=1)
    for mask in range(1, count):
        route = [(i, i ^ mask) for i in range(count)]
        got = lax.ppermute(data, axis, route)
        out = lax.dynamic_update_slice_in_dim(out, got, (me ^ mask) * rows, axis=1)
    return out


def update_probe(num, probe):
    parts = num.shape[0] - 1
    width = probe.shape[-1]
    flat = probe.reshape(parts, width, width)
    cols, rows = lax.axis_size("col"), lax.axis_size("row")
    masks = [1 << n for n in range(cols.bit_length() - 1)]
    piece = num
    offset = jnp.zeros((), jnp.int32)
    span = width
    for mask in masks:
        piece = halve(piece, "col", mask)
        span = span // 2
        offset = offset + jnp.where((lax.axis_index("col") & mask) != 0, span, 0)
    piece = scatter_rows(piece, "row")
    span = span // rows
    offset = offset + lax.axis_index("row") * span
    mine = lax.dynamic_slice_in_dim(flat, offset, span, axis=1)
    fresh = (piece[:parts] + probe_weight * mine) / (piece[parts:] + probe_weight)
    fresh = gather_rows(fresh, "row")
    for mask in reversed(masks):
        fresh = double(fresh, "col", mask)
    return fresh.reshape(probe.shape)


def per_device(amplitude, patches, dual, probe, obj, positions):
    width = amplitude.shape[-1]
    half = width // 2
    tile = obj.shape[1]
    row_index = lax.axis_index("row")
    col_index = lax.axis_index("col")
    origin = jnp.stack([row_index * tile, col_index * tile]).astype(jnp.int32)
    places = positions - origin

    marked = positions + 1
    marked = jnp.concatenate([shift(marked, "col", 1), marked, shift(marked, "col", -1)], axis=0)
    marked = jnp.concatenate([shift(marked, "row", 1), marked, shift(marked, "row", -1)], axis=0)
    around = jnp.where(marked > 0, marked - 1 - origin, -tile * 4)
    bounds = jnp.stack(
        [
            -row_index * tile,
            (lax.axis_size("row") - row_index) * tile,
            -col_index * tile,
            (lax.axis_size("col") - col_index) * tile,
        ]
    ).astype(jnp.int32)
    weight = object_weights(around, bounds, probe, tile)

    top = shift(obj[:, tile - HALO :, :], "row", 1)
    bottom = shift(obj[:, :HALO, :], "row", -1)
    tall = jnp.concatenate([top, obj, bottom], axis=1)
    left = shift(tall[:, :, tile - half :], "col", 1)
    right = shift(tall[:, :, :half], "col", -1)

    dual_new, num, canvas = frames_update(amplitude, patches, dual, probe, places, tile)
    probe_new = update_probe(num, probe)

    from_left = shift(canvas[:, :, tile - half :], "col", 1)
    from_right = shift(canvas[:, :, :half], "col", -1)
    lead, trail, down, up = columns_sum(canvas, from_left, from_right)
    above = shift(down, "row", 1)
    below = shift(up, "row", -1)
    field, edge = object_sweeps(
        canvas, lead, trail, above, below, obj, top, bottom, left, right, weight
    )
    far_right = shift(edge, "col", -1)
    strip = jnp.concatenate([field[:, :half, :], far_right[:, :half, :]], axis=2)
    far_below = shift(strip, "row", -1)
    patches_new = windows(places, field, far_right, far_below, width)
    return (dual_new, field, probe_new, patches_new)


def solution(mesh):
    return jax.shard_map(
        per_device,
        mesh=mesh,
        in_specs=(
            P(("row", "col"), None, None),
            P(("row", "col"), None, None, None),
            P(("row", "col"), None, None, None, None),
            P(),
            P(None, "row", "col"),
            P(("row", "col"), None),
        ),
        out_specs=(
            P(("row", "col"), None, None, None, None),
            P(None, "row", "col"),
            P(),
            P(("row", "col"), None, None, None),
        ),
        check_vma=False,
    )
```

profile of v0, /device:TPU:9, one launch (start us, length us, event | category | flops | bytes accessed | tf_op | source)
XLA Modules:
  0.0 235.2 jit_solution(14677241310175059682)
XLA Ops:
  0.6 0.8 copy.15
  2.0 26.5 %frames.1 = (f32[4,3,2,256,256]{4,3,2,1,0:T(8,128)}, f32[7,256,256]{2,1,0:T(8,128)}, f32[2,896,896]{2,1,0:T(8,128)}) custom-call(s32[4,2]{1,0:T(4,128)} %broadcast_subtract_fusion.place_ref, f32[4,256,256]{2,1,0:T(8,128)} %amp_high_ref.1, f32[4,256,256]{2,1,0:T(8,128)} %amp_high_ref.1, f32[4,2,256,256]{3,2,1,0:T(8,128)} %patch_ref.1, ...), custom_call_target="tpu_custom_call" | custom-call | flops 9663676416 | bytes 20971520 | tf_op jit(solution)/shard_map/frames/pallas_call | solution.py:191
  28.5 1.3 constant_dynamic-slice_fusion.8
  29.8 0.7 collective-permute-start.12
  30.5 1.9 collective-permute-start.9
  32.5 3.6 %collective-permute-start.8 = (s32[4,2]{0,1:T(2,128)S(1)}, s32[4,2]{0,1:T(2,128)S(1)}, u32[]{:S(2)}, u32[]{:S(2)}) collective-permute-start(s32[4,2]{0,1:T(2,128)S(1)} %broadcast_add_fusion), channel_id=1, source_target_pairs={{0,1},{1,2},{2,3},{4,5},{5,6},{6,7},{8,9},{9,10},{10,11},{12,13},{... | collective-permute-start | bytes 104 | tf_op jit(solution)/shard_map/ppermute | solution.py:27
  36.1 1.3 dynamic-slice_add_fusion
  37.5 0.8 fusion.4
  38.4 3.1 %collective-permute-start.4 = (f32[2,8,768]{2,1,0:T(8,128)S(1)}, f32[2,8,768]{2,1,0:T(8,128)S(1)}, u32[]{:S(2)}, u32[]{:S(2)}) collective-permute-start(f32[2,8,768]{2,1,0:T(8,128)S(1)} %get-tuple-element.27), channel_id=1, source_target_pairs={{0,4},{4,8},{8,12},{12,16},{16,20},{20,24},{24,28},{1,5},{5,9},{9,... | collective-permute-start | bytes 147464 | tf_op jit(solution)/shard_map/ppermute | solution.py:27
  41.5 1.6 slice.30
  43.1 2.6 %collective-permute-start = (f32[2,896,256]{2,1,0:T(8,128)S(1)}, f32[2,896,256]{2,1,0:T(8,128)}, u32[]{:S(2)}, u32[]{:S(2)}) collective-permute-start(f32[2,896,256]{2,1,0:T(8,128)S(1)} %slice.30), channel_id=1, source_target_pairs={{0,1},{1,2},{2,3},{4,5},{5,6},{6,7},{8,9},{9,10},{10,11},{12,13},{... | collective-permute-start | bytes 5505032 | tf_op jit(solution)/shard_map/ppermute | solution.py:27
  45.8 2.2 slice.31
  48.6 3.0 %collective-permute-start.11 = (s32[12,2]{0,1:T(2,128)S(1)}, s32[12,2]{0,1:T(2,128)S(1)}, u32[]{:S(2)}, u32[]{:S(2)}) collective-permute-start(s32[12,2]{0,1:T(2,128)S(1)} %pad_add_fusion), channel_id=1, source_target_pairs={{4,0},{8,4},{12,8},{16,12},{20,16},{24,20},{28,24},{5,1},{9,5},{13... | collective-permute-start | bytes 296 | tf_op jit(solution)/shard_map/ppermute | solution.py:27
  51.7 2.2 collective-permute-start.10
  53.9 3.9 %collective-permute-start.5 = (f32[2,8,768]{2,1,0:T(8,128)S(1)}, f32[2,8,768]{2,1,0:T(8,128)S(1)}, u32[]{:S(2)}, u32[]{:S(2)}) collective-permute-start(f32[2,8,768]{2,1,0:T(8,128)S(1)} %get-tuple-element.26), channel_id=1, source_target_pairs={{4,0},{8,4},{12,8},{16,12},{20,16},{24,20},{28,24},{5,1},{9,5},{13... | collective-permute-start | bytes 147464 | tf_op jit(solution)/shard_map/ppermute | solution.py:27
  58.1 1.1 dynamic-slice_add_fusion.1
  59.5 2.4 %collective-permute-start.20 = (f32[7,8,256]{2,1,0:T(8,128)S(1)}, f32[7,8,256]{2,1,0:T(8,128)S(1)}, u32[]{:S(2)}, u32[]{:S(2)}) collective-permute-start(f32[7,8,256]{2,1,0:T(8,128)S(1)} %get-tuple-element.33), channel_id=1, source_target_pairs={{0,28},{4,24},{8,20},{12,16},{16,12},{20,8},{24,4},{28,0},{1,29},{... | collective-permute-start | bytes 172040 | tf_op jit(solution)/shard_map/ppermute | solution.py:507
  62.0 2.7 %constant_dynamic-update-slice_fusion.1 = f32[2,784,768]{2,1,0:T(8,128)S(1)} fusion(f32[2,784,768]{2,1,0:T(8,128)S(1)} %constant_dynamic-update-slice_fusion.2, f32[2,768,768]{2,1,0:T(8,128)} %obj_ref.1), kind=kLoop, calls=%fused_computation.16 | loop fusion | bytes 9437184
  64.8 3.9 %collective-permute-start.18 = (f32[7,8,256]{2,1,0:T(8,128)S(1)}, f32[7,8,256]{2,1,0:T(8,128)S(1)}, u32[]{:S(2)}, u32[]{:S(2)}) collective-permute-start(f32[7,8,256]{2,1,0:T(8,128)S(1)} %get-tuple-element.35), channel_id=1, source_target_pairs={{0,20},{4,16},{8,28},{12,24},{16,4},{20,0},{24,12},{28,8},{1,21},{... | collective-permute-start | bytes 172040 | tf_op jit(solution)/shard_map/ppermute | solution.py:507
  69.0 1.2 collective-permute-start.16
  70.2 1.2 collective-permute-start.15
  71.3 5.5 %collective-permute-start.1 = (f32[2,896,128]{2,1,0:T(8,128)S(1)}, f32[2,896,128]{2,1,0:T(8,128)S(1)}, u32[]{:S(2)}, u32[]{:S(2)}) collective-permute-start(f32[2,896,128]{2,1,0:T(8,128)S(1)} %copy-done.3), channel_id=1, source_target_pairs={{1,0},{2,1},{3,2},{5,4},{6,5},{7,6},{9,8},{10,9},{11,10},{13,12},{... | collective-permute-start | bytes 2752520 | tf_op jit(solution)/shard_map/ppermute | solution.py:27
  77.0 0.8 constant_dynamic-update-slice_fusion.10
  77.8 0.8 collective-permute-start.21
  78.6 1.0 fusion.3
  79.6 2.8 %collective-permute-start.7 = (f32[2,784,128]{2,1,0:T(8,128)}, f32[2,784,128]{2,1,0:T(8,128)}, u32[]{:S(2)}, u32[]{:S(2)}) collective-permute-start(f32[2,784,128]{2,1,0:T(8,128)} %get-tuple-element.24), channel_id=1, source_target_pairs={{1,0},{2,1},{3,2},{5,4},{6,5},{7,6},{9,8},{10,9},{11,10},{13,12},{... | collective-permute-start | bytes 2408456 | tf_op jit(solution)/shard_map/ppermute | solution.py:27
  82.4 2.7 %collective-permute-start.6 = (f32[2,784,128]{2,1,0:T(8,128)S(1)}, f32[2,784,128]{2,1,0:T(8,128)}, u32[]{:S(2)}, u32[]{:S(2)}) collective-permute-start(f32[2,784,128]{2,1,0:T(8,128)S(1)} %get-tuple-element.25), channel_id=1, source_target_pairs={{0,1},{1,2},{2,3},{4,5},{5,6},{6,7},{8,9},{9,10},{10,11},{12,13},{... | collective-permute-start | bytes 2408456 | tf_op jit(solution)/shard_map/ppermute | solution.py:27
  85.2 2.8 %collective-permute-done.1.right_ref = f32[2,896,128]{2,1,0:T(8,128)S(1)} collective-permute-done((f32[2,896,128]{2,1,0:T(8,128)S(1)}, f32[2,896,128]{2,1,0:T(8,128)S(1)}, u32[]{:S(2)}, u32[]{:S(2)}) %collective-permute-start.1) | collective-permute-done | bytes 917536 | tf_op jit(solution)/shard_map/ppermute | solution.py:27
  88.0 1.1 collective-permute-start.26
  89.1 3.3 %collective-permute-start.22 = (f32[6,8,256]{2,1,0:T(8,128)S(1)}, f32[6,8,256]{2,1,0:T(8,128)S(1)}, u32[]{:S(2)}, u32[]{:S(2)}) collective-permute-start(f32[6,8,256]{2,1,0:T(8,128)S(1)} %get-tuple-element.23), channel_id=1, source_target_pairs={{0,8},{4,12},{8,0},{12,4},{16,24},{20,28},{24,16},{28,20},{1,9},{5... | collective-permute-start | bytes 147464 | tf_op jit(solution)/shard_map/ppermute | solution.py:519
  92.5 4.6 %columns.1 = (f32[2,896,128]{2,1,0:T(8,128)}, f32[2,896,128]{2,1,0:T(8,128)}, f32[2,136,896]{2,1,0:T(8,128)}, f32[2,8,896]{2,1,0:T(8,128)}) custom-call(f32[2,896,896]{2,1,0:T(8,128)} %get-tuple-element.14.lead_ref.trail_ref.last_ref.beyond_ref.head_ref.canvas_ref, ...), custom_call_target="tpu_custom_call" | custom-call | tf_op jit(solution)/shard_map/columns/pallas_call | solution.py:327
  97.1 1.9 collective-permute-start.2
  99.0 2.4 %collective-permute-start.23 = (f32[6,8,256]{2,1,0:T(8,128)S(1)}, f32[6,8,256]{2,1,0:T(8,128)S(1)}, u32[]{:S(2)}, u32[]{:S(2)}) collective-permute-start(f32[6,8,256]{2,1,0:T(8,128)S(1)} %get-tuple-element.23), channel_id=1, source_target_pairs={{0,12},{4,8},{8,4},{12,0},{16,28},{20,24},{24,20},{28,16},{1,13},{... | collective-permute-start | bytes 147464 | tf_op jit(solution)/shard_map/ppermute | solution.py:519
  101.5 21.6 %collective-permute-done.23 = f32[6,8,256]{2,1,0:T(8,128)S(1)} collective-permute-done((f32[6,8,256]{2,1,0:T(8,128)S(1)}, f32[6,8,256]{2,1,0:T(8,128)S(1)}, u32[]{:S(2)}, u32[]{:S(2)}) %collective-permute-start.23) | collective-permute-done | bytes 49184 | tf_op jit(solution)/shard_map/ppermute | solution.py:519
  123.1 3.8 %collective-permute-done.24 = f32[6,8,256]{2,1,0:T(8,128)S(1)} collective-permute-done((f32[6,8,256]{2,1,0:T(8,128)S(1)}, f32[6,8,256]{2,1,0:T(8,128)S(1)}, u32[]{:S(2)}, u32[]{:S(2)}) %collective-permute-start.24) | collective-permute-done | bytes 49184 | tf_op jit(solution)/shard_map/ppermute | solution.py:519
  126.9 5.3 %collective-permute-done.25 = f32[6,8,256]{2,1,0:T(8,128)S(1)} collective-permute-done((f32[6,8,256]{2,1,0:T(8,128)S(1)}, f32[6,8,256]{2,1,0:T(8,128)S(1)}, u32[]{:S(2)}, u32[]{:S(2)}) %collective-permute-start.25) | collective-permute-done | bytes 49184 | tf_op jit(solution)/shard_map/ppermute | solution.py:519
  132.3 3.8 %collective-permute-done.27 = f32[6,8,256]{2,1,0:T(8,128)S(1)} collective-permute-done((f32[6,8,256]{2,1,0:T(8,128)S(1)}, f32[6,8,256]{2,1,0:T(8,128)S(1)}, u32[]{:S(2)}, u32[]{:S(2)}) %collective-permute-start.27) | collective-permute-done | bytes 49184 | tf_op jit(solution)/shard_map/ppermute | solution.py:519
  136.1 3.0 %collective-permute-start.3 = (f32[2,8,896]{2,1,0:T(8,128)}, f32[2,8,896]{2,1,0:T(8,128)S(1)}, u32[]{:S(2)}, u32[]{:S(2)}) collective-permute-start(f32[2,8,896]{2,1,0:T(8,128)} %get-tuple-element.18), channel_id=1, source_target_pairs={{4,0},{8,4},{12,8},{16,12},{20,16},{24,20},{28,24},{5,1},{9,5},{13... | collective-permute-start | bytes 172040 | tf_op jit(solution)/shard_map/ppermute | solution.py:27
  139.8 5.3 %weights.1.weight_ref = f32[784,896]{1,0:T(8,128)} custom-call(s32[36,2]{1,0:T(8,128)} %subtract_select_fusion.place_ref, s32[4]{0:T(128)} %pad_add_fusion.2.bound_ref, f32[3,2,256,256]{3,2,1,0:T(8,128)} %probe_ref.3), custom_call_target="tpu_custom_call" | custom-call | tf_op jit(solution)/shard_map/weights/pallas_call | solution.py:292
  146.0 51.4 %sweeps.1 = (f32[2,768,768]{2,1,0:T(8,128)}, f32[2,768,128]{2,1,0:T(8,128)}) custom-call(f32[2,896,896]{2,1,0:T(8,128)} %get-tuple-element.14.lead_ref.trail_ref.last_ref.beyond_ref.head_ref.canvas_ref, f32[2,896,128]{2,1,0:T(8,128)} %get-tuple-element.15.lead_ref, f32[2,896,128]{2,1,0:T(8,128)} %get-tuple-element.16.trail_ref, f32[2,136,896]{2,1,0:T(8,128)} %copy-done.1, ...), custom_call_target="tpu_custom_call" | custom-call | tf_op jit(solution)/shard_map/sweeps/pallas_call | solution.py:421
  197.4 5.0 %collective-permute-start.30 = (f32[2,768,128]{2,1,0:T(8,128)}, f32[2,768,128]{2,1,0:T(8,128)S(1)}, u32[]{:S(2)}, u32[]{:S(2)}) collective-permute-start(f32[2,768,128]{2,1,0:T(8,128)} %get-tuple-element.21), channel_id=1, source_target_pairs={{1,0},{2,1},{3,2},{5,4},{6,5},{7,6},{9,8},{10,9},{11,10},{13,12},{... | collective-permute-start | bytes 2359304 | tf_op jit(solution)/shard_map/ppermute | solution.py:27
  202.6 1.2 slice.38
  203.8 8.9 %collective-permute-done.30.right_ref = f32[2,768,128]{2,1,0:T(8,128)S(1)} collective-permute-done((f32[2,768,128]{2,1,0:T(8,128)}, f32[2,768,128]{2,1,0:T(8,128)S(1)}, u32[]{:S(2)}, u32[]{:S(2)}) %collective-permute-start.30) | collective-permute-done | bytes 786464 | tf_op jit(solution)/shard_map/ppermute | solution.py:27
  212.8 1.9 collective-permute-start.31
  214.9 1.2 pad_maximum_fusion
  216.1 13.2 %collective-permute-done.31.below_ref = f32[2,128,896]{2,1,0:T(8,128)S(1)} collective-permute-done((f32[2,128,896]{2,1,0:T(8,128)S(1)}, f32[2,128,896]{2,1,0:T(8,128)S(1)}, u32[]{:S(2)}, u32[]{:S(2)}) %collective-permute-start.31) | collective-permute-done | bytes 917536 | tf_op jit(solution)/shard_map/ppermute | solution.py:27
  229.4 0.9 copy-done.2
  230.3 4.9 %windows.1 = f32[4,2,256,256]{3,2,1,0:T(8,128)} custom-call(s32[4,2]{1,0:T(4,128)} %broadcast_subtract_fusion.place_ref, f32[2,768,768]{2,1,0:T(8,128)} %get-tuple-element.10.field_ref, f32[2,768,128]{2,1,0:T(8,128)} %copy-done, f32[2,128,896]{2,1,0:T(8,128)} %copy-done.2), custom_call_target="tpu_custom_call" | custom-call | tf_op jit(solution)/shard_map/windows/pallas_call | solution.py:467
  (78 shorter events, 4.5 us)
Async XLA Ops:
  2.0 28.5 %copy-start.8 = (s32[4,2]{0,1:T(2,128)S(1)}, s32[4,2]{0,1:T(2,128)}, u32[]{:S(2)}) copy-start(s32[4,2]{0,1:T(2,128)} %param.14) | copy-start | bytes 100
  29.8 6.3 %collective-permute-start.12 = (f32[7,128,256]{2,1,0:T(8,128)S(1)}, f32[7,128,256]{2,1,0:T(8,128)S(1)}, u32[]{:S(2)}, u32[]{:S(2)}) collective-permute-start(f32[7,128,256]{2,1,0:T(8,128)S(1)} %constant_dynamic-slice_fusion.8), channel_id=1, source_target_pairs={{0,1},{1,0},{2,3},{3,2},{4,5},{5,4},{6,7},{7,6},{8,9},{9,8},{10,11... | collective-permute-start | bytes 2752520 | tf_op jit(solution)/shard_map/ppermute | solution.py:488
  30.5 18.1 %collective-permute-start.9 = (s32[4,2]{0,1:T(2,128)S(1)}, s32[4,2]{0,1:T(2,128)S(1)}, u32[]{:S(2)}, u32[]{:S(2)}) collective-permute-start(s32[4,2]{0,1:T(2,128)S(1)} %broadcast_add_fusion), channel_id=1, source_target_pairs={{1,0},{2,1},{3,2},{5,4},{6,5},{7,6},{9,8},{10,9},{11,10},{13,12},{... | collective-permute-start | bytes 104 | tf_op jit(solution)/shard_map/ppermute | solution.py:27
  32.5 16.1 %collective-permute-start.8 = (s32[4,2]{0,1:T(2,128)S(1)}, s32[4,2]{0,1:T(2,128)S(1)}, u32[]{:S(2)}, u32[]{:S(2)}) collective-permute-start(s32[4,2]{0,1:T(2,128)S(1)} %broadcast_add_fusion), channel_id=1, source_target_pairs={{0,1},{1,2},{2,3},{4,5},{5,6},{6,7},{8,9},{9,10},{10,11},{12,13},{... | collective-permute-start | bytes 104 | tf_op jit(solution)/shard_map/ppermute | solution.py:27
  37.5 20.7 %collective-permute-start.13 = (f32[7,64,256]{2,1,0:T(8,128)S(1)}, f32[7,64,256]{2,1,0:T(8,128)}, u32[]{:S(2)}, u32[]{:S(2)}) collective-permute-start(f32[7,64,256]{2,1,0:T(8,128)S(1)} %constant_dynamic-slice_fusion.7), channel_id=1, source_target_pairs={{0,2},{1,3},{2,0},{3,1},{4,6},{5,7},{6,4},{7,5},{8,10},{9,11},{10,... | collective-permute-start | bytes 1376264 | tf_op jit(solution)/shard_map/ppermute | solution.py:488
  38.4 19.7 %collective-permute-start.4 = (f32[2,8,768]{2,1,0:T(8,128)S(1)}, f32[2,8,768]{2,1,0:T(8,128)S(1)}, u32[]{:S(2)}, u32[]{:S(2)}) collective-permute-start(f32[2,8,768]{2,1,0:T(8,128)S(1)} %get-tuple-element.27), channel_id=1, source_target_pairs={{0,4},{4,8},{8,12},{12,16},{16,20},{20,24},{24,28},{1,5},{5,9},{9,... | collective-permute-start | bytes 147464 | tf_op jit(solution)/shard_map/ppermute | solution.py:27
  43.1 46.0 %collective-permute-start = (f32[2,896,256]{2,1,0:T(8,128)S(1)}, f32[2,896,256]{2,1,0:T(8,128)}, u32[]{:S(2)}, u32[]{:S(2)}) collective-permute-start(f32[2,896,256]{2,1,0:T(8,128)S(1)} %slice.30), channel_id=1, source_target_pairs={{0,1},{1,2},{2,3},{4,5},{5,6},{6,7},{8,9},{9,10},{10,11},{12,13},{... | collective-permute-start | bytes 5505032 | tf_op jit(solution)/shard_map/ppermute | solution.py:27
  48.6 5.3 %collective-permute-start.11 = (s32[12,2]{0,1:T(2,128)S(1)}, s32[12,2]{0,1:T(2,128)S(1)}, u32[]{:S(2)}, u32[]{:S(2)}) collective-permute-start(s32[12,2]{0,1:T(2,128)S(1)} %pad_add_fusion), channel_id=1, source_target_pairs={{4,0},{8,4},{12,8},{16,12},{20,16},{24,20},{28,24},{5,1},{9,5},{13... | collective-permute-start | bytes 296 | tf_op jit(solution)/shard_map/ppermute | solution.py:27
  51.7 6.2 %collective-permute-start.10 = (s32[12,2]{0,1:T(2,128)S(1)}, s32[12,2]{0,1:T(2,128)S(1)}, u32[]{:S(2)}, u32[]{:S(2)}) collective-permute-start(s32[12,2]{0,1:T(2,128)S(1)} %pad_add_fusion), channel_id=1, source_target_pairs={{0,4},{4,8},{8,12},{12,16},{16,20},{20,24},{24,28},{1,5},{5,9},{9,... | collective-permute-start | bytes 296 | tf_op jit(solution)/shard_map/ppermute | solution.py:27
  53.9 10.8 %collective-permute-start.5 = (f32[2,8,768]{2,1,0:T(8,128)S(1)}, f32[2,8,768]{2,1,0:T(8,128)S(1)}, u32[]{:S(2)}, u32[]{:S(2)}) collective-permute-start(f32[2,8,768]{2,1,0:T(8,128)S(1)} %get-tuple-element.26), channel_id=1, source_target_pairs={{4,0},{8,4},{12,8},{16,12},{20,16},{24,20},{28,24},{5,1},{9,5},{13... | collective-permute-start | bytes 147464 | tf_op jit(solution)/shard_map/ppermute | solution.py:27
  58.1 6.6 %copy-start.5 = (f32[2,8,768]{2,1,0:T(8,128)}, f32[2,8,768]{2,1,0:T(8,128)S(1)}, u32[]{:S(2)}) copy-start(f32[2,8,768]{2,1,0:T(8,128)S(1)} %collective-permute-done.4.top_ref) | copy-start | bytes 147460
  59.3 9.4 %collective-permute-start.14 = (f32[7,8,256]{2,1,0:T(8,128)S(1)}, f32[7,8,256]{2,1,0:T(8,128)S(1)}, u32[]{:S(2)}, u32[]{:S(2)}) collective-permute-start(f32[7,8,256]{2,1,0:T(8,128)S(1)} %get-tuple-element.32), channel_id=1, source_target_pairs={{0,4},{4,0},{8,12},{12,8},{16,20},{20,16},{24,28},{28,24},{1,5},{5... | collective-permute-start | bytes 172040 | tf_op jit(solution)/shard_map/ppermute | solution.py:507
  59.5 9.5 %collective-permute-start.20 = (f32[7,8,256]{2,1,0:T(8,128)S(1)}, f32[7,8,256]{2,1,0:T(8,128)S(1)}, u32[]{:S(2)}, u32[]{:S(2)}) collective-permute-start(f32[7,8,256]{2,1,0:T(8,128)S(1)} %get-tuple-element.33), channel_id=1, source_target_pairs={{0,28},{4,24},{8,20},{12,16},{16,12},{20,8},{24,4},{28,0},{1,29},{... | collective-permute-start | bytes 172040 | tf_op jit(solution)/shard_map/ppermute | solution.py:507
  61.8 9.5 %copy-start.3 = (f32[2,896,128]{2,1,0:T(8,128)S(1)}, f32[2,896,128]{2,1,0:T(8,128)}, u32[]{:S(2)}) copy-start(f32[2,896,128]{2,1,0:T(8,128)} %slice.31) | copy-start | bytes 2752516
  61.8 8.3 %collective-permute-start.19 = (f32[7,8,256]{2,1,0:T(8,128)S(1)}, f32[7,8,256]{2,1,0:T(8,128)S(1)}, u32[]{:S(2)}, u32[]{:S(2)}) collective-permute-start(f32[7,8,256]{2,1,0:T(8,128)S(1)} %get-tuple-element.34), channel_id=1, source_target_pairs={{0,24},{4,28},{8,16},{12,20},{16,8},{20,12},{24,0},{28,4},{1,25},{... | collective-permute-start | bytes 172040 | tf_op jit(solution)/shard_map/ppermute | solution.py:507
  64.7 13.1 %copy-start.6 = (f32[2,8,768]{2,1,0:T(8,128)}, f32[2,8,768]{2,1,0:T(8,128)S(1)}, u32[]{:S(2)}) copy-start(f32[2,8,768]{2,1,0:T(8,128)S(1)} %collective-permute-done.5.bottom_ref) | copy-start | bytes 147460
  64.8 6.6 %collective-permute-start.18 = (f32[7,8,256]{2,1,0:T(8,128)S(1)}, f32[7,8,256]{2,1,0:T(8,128)S(1)}, u32[]{:S(2)}, u32[]{:S(2)}) collective-permute-start(f32[7,8,256]{2,1,0:T(8,128)S(1)} %get-tuple-element.35), channel_id=1, source_target_pairs={{0,20},{4,16},{8,28},{12,24},{16,4},{20,0},{24,12},{28,8},{1,21},{... | collective-permute-start | bytes 172040 | tf_op jit(solution)/shard_map/ppermute | solution.py:507
  68.7 8.2 %collective-permute-start.17 = (f32[7,8,256]{2,1,0:T(8,128)S(1)}, f32[7,8,256]{2,1,0:T(8,128)S(1)}, u32[]{:S(2)}, u32[]{:S(2)}) collective-permute-start(f32[7,8,256]{2,1,0:T(8,128)S(1)} %get-tuple-element.36), channel_id=1, source_target_pairs={{0,16},{4,20},{8,24},{12,28},{16,0},{20,4},{24,8},{28,12},{1,17},{... | collective-permute-start | bytes 172040 | tf_op jit(solution)/shard_map/ppermute | solution.py:507
  69.0 7.9 %collective-permute-start.16 = (f32[7,8,256]{2,1,0:T(8,128)S(1)}, f32[7,8,256]{2,1,0:T(8,128)S(1)}, u32[]{:S(2)}, u32[]{:S(2)}) collective-permute-start(f32[7,8,256]{2,1,0:T(8,128)S(1)} %get-tuple-element.37), channel_id=1, source_target_pairs={{0,12},{4,8},{8,4},{12,0},{16,28},{20,24},{24,20},{28,16},{1,13},{... | collective-permute-start | bytes 172040 | tf_op jit(solution)/shard_map/ppermute | solution.py:507
  70.2 6.8 %collective-permute-start.15 = (f32[7,8,256]{2,1,0:T(8,128)S(1)}, f32[7,8,256]{2,1,0:T(8,128)S(1)}, u32[]{:S(2)}, u32[]{:S(2)}) collective-permute-start(f32[7,8,256]{2,1,0:T(8,128)S(1)} %get-tuple-element.38), channel_id=1, source_target_pairs={{0,8},{4,12},{8,0},{12,4},{16,24},{20,28},{24,16},{28,20},{1,9},{5... | collective-permute-start | bytes 172040 | tf_op jit(solution)/shard_map/ppermute | solution.py:507
  71.3 16.6 %collective-permute-start.1 = (f32[2,896,128]{2,1,0:T(8,128)S(1)}, f32[2,896,128]{2,1,0:T(8,128)S(1)}, u32[]{:S(2)}, u32[]{:S(2)}) collective-permute-start(f32[2,896,128]{2,1,0:T(8,128)S(1)} %copy-done.3), channel_id=1, source_target_pairs={{1,0},{2,1},{3,2},{5,4},{6,5},{7,6},{9,8},{10,9},{11,10},{13,12},{... | collective-permute-start | bytes 2752520 | tf_op jit(solution)/shard_map/ppermute | solution.py:27
  77.8 19.2 %collective-permute-start.21 = (f32[6,8,256]{2,1,0:T(8,128)S(1)}, f32[6,8,256]{2,1,0:T(8,128)S(1)}, u32[]{:S(2)}, u32[]{:S(2)}) collective-permute-start(f32[6,8,256]{2,1,0:T(8,128)S(1)} %get-tuple-element.23), channel_id=1, source_target_pairs={{0,4},{4,0},{8,12},{12,8},{16,20},{20,16},{24,28},{28,24},{1,5},{5... | collective-permute-start | bytes 147464 | tf_op jit(solution)/shard_map/ppermute | solution.py:519
  79.6 65.4 %collective-permute-start.7 = (f32[2,784,128]{2,1,0:T(8,128)}, f32[2,784,128]{2,1,0:T(8,128)}, u32[]{:S(2)}, u32[]{:S(2)}) collective-permute-start(f32[2,784,128]{2,1,0:T(8,128)} %get-tuple-element.24), channel_id=1, source_target_pairs={{1,0},{2,1},{3,2},{5,4},{6,5},{7,6},{9,8},{10,9},{11,10},{13,12},{... | collective-permute-start | bytes 2408456 | tf_op jit(solution)/shard_map/ppermute | solution.py:27
  82.4 62.6 %collective-permute-start.6 = (f32[2,784,128]{2,1,0:T(8,128)S(1)}, f32[2,784,128]{2,1,0:T(8,128)}, u32[]{:S(2)}, u32[]{:S(2)}) collective-permute-start(f32[2,784,128]{2,1,0:T(8,128)S(1)} %get-tuple-element.25), channel_id=1, source_target_pairs={{0,1},{1,2},{2,3},{4,5},{5,6},{6,7},{8,9},{9,10},{10,11},{12,13},{... | collective-permute-start | bytes 2408456 | tf_op jit(solution)/shard_map/ppermute | solution.py:27
  88.0 1.1 copy-start.4
  88.0 44.3 %collective-permute-start.26 = (f32[6,8,256]{2,1,0:T(8,128)S(1)}, f32[6,8,256]{2,1,0:T(8,128)S(1)}, u32[]{:S(2)}, u32[]{:S(2)}) collective-permute-start(f32[6,8,256]{2,1,0:T(8,128)S(1)} %get-tuple-element.23), channel_id=1, source_target_pairs={{0,24},{4,28},{8,16},{12,20},{16,8},{20,12},{24,0},{28,4},{1,25},{... | collective-permute-start | bytes 147464 | tf_op jit(solution)/shard_map/ppermute | solution.py:519
  89.1 9.9 %collective-permute-start.22 = (f32[6,8,256]{2,1,0:T(8,128)S(1)}, f32[6,8,256]{2,1,0:T(8,128)S(1)}, u32[]{:S(2)}, u32[]{:S(2)}) collective-permute-start(f32[6,8,256]{2,1,0:T(8,128)S(1)} %get-tuple-element.23), channel_id=1, source_target_pairs={{0,8},{4,12},{8,0},{12,4},{16,24},{20,28},{24,16},{28,20},{1,9},{5... | collective-permute-start | bytes 147464 | tf_op jit(solution)/shard_map/ppermute | solution.py:519
  97.1 48.0 %collective-permute-start.2 = (f32[2,136,896]{2,1,0:T(8,128)}, f32[2,136,896]{2,1,0:T(8,128)S(1)}, u32[]{:S(2)}, u32[]{:S(2)}) collective-permute-start(f32[2,136,896]{2,1,0:T(8,128)} %get-tuple-element.17), channel_id=1, source_target_pairs={{0,4},{4,8},{8,12},{12,16},{16,20},{20,24},{24,28},{1,5},{5,9},{9,... | collective-permute-start | bytes 2924552 | tf_op jit(solution)/shard_map/ppermute | solution.py:27
  99.0 24.1 %collective-permute-start.23 = (f32[6,8,256]{2,1,0:T(8,128)S(1)}, f32[6,8,256]{2,1,0:T(8,128)S(1)}, u32[]{:S(2)}, u32[]{:S(2)}) collective-permute-start(f32[6,8,256]{2,1,0:T(8,128)S(1)} %get-tuple-element.23), channel_id=1, source_target_pairs={{0,12},{4,8},{8,4},{12,0},{16,28},{20,24},{24,20},{28,16},{1,13},{... | collective-permute-start | bytes 147464 | tf_op jit(solution)/shard_map/ppermute | solution.py:519
  123.1 3.8 %collective-permute-start.24 = (f32[6,8,256]{2,1,0:T(8,128)S(1)}, f32[6,8,256]{2,1,0:T(8,128)S(1)}, u32[]{:S(2)}, u32[]{:S(2)}) collective-permute-start(f32[6,8,256]{2,1,0:T(8,128)S(1)} %get-tuple-element.23), channel_id=1, source_target_pairs={{0,16},{4,20},{8,24},{12,28},{16,0},{20,4},{24,8},{28,12},{1,17},{... | collective-permute-start | bytes 147464 | tf_op jit(solution)/shard_map/ppermute | solution.py:519
  126.9 5.4 %collective-permute-start.25 = (f32[6,8,256]{2,1,0:T(8,128)S(1)}, f32[6,8,256]{2,1,0:T(8,128)S(1)}, u32[]{:S(2)}, u32[]{:S(2)}) collective-permute-start(f32[6,8,256]{2,1,0:T(8,128)S(1)} %get-tuple-element.23), channel_id=1, source_target_pairs={{0,20},{4,16},{8,28},{12,24},{16,4},{20,0},{24,12},{28,8},{1,21},{... | collective-permute-start | bytes 147464 | tf_op jit(solution)/shard_map/ppermute | solution.py:519
  132.3 3.8 %collective-permute-start.27 = (f32[6,8,256]{2,1,0:T(8,128)S(1)}, f32[6,8,256]{2,1,0:T(8,128)S(1)}, u32[]{:S(2)}, u32[]{:S(2)}) collective-permute-start(f32[6,8,256]{2,1,0:T(8,128)S(1)} %get-tuple-element.23), channel_id=1, source_target_pairs={{0,28},{4,24},{8,20},{12,16},{16,12},{20,8},{24,4},{28,0},{1,29},{... | collective-permute-start | bytes 147464 | tf_op jit(solution)/shard_map/ppermute | solution.py:519
  136.1 66.3 %collective-permute-start.28 = (f32[6,64,256]{2,1,0:T(8,128)S(1)}, f32[6,64,256]{2,1,0:T(8,128)S(1)}, u32[]{:S(2)}, u32[]{:S(2)}) collective-permute-start(f32[6,64,256]{2,1,0:T(8,128)S(1)} %constant_dynamic-update-slice_fusion.3), channel_id=1, source_target_pairs={{0,2},{1,3},{2,0},{3,1},{4,6},{5,7},{6,4},{7,5},{8,10},{9,11},{10,... | collective-permute-start | bytes 1179656 | tf_op jit(solution)/shard_map/ppermute | solution.py:495
  136.1 8.9 %collective-permute-start.3 = (f32[2,8,896]{2,1,0:T(8,128)}, f32[2,8,896]{2,1,0:T(8,128)S(1)}, u32[]{:S(2)}, u32[]{:S(2)}) collective-permute-start(f32[2,8,896]{2,1,0:T(8,128)} %get-tuple-element.18), channel_id=1, source_target_pairs={{4,0},{8,4},{12,8},{16,12},{20,16},{24,20},{28,24},{5,1},{9,5},{13... | collective-permute-start | bytes 172040 | tf_op jit(solution)/shard_map/ppermute | solution.py:27
  145.0 0.6 copy-start.7
  145.1 0.9 copy-start.1
  197.4 15.4 %collective-permute-start.30 = (f32[2,768,128]{2,1,0:T(8,128)}, f32[2,768,128]{2,1,0:T(8,128)S(1)}, u32[]{:S(2)}, u32[]{:S(2)}) collective-permute-start(f32[2,768,128]{2,1,0:T(8,128)} %get-tuple-element.21), channel_id=1, source_target_pairs={{1,0},{2,1},{3,2},{5,4},{6,5},{7,6},{9,8},{10,9},{11,10},{13,12},{... | collective-permute-start | bytes 2359304 | tf_op jit(solution)/shard_map/ppermute | solution.py:27
  202.5 12.2 %collective-permute-start.29 = (f32[6,128,256]{2,1,0:T(8,128)S(1)}, f32[6,128,256]{2,1,0:T(8,128)S(1)}, u32[]{:S(2)}, u32[]{:S(2)}) collective-permute-start(f32[6,128,256]{2,1,0:T(8,128)S(1)} %pad_maximum_fusion.2), channel_id=1, source_target_pairs={{0,1},{1,0},{2,3},{3,2},{4,5},{5,4},{6,7},{7,6},{8,9},{9,8},{10,11... | collective-permute-start | bytes 2359304 | tf_op jit(solution)/shard_map/ppermute | solution.py:495
  212.7 16.6 %copy-start = (f32[2,768,128]{2,1,0:T(8,128)}, f32[2,768,128]{2,1,0:T(8,128)S(1)}, u32[]{:S(2)}) copy-start(f32[2,768,128]{2,1,0:T(8,128)S(1)} %collective-permute-done.30.right_ref) | copy-start | bytes 2359300
  212.8 16.5 %collective-permute-start.31 = (f32[2,128,896]{2,1,0:T(8,128)S(1)}, f32[2,128,896]{2,1,0:T(8,128)S(1)}, u32[]{:S(2)}, u32[]{:S(2)}) collective-permute-start(f32[2,128,896]{2,1,0:T(8,128)S(1)} %pad_maximum_fusion.1), channel_id=1, source_target_pairs={{4,0},{8,4},{12,8},{16,12},{20,16},{24,20},{28,24},{5,1},{9,5},{13... | collective-permute-start | bytes 2752520 | tf_op jit(solution)/shard_map/ppermute | solution.py:27
  229.4 1.0 copy-start.2
where the time goes:
time: 236 us; the launch traced here: 235 us
  Pallas kernels  92.6 us (39%)
  starting transfers between devices  61.2 us (26%)
  waiting for transfers between devices  59.6 us (25%)
  local copies, waits for them, and re-layouts  13.8 us (6%)
  other arithmetic  6.74 us (3%)
    pallas_call x1, Pallas kernels, object_sweeps(): pl.pallas_call(sweeps_kernel, out_shape=(jax.ShapeDtypeStruct(obj.shape,...  51.4 us
    ppermute x14, starting transfers between devices, shift(): return lax.ppermute(block, axis, route)  43.4 us
    ppermute x7, waiting for transfers between devices, gather_rows(): got = lax.ppermute(data, axis, route)  34.6 us
    pallas_call x1, Pallas kernels, frames_update(): pl.pallas_call(frames_kernel, out_shape=(jax.ShapeDtypeStruct(dual.shape,...  26.5 us
    ppermute x14, waiting for transfers between devices, shift(): return lax.ppermute(block, axis, route)  25 us
    ppermute x7, starting transfers between devices, scatter_rows(): total = total + lax.ppermute(piece, axis, route)  9.26 us
    ppermute x7, starting transfers between devices, gather_rows(): got = lax.ppermute(data, axis, route)  7.68 us
    unnamed x21, local copies, waits for them, and re-layouts  5.41 us
  transfers between devices with their start and end apart: 32, of which 7 were waited for; matrix products, arithmetic and copies ran while one was open for 7% of the time, Pallas kernels for 26%

commit v1 on v0

v1 whole, which is shorter than its diff:
```python
import math

import jax
import jax.numpy as jnp
import numpy as np
from jax import lax
from jax.experimental import pallas as pl
from jax.experimental.pallas import tpu as pltpu
from jax.sharding import PartitionSpec as P


SWEEPS = 4
HALO = 8

amp_floor = 1.0
obj_weight = 0.5
smooth_weight = 16.0
probe_weight = 1.0

VMEM_SPEC = pl.BlockSpec(memory_space=pltpu.VMEM)
VMEM_LIMIT = 60 * 1024 * 1024


def shift(block, axis, distance):
    count = lax.axis_size(axis)
    route = [(i, i + distance) for i in range(count) if 0 <= i + distance < count]
    return lax.ppermute(block, axis, route)


def swap(block, axis, mask):
    return lax.ppermute(block, axis, [(i, i ^ mask) for i in range(lax.axis_size(axis))])


def split_two(value):
    high = value.astype(jnp.bfloat16)
    low = (value - high.astype(jnp.float32)).astype(jnp.bfloat16)
    return high, low


def dft_weights(width):
    half = width // 2
    k = np.arange(half)[:, None]
    j = np.arange(half)[None, :]
    mats = []
    for parity in range(2):
        angle = 2.0 * math.pi * ((k * (2 * j + parity)) % width) / width
        re = np.cos(angle) / math.sqrt(width)
        im = -np.sin(angle) / math.sqrt(width)
        mats.append(np.block([[re, im], [-im, re]]))
    pairs = []
    for m in mats + [m.T for m in mats]:
        high = m.astype(np.float32).astype(jnp.bfloat16)
        low = (m - high.astype(np.float64)).astype(np.float32).astype(jnp.bfloat16)
        pairs.append(np.stack([high, low]))
    order = np.concatenate([np.arange(0, width, 2), np.arange(1, width, 2)])
    perm = np.zeros((width, width), np.float32)
    perm[order, np.arange(width)] = 1.0
    return np.stack(pairs), perm.astype(jnp.bfloat16)


def mark_block(place_ref, origin, part, shape):
    lane = lane_of(shape)
    row = lax.broadcasted_iota(jnp.int32, shape, 0)
    block = jnp.zeros(shape, jnp.int32)
    for frame in range(place_ref.shape[0]):
        block = jnp.where((lane == frame) & (row == 0), place_ref[frame, part] + origin + 1, block)
    return block.astype(jnp.float32)


def lane_of(shape):
    return lax.broadcasted_iota(jnp.int32, shape, len(shape) - 1)


def edge_block(right_part, left_part):
    lane = lane_of(right_part.shape)
    width = right_part.shape[-1]
    return jnp.where(lane < HALO, right_part, jnp.where(lane >= width - HALO, left_part, 0.0))


def frames_kernel(
    place_ref, self_ref, amp_low_ref, amp_high_ref, patch_ref, dual_ref, probe_ref, pair_ref, perm_ref,
    obj_low_ref, obj_high_ref, obj_first_ref, obj_last_ref,
    new_ref, keep_ref, give_ref, canvas_ref, lead_ref, trail_ref, down_ref, up_ref,
    even_ref, odd_ref, num_ref, right_ref, left_ref,
):
    frame = pl.program_id(0)
    modes = probe_ref.shape[0]
    width = probe_ref.shape[-1]
    half = width // 2

    @pl.when(frame == 0)
    def _():
        canvas_ref[...] = jnp.zeros_like(canvas_ref)
        num_ref[...] = jnp.zeros_like(num_ref)
        for n in range(4):
            high, low = pair_ref[n, 0], pair_ref[n, 1]
            for k, m in enumerate((high, high, low)):
                right_ref[n, k * width : (k + 1) * width, :] = m
            for k, m in enumerate((high, low, high)):
                left_ref[(n + 2) % 4, :, k * width : (k + 1) * width] = m

    def dot(a, b):
        return jnp.dot(a, b, preferred_element_type=jnp.float32)

    def times_right(value, which):
        high, low = split_two(value)
        return dot(jnp.concatenate([high, low, high], axis=1), right_ref[which])

    def times_left(which, value):
        high, low = split_two(value)
        return dot(left_ref[which], jnp.concatenate([high, high, low], axis=0))

    patch_re = patch_ref[0, 0]
    patch_im = patch_ref[0, 1]

    def exit_wave(m):
        probe_re = probe_ref[m, 0]
        probe_im = probe_ref[m, 1]
        return probe_re * patch_re - probe_im * patch_im, probe_re * patch_im + probe_im * patch_re

    amps = []
    for parity in range(2):
        every = pl.ds(parity, half, stride=2)
        rows = jnp.concatenate([amp_low_ref[0, every, :], amp_high_ref[0, every, :]], axis=1)
        first = rows.astype(jnp.bfloat16)
        rest = rows - first.astype(jnp.float32)
        second, third = split_two(rest)
        amps.append(dot(first, perm_ref[...]) + (dot(second, perm_ref[...]) + dot(third, perm_ref[...])))

    power = [None, None]
    for m in range(modes):
        exit_re, exit_im = exit_wave(m)
        wave_re = exit_re + dual_ref[0, m, 0]
        wave_im = exit_im + dual_ref[0, m, 1]
        sums = jnp.concatenate(
            [wave_re[:, :half] + wave_re[:, half:], wave_im[:, :half] + wave_im[:, half:]], axis=1
        )
        diffs = jnp.concatenate(
            [wave_re[:, :half] - wave_re[:, half:], wave_im[:, :half] - wave_im[:, half:]], axis=1
        )
        even = times_right(sums, 0)
        odd = times_right(diffs, 1)

        def stack(op):
            return jnp.concatenate(
                [
                    jnp.concatenate([op(x[:half, part], x[half:, part]) for x in (even, odd)], axis=1)
                    for part in (slice(0, half), slice(half, width))
                ],
                axis=0,
            )

        far_even = times_left(0, stack(lambda a, b: a + b))
        far_odd = times_left(1, stack(lambda a, b: a - b))
        even_ref[m] = far_even
        odd_ref[m] = far_odd
        for parity, far in enumerate((far_even, far_odd)):
            term = far[:half] * far[:half] + far[half:] * far[half:]
            power[parity] = term if m == 0 else power[parity] + term

    ratios = []
    for parity in range(2):
        ratio = amps[parity] / jnp.sqrt(power[parity] + amp_floor)
        ratios.append(jnp.concatenate([ratio, ratio], axis=0))

    start_row = pl.multiple_of(place_ref[frame, 0], half)
    start_col = pl.multiple_of(place_ref[frame, 1], half)
    obj_re = jnp.zeros((width, width), jnp.float32)
    obj_im = jnp.zeros((width, width), jnp.float32)
    for m in range(modes):
        even = times_left(2, even_ref[m] * ratios[0])
        odd = times_left(3, odd_ref[m] * ratios[1])
        top = even + odd
        bottom = even - odd

        def rows_of(part):
            return jnp.concatenate(
                [
                    jnp.concatenate([x[:half, part], x[half:, part]], axis=1)
                    for x in (top, bottom)
                ],
                axis=0,
            )

        even = times_right(rows_of(slice(0, half)), 2)
        odd = times_right(rows_of(slice(half, width)), 3)
        low = even + odd
        high = even - odd
        near_re = jnp.concatenate([low[:, :half], high[:, :half]], axis=1)
        near_im = jnp.concatenate([low[:, half:], high[:, half:]], axis=1)
        exit_re, exit_im = exit_wave(m)
        new_re = dual_ref[0, m, 0] + exit_re - near_re
        new_im = dual_ref[0, m, 1] + exit_im - near_im
        new_ref[0, m, 0] = new_re
        new_ref[0, m, 1] = new_im
        target_re = near_re - new_re
        target_im = near_im - new_im
        num_ref[2 * m] += patch_re * target_re + patch_im * target_im
        num_ref[2 * m + 1] += patch_re * target_im - patch_im * target_re
        probe_re = probe_ref[m, 0]
        probe_im = probe_ref[m, 1]
        obj_re += probe_re * target_re + probe_im * target_im
        obj_im += probe_re * target_im - probe_im * target_re
    num_ref[2 * modes] += patch_re * patch_re + patch_im * patch_im
    canvas_ref[0, pl.ds(start_row, width), pl.ds(start_col, width)] += obj_re
    canvas_ref[1, pl.ds(start_row, width), pl.ds(start_col, width)] += obj_im

    @pl.when(frame == pl.num_programs(0) - 1)
    def _():
        grow = canvas_ref.shape[1]
        tile = grow - half
        blocks = grow // half
        kept = pl.multiple_of(self_ref[2] * half, half)
        given = pl.multiple_of((1 - self_ref[2]) * half, half)
        keep_ref[...] = num_ref[:, pl.ds(kept, half), :]
        give_ref[...] = num_ref[:, pl.ds(given, half), :]
        for part in range(2):
            origin = self_ref[part] * tile
            lead_ref[part, :grow, :] = canvas_ref[part, :, tile:]
            down_ref[part, : half + HALO, :] = canvas_ref[part, tile - HALO :, :]
            up_ref[part, :HALO, :] = canvas_ref[part, :HALO, :]
            ends = edge_block(canvas_ref[part, :, :half], canvas_ref[part, :, tile - half : tile]).T
            for n in range(blocks):
                at = slice(n * half, (n + 1) * half)
                trail_ref[part, n * HALO : (n + 1) * HALO, :] = ends[:HALO, at]
                lead_ref[part, grow + n * HALO : grow + (n + 1) * HALO, :] = ends[half - HALO :, at]
            ends = edge_block(obj_low_ref[part], obj_high_ref[part]).T
            for n in range(blocks - 1):
                at = slice(n * half, (n + 1) * half)
                to = (blocks + n) * HALO
                trail_ref[part, to : to + HALO, :] = ends[:HALO, at]
                lead_ref[part, grow + to : grow + to + HALO, :] = ends[half - HALO :, at]
            note = mark_block(place_ref, origin, part, (HALO, half))
            to = (2 * blocks - 1) * HALO
            trail_ref[part, to:, :] = note
            lead_ref[part, grow + to :, :] = note
            down_ref[part, half + HALO : half + 2 * HALO, :tile] = obj_last_ref[part]
            up_ref[part, HALO : 2 * HALO, :tile] = obj_first_ref[part]
            for ref, at in ((down_ref, half + 2 * HALO), (up_ref, 2 * HALO)):
                ref[part, at - HALO : at, tile:] = jnp.zeros((HALO, half), jnp.float32)
                ref[part, at:, :half] = note
                ref[part, at:, half:] = jnp.zeros((HALO, tile), jnp.float32)


def frames_update(amplitude, patches, dual, probe, obj, places, self_index):
    count, modes = dual.shape[:2]
    width = amplitude.shape[-1]
    pairs, perm = dft_weights(width)
    half = width // 2
    tile = obj.shape[1]
    grow = tile + half
    notes = 2 * grow // half * HALO
    last = tile // half - 1
    messages = (
        (2 * modes + 1, half, width),
        (2 * modes + 1, half, width),
        (2, grow, grow),
        (2, grow + notes, half),
        (2, notes, half),
        (2, half + 3 * HALO, grow),
        (2, 3 * HALO, grow),
    )

    def whole(shape):
        return pl.BlockSpec(shape, lambda f, *_: (0,) * len(shape))

    return pl.pallas_call(
        frames_kernel,
        out_shape=(jax.ShapeDtypeStruct(dual.shape, jnp.float32),)
        + tuple(jax.ShapeDtypeStruct(m, jnp.float32) for m in messages),
        grid_spec=pltpu.PrefetchScalarGridSpec(
            num_scalar_prefetch=2,
            grid=(count,),
            in_specs=[
                pl.BlockSpec((1, width, half), lambda f, *_: (f, 0, 0)),
                pl.BlockSpec((1, width, half), lambda f, *_: (f, 0, 1)),
                pl.BlockSpec((1, 2, width, width), lambda f, *_: (f, 0, 0, 0)),
                pl.BlockSpec((1, modes, 2, width, width), lambda f, *_: (f, 0, 0, 0, 0)),
                whole(probe.shape),
                whole(pairs.shape),
                whole(perm.shape),
                pl.BlockSpec((2, tile, half), lambda f, *_: (0, 0, 0)),
                pl.BlockSpec((2, tile, half), lambda f, *_: (0, 0, last)),
                pl.BlockSpec((2, HALO, tile), lambda f, *_: (0, 0, 0)),
                pl.BlockSpec((2, HALO, tile), lambda f, *_: (0, tile // HALO - 1, 0)),
            ],
            out_specs=[
                pl.BlockSpec((1, modes, 2, width, width), lambda f, *_: (f, 0, 0, 0, 0)),
            ]
            + [whole(m) for m in messages],
            scratch_shapes=[
                pltpu.VMEM((modes, width, width), jnp.float32),
                pltpu.VMEM((modes, width, width), jnp.float32),
                pltpu.VMEM((2 * modes + 1, width, width), jnp.float32),
                pltpu.VMEM((4, 3 * width, width), jnp.bfloat16),
                pltpu.VMEM((4, width, 3 * width), jnp.bfloat16),
            ],
        ),
        compiler_params=pltpu.CompilerParams(vmem_limit_bytes=VMEM_LIMIT),
        cost_estimate=pl.CostEstimate(
            flops=count * modes * 24 * 2 * width**3, bytes_accessed=20 << 20, transcendentals=0
        ),
        name="frames",
    )(
        places, self_index, amplitude, amplitude, patches, dual, probe,
        jnp.asarray(pairs), jnp.asarray(perm), obj, obj, obj, obj,
    )


def weights_kernel(place_ref, bound_ref, probe_ref, out_ref, sums_ref):
    modes = probe_ref.shape[0]
    width = probe_ref.shape[-1]
    half = width // 2
    rows = out_ref.shape[1]
    tile = rows - 2 * HALO
    power = jnp.zeros((width, width), jnp.float32)
    for m in range(modes):
        power += probe_ref[m, 0] * probe_ref[m, 0] + probe_ref[m, 1] * probe_ref[m, 1]
    sums_ref[...] = jnp.zeros_like(sums_ref)

    def place(frame, carry):
        row = place_ref[frame, 0]
        col = place_ref[frame, 1]

        @pl.when((row >= -width) & (row <= tile) & (col >= -width) & (col <= tile))
        def _():
            at_row = pl.ds(pl.multiple_of(row + width, half), width)
            at_col = pl.ds(pl.multiple_of(col + width, half), width)
            sums_ref[at_row, at_col] += power

        return carry

    lax.fori_loop(0, place_ref.shape[0], place, 0)
    low_row, high_row, low_col, high_col = (bound_ref[n] for n in range(4))

    chunk = 56

    def finish(step, carry):
        base = pl.multiple_of(step * chunk, 8)
        at = pl.ds(pl.multiple_of(base + width - HALO, 8), chunk)
        den = jnp.concatenate(
            [
                sums_ref[at, width : width + tile],
                edge_block(sums_ref[at, width + tile : width + tile + half], sums_ref[at, half:width]),
            ],
            axis=1,
        )
        row = lax.broadcasted_iota(jnp.int32, den.shape, 0) + (base - HALO)
        lane = lane_of(den.shape)
        col = jnp.where(lane >= tile + half - HALO, lane - (tile + half), lane)
        inside = (row >= low_row) & (row < high_row) & (col >= low_col) & (col < high_col)
        ratio = jnp.where(inside, smooth_weight / (den + (obj_weight + 4.0 * smooth_weight)), 0.0)
        for n in range(out_ref.shape[0]):
            out_ref[n, pl.ds(base, chunk), :] = ratio[:, n * half : (n + 1) * half]
        return carry

    lax.fori_loop(0, rows // chunk, finish, 0)


def object_weights(places, bounds, probe, tile):
    width = probe.shape[-1]
    smem = pl.BlockSpec(memory_space=pltpu.SMEM)
    return pl.pallas_call(
        weights_kernel,
        out_shape=jax.ShapeDtypeStruct(
            (2 * tile // width + 1, tile + 2 * HALO, width // 2), jnp.float32
        ),
        in_specs=[smem, smem, VMEM_SPEC],
        out_specs=VMEM_SPEC,
        scratch_shapes=[pltpu.VMEM((tile + 2 * width, tile + 2 * width), jnp.float32)],
        compiler_params=pltpu.CompilerParams(vmem_limit_bytes=VMEM_LIMIT),
        name="weights",
    )(places, bounds, probe)


PAD = 8


def sweeps_kernel(
    canvas_ref, lead_ref, trail_ref, above_ref, below_ref, corner_above_ref, corner_below_ref,
    obj_ref, weight_ref, *refs,
):
    field_ref, edge_ref, head_ref, rhs_ref, first_ref, second_ref = refs[-6:]
    tile = obj_ref.shape[1]
    half = lead_ref.shape[-1]
    rows = tile + 2 * HALO
    grow = tile + half
    blocks = grow // half
    wide = blocks - 1
    chunk = 56
    tall = half + HALO
    own = slice(PAD + HALO, PAD + HALO + tile)
    upper = slice(PAD, PAD + HALO)
    lower = slice(PAD + HALO + tile, PAD + 2 * HALO + tile)
    near_top = slice(PAD + HALO, PAD + HALO + half)
    lane = lane_of((rows, half))

    def thin(ref, start, count):
        return jnp.concatenate(
            [ref[0, start + n * HALO : start + (n + 1) * HALO, :] for n in range(count)], axis=1
        )

    def halo(middle, above, below):
        return jnp.concatenate(
            [above[:, :half], middle[:, :half] + above[:, half:], middle[:, half:tile], middle[:, tile:] + below],
            axis=1,
        )

    def columns(right_halo, left_halo):
        gap = jnp.zeros((half - 2 * HALO, right_halo.shape[1]), jnp.float32)
        return jnp.concatenate([right_halo, gap, left_halo], axis=0).T[half - HALO : half + tile + HALO]

    nothing = jnp.zeros((HALO, half), jnp.float32)
    sides = columns(
        halo(
            thin(trail_ref, 0, blocks),
            thin(corner_above_ref, tall + 4 * HALO, 2),
            corner_below_ref[0, 4 * HALO : 5 * HALO, :],
        ),
        halo(
            thin(lead_ref, grow, blocks),
            thin(corner_above_ref, tall, 2),
            corner_below_ref[0, HALO : 2 * HALO, :],
        ),
    )
    first_ref[wide, PAD : PAD + rows, :] = columns(
        halo(
            jnp.concatenate([thin(trail_ref, blocks * HALO, blocks - 1), nothing], axis=1),
            jnp.concatenate([corner_above_ref[0, tall + 6 * HALO : tall + 7 * HALO, :], nothing], axis=1),
            corner_below_ref[0, 5 * HALO : 6 * HALO, :],
        ),
        halo(
            jnp.concatenate([thin(lead_ref, grow + blocks * HALO, blocks - 1), nothing], axis=1),
            jnp.concatenate([corner_above_ref[0, tall + 2 * HALO : tall + 3 * HALO, :], nothing], axis=1),
            corner_below_ref[0, 2 * HALO : 3 * HALO, :],
        ),
    )
    for n in range(blocks):
        at = slice(n * half, (n + 1) * half)
        if n < wide:
            first_ref[n, upper, :] = above_ref[0, tall : tall + HALO, at]
            first_ref[n, own, :] = obj_ref[0, :, at]
            first_ref[n, lower, :] = below_ref[0, HALO : 2 * HALO, at]
        rhs_ref[n, upper, :] = above_ref[0, :HALO, at]
        rhs_ref[n, own, :] = canvas_ref[0, :tile, at]
        rhs_ref[n, lower, :] = canvas_ref[0, tile : tile + HALO, at] + below_ref[0, :HALO, at]
        rhs_ref[n, near_top, :] += above_ref[0, HALO:tall, at]
        for ref in (first_ref, second_ref):
            ref[n, :PAD, :] = jnp.zeros((PAD, half), jnp.float32)
            ref[n, PAD + rows :, :] = jnp.zeros((PAD, half), jnp.float32)
    rhs_ref[0, PAD + HALO : PAD + 2 * HALO + tile, :] += lead_ref[0, : tile + HALO, :]
    rhs_ref[0, PAD : PAD + tall, :] += corner_above_ref[0, :tall, :]
    rhs_ref[0, lower, :] += corner_below_ref[0, :HALO, :]
    rhs_ref[wide, PAD : PAD + rows, :] = sides + jnp.where(
        lane < HALO, rhs_ref[wide, PAD : PAD + rows, :], 0.0
    )

    def prepare(step, carry):
        base = pl.multiple_of(step * chunk, 8)
        for n in range(blocks):
            at = pl.ds(base + PAD, chunk)
            rhs_ref[n, at, :] = (rhs_ref[n, at, :] + obj_weight * first_ref[n, at, :]) * (
                weight_ref[n, pl.ds(base, chunk), :] * (1.0 / smooth_weight)
            )
        return carry

    lax.fori_loop(0, rows // chunk, prepare, 0)
    narrow = lane_of((8, half))
    stride = 2 * chunk

    def sweep(source, target):
        def step_rows(step, carry):
            base = pl.multiple_of(step * stride, 8)

            def turned(group):
                at = pl.ds(base + (PAD + 8 * group), 8)
                mids = [source[n, at, :] for n in range(blocks)]
                return [pltpu.roll(m, 1, 1) for m in mids], [pltpu.roll(m, half - 1, 1) for m in mids]

            ahead = turned(0)
            for group in range(stride // 8):
                froms, tos = ahead
                if group + 1 < stride // 8:
                    ahead = turned(group + 1)
                here = base + (PAD + 8 * group)
                for n in range(blocks):
                    west = jnp.where(narrow == 0, froms[n - 1], froms[n])
                    east = jnp.where(narrow == half - 1, tos[(n + 1) % blocks], tos[n])
                    north = source[n, pl.ds(here - 1, 8), :]
                    south = source[n, pl.ds(here + 1, 8), :]
                    target[n, pl.ds(here, 8), :] = rhs_ref[n, pl.ds(here, 8), :] + weight_ref[
                        n, pl.ds(base + 8 * group, 8), :
                    ] * ((north + south) + (west + east))
            return carry

        lax.fori_loop(0, rows // stride, step_rows, 0)

    source, target = first_ref, second_ref
    for _ in range(SWEEPS):
        sweep(source, target)
        source, target = target, source
    for n in range(wide):
        at = slice(n * half, (n + 1) * half)
        field_ref[0, :, at] = source[n, own, :]
        head_ref[0, :, at] = source[n, near_top, :]
    edge_ref[0] = source[0, own, :]


def object_sweeps(part, canvas, lead, trail, above, below, corner_above, corner_below, obj, weight, field):
    tile = obj.shape[1]
    half = lead.shape[-1]
    work = pltpu.VMEM((tile // half + 1, tile + 2 * HALO + 2 * PAD, half), jnp.float32)
    sources = [canvas, lead, trail, above, below, corner_above, corner_below, obj]

    def one(shape):
        return pl.BlockSpec((1,) + tuple(shape[1:]), lambda g: (part, 0, 0))

    extra = [] if field is None else [field]
    return pl.pallas_call(
        sweeps_kernel,
        out_shape=(
            jax.ShapeDtypeStruct(obj.shape, jnp.float32),
            jax.ShapeDtypeStruct((1, tile, half), jnp.float32),
            jax.ShapeDtypeStruct((1, half, tile), jnp.float32),
        ),
        grid=(1,),
        in_specs=[one(x.shape) for x in sources]
        + [pl.BlockSpec(weight.shape, lambda g: (0, 0, 0))]
        + [pl.BlockSpec(memory_space=pl.ANY)] * len(extra),
        out_specs=[
            one(obj.shape),
            pl.BlockSpec((1, tile, half), lambda g: (0, 0, 0)),
            pl.BlockSpec((1, half, tile), lambda g: (0, 0, 0)),
        ],
        scratch_shapes=[work, work, work],
        input_output_aliases={9: 0} if extra else {},
        compiler_params=pltpu.CompilerParams(vmem_limit_bytes=VMEM_LIMIT),
    )(*sources, weight, *extra)


def windows_kernel(place_ref, field_ref, *refs):
    strips = refs[:6]
    out_ref, whole_ref, load_sem, store_sem = refs[6:]
    tile = field_ref.shape[1]
    width = out_ref.shape[-1]
    half = width // 2
    loads = [pltpu.make_async_copy(field_ref, whole_ref.at[:, :tile, :tile], load_sem.at[0])]
    for part in range(2):
        spots = (
            whole_ref.at[part, :tile, tile:],
            whole_ref.at[part, tile:, :tile],
            whole_ref.at[part, tile:, tile:],
        )
        for n, spot in enumerate(spots):
            loads.append(
                pltpu.make_async_copy(strips[3 * part + n].at[0], spot, load_sem.at[1 + 3 * part + n])
            )
    for copy in loads:
        copy.start()
    for copy in loads:
        copy.wait()
    stores = []
    for frame in range(out_ref.shape[0]):
        row = pl.multiple_of(place_ref[frame, 0], half)
        col = pl.multiple_of(place_ref[frame, 1], half)
        stores.append(
            pltpu.make_async_copy(
                whole_ref.at[:, pl.ds(row, width), pl.ds(col, width)], out_ref.at[frame], store_sem.at[frame]
            )
        )
    for copy in stores:
        copy.start()
    for copy in stores:
        copy.wait()


def windows(places, field, strips, width):
    count = places.shape[0]
    grow = field.shape[1] + width // 2
    anywhere = pl.BlockSpec(memory_space=pl.ANY)
    return pl.pallas_call(
        windows_kernel,
        out_shape=jax.ShapeDtypeStruct((count, 2, width, width), jnp.float32),
        in_specs=[pl.BlockSpec(memory_space=pltpu.SMEM)] + [anywhere] * 7,
        out_specs=anywhere,
        scratch_shapes=[
            pltpu.VMEM((2, grow, grow), jnp.float32),
            pltpu.SemaphoreType.DMA((7,)),
            pltpu.SemaphoreType.DMA((count,)),
        ],
        compiler_params=pltpu.CompilerParams(vmem_limit_bytes=VMEM_LIMIT),
        name="windows",
    )(places, field, *strips)


def halve(data, axis, mask):
    rows = data.shape[1] // 2
    upper = (lax.axis_index(axis) & mask) != 0
    keep = jnp.where(upper, rows, 0)
    give = jnp.where(upper, 0, rows)
    got = swap(lax.dynamic_slice_in_dim(data, give, rows, axis=1), axis, mask)
    return lax.dynamic_slice_in_dim(data, keep, rows, axis=1) + got


def double(data, axis, mask):
    upper = (lax.axis_index(axis) & mask) != 0
    got = swap(data, axis, mask)
    return jnp.concatenate([jnp.where(upper, got, data), jnp.where(upper, data, got)], axis=1)


def probe_steps():
    cols, rows = lax.axis_size("col"), lax.axis_size("row")
    steps = [("col", 1 << n) for n in range(cols.bit_length() - 1)]
    return steps + [("row", 1 << n) for n in (0, *reversed(range(1, rows.bit_length() - 1)))]


def update_probe(keep, give, probe):
    parts = keep.shape[0] - 1
    width = probe.shape[-1]
    flat = probe.reshape(parts, width, width)
    steps = probe_steps()
    piece = keep + swap(give, *steps[0])
    offset = jnp.zeros((), jnp.int32)
    span = width
    for n, (axis, mask) in enumerate(steps):
        if n > 0:
            piece = halve(piece, axis, mask)
        span = span // 2
        offset = offset + jnp.where((lax.axis_index(axis) & mask) != 0, span, 0)
    mine = lax.dynamic_slice_in_dim(flat, offset, span, axis=1)
    fresh = (piece[:parts] + probe_weight * mine) / (piece[parts:] + probe_weight)
    for n, (axis, mask) in reversed(list(enumerate(steps))):
        fresh = double(fresh, axis, mask)
    return fresh.reshape(probe.shape)


def per_device(amplitude, patches, dual, probe, obj, positions):
    width = amplitude.shape[-1]
    half = width // 2
    tile = obj.shape[1]
    count = positions.shape[0]
    row_index = lax.axis_index("row")
    col_index = lax.axis_index("col")
    origin = jnp.stack([row_index * tile, col_index * tile]).astype(jnp.int32)
    places = positions - origin
    self_index = jnp.stack([row_index, col_index, col_index & 1]).astype(jnp.int32)

    dual_new, keep, give, canvas, lead, trail, down, up = frames_update(
        amplitude, patches, dual, probe, obj, places, self_index
    )
    lead = shift(lead, "col", 1)
    trail = shift(trail, "col", -1)
    above = shift(down, "row", 1)
    below = shift(up, "row", -1)
    grow = tile + half
    blocks = grow // half
    notes = (2 * blocks - 1) * HALO
    corner_down = jnp.concatenate(
        [
            lead[:, tile - HALO : grow],
            lead[:, grow + (blocks - 2) * HALO : grow + blocks * HALO],
            lead[:, grow + notes - HALO :],
            trail[:, (blocks - 2) * HALO : blocks * HALO],
            trail[:, notes - HALO :],
        ],
        axis=1,
    )
    corner_up = jnp.concatenate(
        [
            lead[:, :HALO],
            lead[:, grow : grow + HALO],
            lead[:, grow + blocks * HALO : grow + (blocks + 1) * HALO],
            lead[:, grow + notes :],
            trail[:, :HALO],
            trail[:, blocks * HALO : (blocks + 1) * HALO],
            trail[:, notes:],
        ],
        axis=1,
    )
    corner_above = shift(corner_down, "row", 1)
    corner_below = shift(corner_up, "row", -1)
    tall = half + HALO
    own_marks = (positions + 1).astype(jnp.float32).T
    marks = jnp.concatenate(
        [
            own_marks,
            lead[:, grow + notes, :count],
            trail[:, notes, :count],
            above[:, tall + HALO, :count],
            below[:, 2 * HALO, :count],
            corner_above[:, tall + 3 * HALO, :count],
            corner_above[:, tall + 7 * HALO, :count],
            corner_below[:, 3 * HALO, :count],
            corner_below[:, 6 * HALO, :count],
        ],
        axis=1,
    )
    marks = marks.T.astype(jnp.int32)
    around = jnp.where(marks > 0, marks - 1 - origin, -tile * 4)
    bounds = jnp.stack(
        [
            -row_index * tile,
            (lax.axis_size("row") - row_index) * tile,
            -col_index * tile,
            (lax.axis_size("col") - col_index) * tile,
        ]
    ).astype(jnp.int32)
    weight = object_weights(around, bounds, probe, tile)
    field = None
    strips = []
    for part in range(2):
        field, edge, head = object_sweeps(
            part, canvas, lead, trail, above, below, corner_above, corner_below, obj, weight, field
        )
        far_below = shift(head, "row", -1)
        far_right = shift(edge, "col", -1)
        far_corner = shift(far_right[:, :half, :], "row", -1)
        strips += [far_right, far_below, far_corner]
    probe_new = update_probe(keep, give, probe)
    patches_new = windows(places, field, strips, width)
    return (dual_new, field, probe_new, patches_new)


def solution(mesh):
    return jax.shard_map(
        per_device,
        mesh=mesh,
        in_specs=(
            P(("row", "col"), None, None),
            P(("row", "col"), None, None, None),
            P(("row", "col"), None, None, None, None),
            P(),
            P(None, "row", "col"),
            P(("row", "col"), None),
        ),
        out_specs=(
            P(("row", "col"), None, None, None, None),
            P(None, "row", "col"),
            P(),
            P(("row", "col"), None, None, None),
        ),
        check_vma=False,
    )
```

time: 236 us -> 187 us (0.79)
  Pallas kernels: 92.6 us -> 69 us
  local copies, waits for them, and re-layouts: 13.8 us -> 1.78 us
  starting transfers between devices: 61.2 us -> 49.8 us
  waiting for transfers between devices: 59.6 us -> 55.7 us
    pallas_call x1 -> x2, Pallas kernels: 51.4 us -> 31.1 us  [object_sweeps(): pl.pallas_call(sweeps_kernel, out_shape=(jax.ShapeDtypeStruct(obj.shape,...]
    ppermute x14 -> x12, waiting for transfers between devices: 25 us -> 14.4 us  [shift(): return lax.ppermute(block, axis, route)]
    ppermute x14 -> x12, starting transfers between devices: 43.4 us -> 33.2 us  [shift(): return lax.ppermute(block, axis, route)]
    slice x6 -> x8, local copies, waits for them, and re-layouts: 6.8 us -> 0.03 us  [the longest x2 0.01 us: per_device(): far_corner = shift(far_right[:, :half, :], 'row', -1)]
    ppermute x18 -> x10, waiting for transfers between devices: 34.6 us -> 41.2 us  [swap(): lax.ppermute(block, axis, [(i, i ^ mask) for i in range(lax.axis_size(axi...]
    pallas_call x2 -> x1, Pallas kernels: 9.87 us -> 5.25 us  [object_weights(): pl.pallas_call(weights_kernel, out_shape=jax.ShapeDtypeStruct((2 * tile /...]
    unnamed x21 -> x37, local copies, waits for them, and re-layouts: 5.41 us -> 1.45 us
    ppermute x18 -> x10, starting transfers between devices: 17.8 us -> 16.6 us  [swap(): lax.ppermute(block, axis, [(i, i ^ mask) for i in range(lax.axis_size(axi...]
  transfers between devices with their start and end apart: 32 -> 22, of which waited for: 7 -> 15; matrix products, arithmetic and copies ran while one was open for 7% -> 2% of each run, Pallas kernels for 26% -> 22%
where the time goes in v1:
time: 187 us; the launch traced here: 185 us
  Pallas kernels  69 us (37%)
  waiting for transfers between devices  55.7 us (30%)
  starting transfers between devices  49.8 us (27%)
  other arithmetic  7.6 us (4%)
    ppermute x10, waiting for transfers between devices, swap(): lax.ppermute(block, axis, [(i, i ^ mask) for i in range(lax.axis_size(axi...  41.2 us
    ppermute x12, starting transfers between devices, shift(): return lax.ppermute(block, axis, route)  33.2 us
    pallas_call x2, Pallas kernels, object_sweeps(): pl.pallas_call(sweeps_kernel, out_shape=(jax.ShapeDtypeStruct(obj.shape,...  31.1 us
    pallas_call x1, Pallas kernels, frames_update(): pl.pallas_call(frames_kernel, out_shape=(jax.ShapeDtypeStruct(dual.shape,...  27.7 us
    ppermute x10, starting transfers between devices, swap(): lax.ppermute(block, axis, [(i, i ^ mask) for i in range(lax.axis_size(axi...  16.6 us
    ppermute x12, waiting for transfers between devices, shift(): return lax.ppermute(block, axis, route)  14.4 us
    pallas_call x1, Pallas kernels, object_weights(): pl.pallas_call(weights_kernel, out_shape=jax.ShapeDtypeStruct((2 * tile /...  5.25 us
    pallas_call x1, Pallas kernels, windows(): pl.pallas_call(windows_kernel, out_shape=jax.ShapeDtypeStruct((count, 2,...  4.88 us
  transfers between devices with their start and end apart: 22, of which 15 were waited for; matrix products, arithmetic and copies ran while one was open for 2% of the time, Pallas kernels for 22%

profile of v1, /device:TPU:9, one launch (start us, length us, event | category | flops | bytes accessed | tf_op | source)
XLA Modules:
  0.0 184.9 jit_solution(10201088979348064909)
XLA Ops:
  0.6 0.8 copy.23
  1.5 0.6 broadcast_subtract_fusion.place_ref
  2.1 0.6 pad_add_fusion.1.self_ref
  2.7 27.7 %frames.1 = (f32[4,3,2,256,256]{4,3,2,1,0:T(8,128)}, f32[7,128,256]{2,1,0:T(8,128)}, f32[7,128,256]{2,1,0:T(8,128)}, f32[2,896,896]{2,1,0:T(8,128)}, f32[2,1008,...) custom-call(s32[4,2]{1,0:T(4,128)} %broadcast_subtract_fusion.place_ref, ...), custom_call_target="tpu_custom_call" | custom-call | flops 9663676416 | bytes 20971520 | tf_op jit(solution)/shard_map/frames/pallas_call | solution.py:267
  30.4 0.8 collective-permute-start.6
  31.2 3.0 %collective-permute-start = (f32[2,1008,128]{2,1,0:T(8,128)}, f32[2,1008,128]{2,1,0:T(8,128)S(1)}, u32[]{:S(2)}, u32[]{:S(2)}) collective-permute-start(f32[2,1008,128]{2,1,0:T(8,128)} %get-tuple-element.20), channel_id=1, source_target_pairs={{0,1},{1,2},{2,3},{4,5},{5,6},{6,7},{8,9},{9,10},{10,11},{12,13},{... | collective-permute-start | bytes 3096584 | tf_op jit(solution)/shard_map/ppermute | solution.py:27
  34.2 1.9 %collective-permute-start.1 = (f32[2,112,128]{2,1,0:T(8,128)}, f32[2,112,128]{2,1,0:T(8,128)S(1)}, u32[]{:S(2)}, u32[]{:S(2)}) collective-permute-start(f32[2,112,128]{2,1,0:T(8,128)} %get-tuple-element.21), channel_id=1, source_target_pairs={{1,0},{2,1},{3,2},{5,4},{6,5},{7,6},{9,8},{10,9},{11,10},{13,12},{... | collective-permute-start | bytes 344072 | tf_op jit(solution)/shard_map/ppermute | solution.py:27
  36.1 3.0 %collective-permute-start.3 = (f32[2,24,896]{2,1,0:T(8,128)}, f32[2,24,896]{2,1,0:T(8,128)S(1)}, u32[]{:S(2)}, u32[]{:S(2)}) collective-permute-start(f32[2,24,896]{2,1,0:T(8,128)} %get-tuple-element.23), channel_id=1, source_target_pairs={{4,0},{8,4},{12,8},{16,12},{20,16},{24,20},{28,24},{5,1},{9,5},{13... | collective-permute-start | bytes 516104 | tf_op jit(solution)/shard_map/ppermute | solution.py:27
  39.1 2.3 %collective-permute-start.2 = (f32[2,152,896]{2,1,0:T(8,128)}, f32[2,152,896]{2,1,0:T(8,128)S(1)}, u32[]{:S(2)}, u32[]{:S(2)}) collective-permute-start(f32[2,152,896]{2,1,0:T(8,128)} %get-tuple-element.22), channel_id=1, source_target_pairs={{0,4},{4,8},{8,12},{12,16},{16,20},{20,24},{24,28},{1,5},{5,9},{9,... | collective-permute-start | bytes 3268616 | tf_op jit(solution)/shard_map/ppermute | solution.py:27
  41.5 0.7 pad_add_fusion.2.bound_ref
  42.2 1.5 collective-permute-done.3.below_ref
  43.6 1.4 add.53
  45.1 0.9 collective-permute-done.lead_ref
  46.1 10.9 %collective-permute-done.7 = f32[7,64,256]{2,1,0:T(8,128)S(1)} collective-permute-done((f32[7,64,256]{2,1,0:T(8,128)S(1)}, f32[7,64,256]{2,1,0:T(8,128)S(1)}, u32[]{:S(2)}, u32[]{:S(2)}) %collective-permute-start.7) | collective-permute-done | bytes 458784 | tf_op jit(solution)/shard_map/ppermute | solution.py:31
  57.1 2.3 %collective-permute-start.8 = (f32[7,32,256]{2,1,0:T(8,128)S(1)}, f32[7,32,256]{2,1,0:T(8,128)S(1)}, u32[]{:S(2)}, u32[]{:S(2)}) collective-permute-start(f32[7,32,256]{2,1,0:T(8,128)S(1)} %constant_dynamic-slice_fusion.2), channel_id=1, source_target_pairs={{0,4},{4,0},{8,12},{12,8},{16,20},{20,16},{24,28},{28,24},{1,5},{5... | collective-permute-start | bytes 688136 | tf_op jit(solution)/shard_map/ppermute | solution.py:31
  59.3 13.3 %collective-permute-done.8 = f32[7,32,256]{2,1,0:T(8,128)S(1)} collective-permute-done((f32[7,32,256]{2,1,0:T(8,128)S(1)}, f32[7,32,256]{2,1,0:T(8,128)S(1)}, u32[]{:S(2)}, u32[]{:S(2)}) %collective-permute-start.8) | collective-permute-done | bytes 229408 | tf_op jit(solution)/shard_map/ppermute | solution.py:31
  72.7 2.4 %collective-permute-start.9 = (f32[7,16,256]{2,1,0:T(8,128)S(1)}, f32[7,16,256]{2,1,0:T(8,128)S(1)}, u32[]{:S(2)}, u32[]{:S(2)}) collective-permute-start(f32[7,16,256]{2,1,0:T(8,128)S(1)} %constant_dynamic-slice_fusion.1), channel_id=1, source_target_pairs={{0,16},{4,20},{8,24},{12,28},{16,0},{20,4},{24,8},{28,12},{1,17},{... | collective-permute-start | bytes 344072 | tf_op jit(solution)/shard_map/ppermute | solution.py:31
  75.0 3.4 %collective-permute-start.5 = (f32[2,56,128]{2,1,0:T(8,128)S(1)}, f32[2,56,128]{2,1,0:T(8,128)S(1)}, u32[]{:S(2)}, u32[]{:S(2)}) collective-permute-start(f32[2,56,128]{2,1,0:T(8,128)S(1)} %constant_dynamic-update-slice_fusion.4), channel_id=1, source_target_pairs={{4,0},{8,4},{12,8},{16,12},{20,16},{24,20},{28,24},{5,1},{9,5},{13... | collective-permute-start | bytes 172040 | tf_op jit(solution)/shard_map/ppermute | solution.py:27
  78.5 1.8 collective-permute-done.9
  80.3 0.5 collective-permute-start.10
  80.8 2.6 %collective-permute-done.10 = f32[7,8,256]{2,1,0:T(8,128)S(1)} collective-permute-done((f32[7,8,256]{2,1,0:T(8,128)S(1)}, f32[7,8,256]{2,1,0:T(8,128)S(1)}, u32[]{:S(2)}, u32[]{:S(2)}) %collective-permute-start.10) | collective-permute-done | bytes 57376 | tf_op jit(solution)/shard_map/ppermute | solution.py:31
  83.4 0.8 fusion
  84.2 0.5 collective-permute-start.11
  84.7 2.5 %collective-permute-done.11 = f32[6,8,256]{2,1,0:T(8,128)S(1)} collective-permute-done((f32[6,8,256]{2,1,0:T(8,128)S(1)}, f32[6,8,256]{2,1,0:T(8,128)S(1)}, u32[]{:S(2)}, u32[]{:S(2)}) %collective-permute-start.11) | collective-permute-done | bytes 49184 | tf_op jit(solution)/shard_map/ppermute | solution.py:31
  87.3 3.2 %collective-permute-start.12 = (f32[6,16,256]{2,1,0:T(8,128)S(1)}, f32[6,16,256]{2,1,0:T(8,128)S(1)}, u32[]{:S(2)}, u32[]{:S(2)}) collective-permute-start(f32[6,16,256]{2,1,0:T(8,128)S(1)} %pad_maximum_fusion.4), channel_id=1, source_target_pairs={{0,16},{4,20},{8,24},{12,28},{16,0},{20,4},{24,8},{28,12},{1,17},{... | collective-permute-start | bytes 294920 | tf_op jit(solution)/shard_map/ppermute | solution.py:31
  90.4 2.3 %collective-permute-done.12 = f32[6,16,256]{2,1,0:T(8,128)S(1)} collective-permute-done((f32[6,16,256]{2,1,0:T(8,128)S(1)}, f32[6,16,256]{2,1,0:T(8,128)S(1)}, u32[]{:S(2)}, u32[]{:S(2)}) %collective-permute-start.12) | collective-permute-done | bytes 98336 | tf_op jit(solution)/shard_map/ppermute | solution.py:31
  92.9 4.5 %collective-permute-done.13 = f32[6,32,256]{2,1,0:T(8,128)S(1)} collective-permute-done((f32[6,32,256]{2,1,0:T(8,128)S(1)}, f32[6,32,256]{2,1,0:T(8,128)S(1)}, u32[]{:S(2)}, u32[]{:S(2)}) %collective-permute-start.13) | collective-permute-done | bytes 196640 | tf_op jit(solution)/shard_map/ppermute | solution.py:31
  97.5 1.1 collective-permute-start.14
  98.6 2.1 %collective-permute-start.4 = (f32[2,200,128]{2,1,0:T(8,128)S(1)}, f32[2,200,128]{2,1,0:T(8,128)S(1)}, u32[]{:S(2)}, u32[]{:S(2)}) collective-permute-start(f32[2,200,128]{2,1,0:T(8,128)S(1)} %constant_dynamic-update-slice_fusion), channel_id=1, source_target_pairs={{0,4},{4,8},{8,12},{12,16},{16,20},{20,24},{24,28},{1,5},{5,9},{9,... | collective-permute-start | bytes 614408 | tf_op jit(solution)/shard_map/ppermute | solution.py:27
  100.7 3.4 %collective-permute-done.14 = f32[6,64,256]{2,1,0:T(8,128)S(1)} collective-permute-done((f32[6,64,256]{2,1,0:T(8,128)S(1)}, f32[6,64,256]{2,1,0:T(8,128)S(1)}, u32[]{:S(2)}, u32[]{:S(2)}) %collective-permute-start.14) | collective-permute-done | bytes 393248 | tf_op jit(solution)/shard_map/ppermute | solution.py:31
  104.3 5.8 %collective-permute-start.15 = (f32[6,128,256]{2,1,0:T(8,128)S(1)}, f32[6,128,256]{2,1,0:T(8,128)}, u32[]{:S(2)}, u32[]{:S(2)}) collective-permute-start(f32[6,128,256]{2,1,0:T(8,128)S(1)} %pad_maximum_fusion.1), channel_id=1, source_target_pairs={{0,1},{1,0},{2,3},{3,2},{4,5},{5,4},{6,7},{7,6},{8,9},{9,8},{10,11... | collective-permute-start | bytes 2359304 | tf_op jit(solution)/shard_map/ppermute | solution.py:31
  110.3 0.6 select_bitcast_fusion.place_ref
  110.9 5.3 %weights.1.weight_ref = f32[7,784,128]{2,1,0:T(8,128)} custom-call(s32[36,2]{1,0:T(8,128)} %select_bitcast_fusion.place_ref, s32[4]{0:T(128)} %pad_add_fusion.2.bound_ref, f32[3,2,256,256]{3,2,1,0:T(8,128)} %probe_ref.3), custom_call_target="tpu_custom_call" | custom-call | tf_op jit(solution)/shard_map/weights/pallas_call | solution.py:363
  116.2 15.6 %shard_map.111 = (f32[2,768,768]{2,1,0:T(8,128)}, f32[1,768,128]{2,1,0:T(8,128)}, f32[1,128,768]{2,1,0:T(8,128)}) custom-call(f32[2,896,896]{2,1,0:T(8,128)} %get-tuple-element.19.canvas_ref, f32[2,1008,128]{2,1,0:T(8,128)} %copy-done, f32[2,112,128]{2,1,0:T(8,128)} %copy-done.3, f32[2,152,896]{2,1,0:T(8,128)} %copy-done.1, f32[2,24,896]{2,1,0:T(8,128)} %copy-done.4, ...), custom_call_target="tpu_custom_call" | custom-call | tf_op jit(solution)/shard_map/pallas_call | solution.py:519
  131.8 15.6 %shard_map.112 = (f32[2,768,768]{2,1,0:T(8,128)}, f32[1,768,128]{2,1,0:T(8,128)}, f32[1,128,768]{2,1,0:T(8,128)}) custom-call(f32[2,896,896]{2,1,0:T(8,128)} %get-tuple-element.19.canvas_ref, f32[2,1008,128]{2,1,0:T(8,128)} %copy-done, f32[2,112,128]{2,1,0:T(8,128)} %copy-done.3, f32[2,152,896]{2,1,0:T(8,128)} %copy-done.1, ...), custom_call_target="tpu_custom_call", output_to_operand_aliasing={{0}: (9, {})} | custom-call | tf_op jit(solution)/shard_map/pallas_call | solution.py:519
  147.3 4.2 %collective-permute-start.19 = (f32[1,768,128]{2,1,0:T(8,128)}, f32[1,768,128]{2,1,0:T(8,128)S(1)}, u32[]{:S(2)}, u32[]{:S(2)}) collective-permute-start(f32[1,768,128]{2,1,0:T(8,128)} %get-tuple-element.30), channel_id=1, source_target_pairs={{1,0},{2,1},{3,2},{5,4},{6,5},{7,6},{9,8},{10,9},{11,10},{13,12},{... | collective-permute-start | bytes 1179656 | tf_op jit(solution)/shard_map/ppermute | solution.py:27
  151.6 1.9 %collective-permute-start.16 = (f32[1,768,128]{2,1,0:T(8,128)}, f32[1,768,128]{2,1,0:T(8,128)S(1)}, u32[]{:S(2)}, u32[]{:S(2)}) collective-permute-start(f32[1,768,128]{2,1,0:T(8,128)} %get-tuple-element.28), channel_id=1, source_target_pairs={{1,0},{2,1},{3,2},{5,4},{6,5},{7,6},{9,8},{10,9},{11,10},{13,12},{... | collective-permute-start | bytes 1179656 | tf_op jit(solution)/shard_map/ppermute | solution.py:27
  153.5 3.6 %collective-permute-start.20 = (f32[1,128,768]{2,1,0:T(8,128)}, f32[1,128,768]{2,1,0:T(8,128)S(1)}, u32[]{:S(2)}, u32[]{:S(2)}) collective-permute-start(f32[1,128,768]{2,1,0:T(8,128)} %get-tuple-element.31), channel_id=1, source_target_pairs={{4,0},{8,4},{12,8},{16,12},{20,16},{24,20},{28,24},{5,1},{9,5},{13... | collective-permute-start | bytes 1179656 | tf_op jit(solution)/shard_map/ppermute | solution.py:27
  157.1 1.9 %collective-permute-start.17 = (f32[1,128,768]{2,1,0:T(8,128)}, f32[1,128,768]{2,1,0:T(8,128)S(1)}, u32[]{:S(2)}, u32[]{:S(2)}) collective-permute-start(f32[1,128,768]{2,1,0:T(8,128)} %get-tuple-element.29), channel_id=1, source_target_pairs={{4,0},{8,4},{12,8},{16,12},{20,16},{24,20},{28,24},{5,1},{9,5},{13... | collective-permute-start | bytes 1179656 | tf_op jit(solution)/shard_map/ppermute | solution.py:27
  159.0 1.9 %collective-permute-start.21 = (f32[1,128,128]{2,1,0:T(8,128)S(1)}, f32[1,128,128]{2,1,0:T(8,128)S(1)}, u32[]{:S(2)}, u32[]{:S(2)}) collective-permute-start(f32[1,128,128]{2,1,0:T(8,128)S(1)} %slice.119), channel_id=1, source_target_pairs={{4,0},{8,4},{12,8},{16,12},{20,16},{24,20},{28,24},{5,1},{9,5},{13... | collective-permute-start | bytes 196616 | tf_op jit(solution)/shard_map/ppermute | solution.py:27
  161.0 0.6 collective-permute-done.16.refs_0_
  161.6 3.9 %collective-permute-start.18 = (f32[1,128,128]{2,1,0:T(8,128)S(1)}, f32[1,128,128]{2,1,0:T(8,128)S(1)}, u32[]{:S(2)}, u32[]{:S(2)}) collective-permute-start(f32[1,128,128]{2,1,0:T(8,128)S(1)} %slice.118), channel_id=1, source_target_pairs={{4,0},{8,4},{12,8},{16,12},{20,16},{24,20},{28,24},{5,1},{9,5},{13... | collective-permute-start | bytes 196616 | tf_op jit(solution)/shard_map/ppermute | solution.py:27
  165.5 1.2 collective-permute-done.20.refs_4_
  166.7 8.4 %collective-permute-done.17.refs_1_ = f32[1,128,768]{2,1,0:T(8,128)S(1)} collective-permute-done((f32[1,128,768]{2,1,0:T(8,128)}, f32[1,128,768]{2,1,0:T(8,128)S(1)}, u32[]{:S(2)}, u32[]{:S(2)}) %collective-permute-start.17) | collective-permute-done | bytes 393248 | tf_op jit(solution)/shard_map/ppermute | solution.py:27
  175.1 1.2 collective-permute-done.21.refs_5_
  177.5 4.9 %windows.1 = f32[4,2,256,256]{3,2,1,0:T(8,128)} custom-call(s32[4,2]{1,0:T(4,128)} %broadcast_subtract_fusion.place_ref, f32[2,768,768]{2,1,0:T(8,128)} %get-tuple-element.15.field_ref, f32[1,768,128]{2,1,0:T(8,128)} %copy-done.6, f32[1,128,768]{2,1,0:T(8,128)} %copy-done.8, f32[1,128,128]{2,1,0:T(8,128)} %copy-done.11, f32[1,768,128]{2,1,0:T(8,128)} %copy-done.5, ...), custom_call_target="tpu_custom_call" | custom-call | tf_op jit(solution)/shard_map/windows/pallas_call | solution.py:581
  182.4 1.2 broadcast_select_fusion.1
  183.7 1.3 pad_maximum_fusion
  (77 shorter events, 2.1 us)
Async XLA Ops:
  2.7 38.8 %copy-start.12 = (s32[4,2]{0,1:T(2,128)S(1)}, s32[4,2]{0,1:T(2,128)}, u32[]{:S(2)}) copy-start(s32[4,2]{0,1:T(2,128)} %param.13) | copy-start | bytes 100
  30.4 13.2 %collective-permute-start.6 = (f32[7,128,256]{2,1,0:T(8,128)}, f32[7,128,256]{2,1,0:T(8,128)S(1)}, u32[]{:S(2)}, u32[]{:S(2)}) collective-permute-start(f32[7,128,256]{2,1,0:T(8,128)} %get-tuple-element.27), channel_id=1, source_target_pairs={{0,1},{1,0},{2,3},{3,2},{4,5},{5,4},{6,7},{7,6},{8,9},{9,8},{10,11... | collective-permute-start | bytes 2752520 | tf_op jit(solution)/shard_map/ppermute | solution.py:31
  31.2 14.9 %collective-permute-start = (f32[2,1008,128]{2,1,0:T(8,128)}, f32[2,1008,128]{2,1,0:T(8,128)S(1)}, u32[]{:S(2)}, u32[]{:S(2)}) collective-permute-start(f32[2,1008,128]{2,1,0:T(8,128)} %get-tuple-element.20), channel_id=1, source_target_pairs={{0,1},{1,2},{2,3},{4,5},{5,6},{6,7},{8,9},{9,10},{10,11},{12,13},{... | collective-permute-start | bytes 3096584 | tf_op jit(solution)/shard_map/ppermute | solution.py:27
  34.2 8.0 %collective-permute-start.1 = (f32[2,112,128]{2,1,0:T(8,128)}, f32[2,112,128]{2,1,0:T(8,128)S(1)}, u32[]{:S(2)}, u32[]{:S(2)}) collective-permute-start(f32[2,112,128]{2,1,0:T(8,128)} %get-tuple-element.21), channel_id=1, source_target_pairs={{1,0},{2,1},{3,2},{5,4},{6,5},{7,6},{9,8},{10,9},{11,10},{13,12},{... | collective-permute-start | bytes 344072 | tf_op jit(solution)/shard_map/ppermute | solution.py:27
  36.1 7.5 %collective-permute-start.3 = (f32[2,24,896]{2,1,0:T(8,128)}, f32[2,24,896]{2,1,0:T(8,128)S(1)}, u32[]{:S(2)}, u32[]{:S(2)}) collective-permute-start(f32[2,24,896]{2,1,0:T(8,128)} %get-tuple-element.23), channel_id=1, source_target_pairs={{4,0},{8,4},{12,8},{16,12},{20,16},{24,20},{28,24},{5,1},{9,5},{13... | collective-permute-start | bytes 516104 | tf_op jit(solution)/shard_map/ppermute | solution.py:27
  39.1 61.5 %collective-permute-start.2 = (f32[2,152,896]{2,1,0:T(8,128)}, f32[2,152,896]{2,1,0:T(8,128)S(1)}, u32[]{:S(2)}, u32[]{:S(2)}) collective-permute-start(f32[2,152,896]{2,1,0:T(8,128)} %get-tuple-element.22), channel_id=1, source_target_pairs={{0,4},{4,8},{8,12},{12,16},{16,20},{20,24},{24,28},{1,5},{5,9},{9,... | collective-permute-start | bytes 3268616 | tf_op jit(solution)/shard_map/ppermute | solution.py:27
  42.2 56.4 %copy-start.3 = (f32[2,112,128]{2,1,0:T(8,128)}, f32[2,112,128]{2,1,0:T(8,128)S(1)}, u32[]{:S(2)}) copy-start(f32[2,112,128]{2,1,0:T(8,128)S(1)} %collective-permute-done.1.trail_ref) | copy-start | bytes 344068
  43.6 13.4 %copy-start.4 = (f32[2,24,896]{2,1,0:T(8,128)}, f32[2,24,896]{2,1,0:T(8,128)S(1)}, u32[]{:S(2)}) copy-start(f32[2,24,896]{2,1,0:T(8,128)S(1)} %collective-permute-done.3.below_ref) | copy-start | bytes 516100
  45.0 11.9 %collective-permute-start.7 = (f32[7,64,256]{2,1,0:T(8,128)S(1)}, f32[7,64,256]{2,1,0:T(8,128)S(1)}, u32[]{:S(2)}, u32[]{:S(2)}) collective-permute-start(f32[7,64,256]{2,1,0:T(8,128)S(1)} %constant_dynamic-slice_fusion.3), channel_id=1, source_target_pairs={{0,2},{1,3},{2,0},{3,1},{4,6},{5,7},{6,4},{7,5},{8,10},{9,11},{10,... | collective-permute-start | bytes 1376264 | tf_op jit(solution)/shard_map/ppermute | solution.py:31
  46.1 54.6 %copy-start = (f32[2,1008,128]{2,1,0:T(8,128)}, f32[2,1008,128]{2,1,0:T(8,128)S(1)}, u32[]{:S(2)}) copy-start(f32[2,1008,128]{2,1,0:T(8,128)S(1)} %collective-permute-done.lead_ref) | copy-start | bytes 3096580
  57.1 15.5 %collective-permute-start.8 = (f32[7,32,256]{2,1,0:T(8,128)S(1)}, f32[7,32,256]{2,1,0:T(8,128)S(1)}, u32[]{:S(2)}, u32[]{:S(2)}) collective-permute-start(f32[7,32,256]{2,1,0:T(8,128)S(1)} %constant_dynamic-slice_fusion.2), channel_id=1, source_target_pairs={{0,4},{4,0},{8,12},{12,8},{16,20},{20,16},{24,28},{28,24},{1,5},{5... | collective-permute-start | bytes 688136 | tf_op jit(solution)/shard_map/ppermute | solution.py:31
  72.7 7.6 %collective-permute-start.9 = (f32[7,16,256]{2,1,0:T(8,128)S(1)}, f32[7,16,256]{2,1,0:T(8,128)S(1)}, u32[]{:S(2)}, u32[]{:S(2)}) collective-permute-start(f32[7,16,256]{2,1,0:T(8,128)S(1)} %constant_dynamic-slice_fusion.1), channel_id=1, source_target_pairs={{0,16},{4,20},{8,24},{12,28},{16,0},{20,4},{24,8},{28,12},{1,17},{... | collective-permute-start | bytes 344072 | tf_op jit(solution)/shard_map/ppermute | solution.py:31
  75.0 25.7 %collective-permute-start.5 = (f32[2,56,128]{2,1,0:T(8,128)S(1)}, f32[2,56,128]{2,1,0:T(8,128)S(1)}, u32[]{:S(2)}, u32[]{:S(2)}) collective-permute-start(f32[2,56,128]{2,1,0:T(8,128)S(1)} %constant_dynamic-update-slice_fusion.4), channel_id=1, source_target_pairs={{4,0},{8,4},{12,8},{16,12},{20,16},{24,20},{28,24},{5,1},{9,5},{13... | collective-permute-start | bytes 172040 | tf_op jit(solution)/shard_map/ppermute | solution.py:27
  80.3 3.1 %collective-permute-start.10 = (f32[7,8,256]{2,1,0:T(8,128)S(1)}, f32[7,8,256]{2,1,0:T(8,128)S(1)}, u32[]{:S(2)}, u32[]{:S(2)}) collective-permute-start(f32[7,8,256]{2,1,0:T(8,128)S(1)} %constant_dynamic-slice_fusion), channel_id=1, source_target_pairs={{0,8},{4,12},{8,0},{12,4},{16,24},{20,28},{24,16},{28,20},{1,9},{5... | collective-permute-start | bytes 172040 | tf_op jit(solution)/shard_map/ppermute | solution.py:31
  84.2 3.0 %collective-permute-start.11 = (f32[6,8,256]{2,1,0:T(8,128)S(1)}, f32[6,8,256]{2,1,0:T(8,128)S(1)}, u32[]{:S(2)}, u32[]{:S(2)}) collective-permute-start(f32[6,8,256]{2,1,0:T(8,128)S(1)} %fusion), channel_id=1, source_target_pairs={{0,8},{4,12},{8,0},{12,4},{16,24},{20,28},{24,16},{28,20},{1,9},{5... | collective-permute-start | bytes 147464 | tf_op jit(solution)/shard_map/ppermute | solution.py:31
  87.3 5.5 %collective-permute-start.12 = (f32[6,16,256]{2,1,0:T(8,128)S(1)}, f32[6,16,256]{2,1,0:T(8,128)S(1)}, u32[]{:S(2)}, u32[]{:S(2)}) collective-permute-start(f32[6,16,256]{2,1,0:T(8,128)S(1)} %pad_maximum_fusion.4), channel_id=1, source_target_pairs={{0,16},{4,20},{8,24},{12,28},{16,0},{20,4},{24,8},{28,12},{1,17},{... | collective-permute-start | bytes 294920 | tf_op jit(solution)/shard_map/ppermute | solution.py:31
  92.8 4.6 %collective-permute-start.13 = (f32[6,32,256]{2,1,0:T(8,128)S(1)}, f32[6,32,256]{2,1,0:T(8,128)S(1)}, u32[]{:S(2)}, u32[]{:S(2)}) collective-permute-start(f32[6,32,256]{2,1,0:T(8,128)S(1)} %pad_maximum_fusion.3), channel_id=1, source_target_pairs={{0,4},{4,0},{8,12},{12,8},{16,20},{20,16},{24,28},{28,24},{1,5},{5... | collective-permute-start | bytes 589832 | tf_op jit(solution)/shard_map/ppermute | solution.py:31
  97.5 6.7 %collective-permute-start.14 = (f32[6,64,256]{2,1,0:T(8,128)S(1)}, f32[6,64,256]{2,1,0:T(8,128)S(1)}, u32[]{:S(2)}, u32[]{:S(2)}) collective-permute-start(f32[6,64,256]{2,1,0:T(8,128)S(1)} %pad_maximum_fusion.2), channel_id=1, source_target_pairs={{0,2},{1,3},{2,0},{3,1},{4,6},{5,7},{6,4},{7,5},{8,10},{9,11},{10,... | collective-permute-start | bytes 1179656 | tf_op jit(solution)/shard_map/ppermute | solution.py:31
  98.6 11.5 %collective-permute-start.4 = (f32[2,200,128]{2,1,0:T(8,128)S(1)}, f32[2,200,128]{2,1,0:T(8,128)S(1)}, u32[]{:S(2)}, u32[]{:S(2)}) collective-permute-start(f32[2,200,128]{2,1,0:T(8,128)S(1)} %constant_dynamic-update-slice_fusion), channel_id=1, source_target_pairs={{0,4},{4,8},{8,12},{12,16},{16,20},{20,24},{24,28},{1,5},{5,9},{9,... | collective-permute-start | bytes 614408 | tf_op jit(solution)/shard_map/ppermute | solution.py:27
  100.7 15.5 %copy-start.1 = (f32[2,152,896]{2,1,0:T(8,128)}, f32[2,152,896]{2,1,0:T(8,128)S(1)}, u32[]{:S(2)}) copy-start(f32[2,152,896]{2,1,0:T(8,128)S(1)} %collective-permute-done.2.above_ref) | copy-start | bytes 3268612
  100.7 15.5 %copy-start.9 = (f32[2,56,128]{2,1,0:T(8,128)}, f32[2,56,128]{2,1,0:T(8,128)S(1)}, u32[]{:S(2)}) copy-start(f32[2,56,128]{2,1,0:T(8,128)S(1)} %collective-permute-done.5.corner_below_ref) | copy-start | bytes 172036
  104.3 78.1 %collective-permute-start.15 = (f32[6,128,256]{2,1,0:T(8,128)S(1)}, f32[6,128,256]{2,1,0:T(8,128)}, u32[]{:S(2)}, u32[]{:S(2)}) collective-permute-start(f32[6,128,256]{2,1,0:T(8,128)S(1)} %pad_maximum_fusion.1), channel_id=1, source_target_pairs={{0,1},{1,0},{2,3},{3,2},{4,5},{5,4},{6,7},{7,6},{8,9},{9,8},{10,11... | collective-permute-start | bytes 2359304 | tf_op jit(solution)/shard_map/ppermute | solution.py:31
  110.1 6.1 %copy-start.2 = (f32[2,200,128]{2,1,0:T(8,128)}, f32[2,200,128]{2,1,0:T(8,128)S(1)}, u32[]{:S(2)}) copy-start(f32[2,200,128]{2,1,0:T(8,128)S(1)} %collective-permute-done.4.corner_above_ref) | copy-start | bytes 614404
  147.3 11.7 %collective-permute-start.19 = (f32[1,768,128]{2,1,0:T(8,128)}, f32[1,768,128]{2,1,0:T(8,128)S(1)}, u32[]{:S(2)}, u32[]{:S(2)}) collective-permute-start(f32[1,768,128]{2,1,0:T(8,128)} %get-tuple-element.30), channel_id=1, source_target_pairs={{1,0},{2,1},{3,2},{5,4},{6,5},{7,6},{9,8},{10,9},{11,10},{13,12},{... | collective-permute-start | bytes 1179656 | tf_op jit(solution)/shard_map/ppermute | solution.py:27
  151.6 10.0 %collective-permute-start.16 = (f32[1,768,128]{2,1,0:T(8,128)}, f32[1,768,128]{2,1,0:T(8,128)S(1)}, u32[]{:S(2)}, u32[]{:S(2)}) collective-permute-start(f32[1,768,128]{2,1,0:T(8,128)} %get-tuple-element.28), channel_id=1, source_target_pairs={{1,0},{2,1},{3,2},{5,4},{6,5},{7,6},{9,8},{10,9},{11,10},{13,12},{... | collective-permute-start | bytes 1179656 | tf_op jit(solution)/shard_map/ppermute | solution.py:27
  153.5 13.2 %collective-permute-start.20 = (f32[1,128,768]{2,1,0:T(8,128)}, f32[1,128,768]{2,1,0:T(8,128)S(1)}, u32[]{:S(2)}, u32[]{:S(2)}) collective-permute-start(f32[1,128,768]{2,1,0:T(8,128)} %get-tuple-element.31), channel_id=1, source_target_pairs={{4,0},{8,4},{12,8},{16,12},{20,16},{24,20},{28,24},{5,1},{9,5},{13... | collective-permute-start | bytes 1179656 | tf_op jit(solution)/shard_map/ppermute | solution.py:27
  157.1 18.1 %collective-permute-start.17 = (f32[1,128,768]{2,1,0:T(8,128)}, f32[1,128,768]{2,1,0:T(8,128)S(1)}, u32[]{:S(2)}, u32[]{:S(2)}) collective-permute-start(f32[1,128,768]{2,1,0:T(8,128)} %get-tuple-element.29), channel_id=1, source_target_pairs={{4,0},{8,4},{12,8},{16,12},{20,16},{24,20},{28,24},{5,1},{9,5},{13... | collective-permute-start | bytes 1179656 | tf_op jit(solution)/shard_map/ppermute | solution.py:27
  159.0 17.9 %copy-start.5 = (f32[1,768,128]{2,1,0:T(8,128)}, f32[1,768,128]{2,1,0:T(8,128)S(1)}, u32[]{:S(2)}) copy-start(f32[1,768,128]{2,1,0:T(8,128)S(1)} %collective-permute-done.19.refs_3_) | copy-start | bytes 1179652
  159.0 17.4 %collective-permute-start.21 = (f32[1,128,128]{2,1,0:T(8,128)S(1)}, f32[1,128,128]{2,1,0:T(8,128)S(1)}, u32[]{:S(2)}, u32[]{:S(2)}) collective-permute-start(f32[1,128,128]{2,1,0:T(8,128)S(1)} %slice.119), channel_id=1, source_target_pairs={{4,0},{8,4},{12,8},{16,12},{20,16},{24,20},{28,24},{5,1},{9,5},{13... | collective-permute-start | bytes 196616 | tf_op jit(solution)/shard_map/ppermute | solution.py:27
  161.6 15.3 %copy-start.6 = (f32[1,768,128]{2,1,0:T(8,128)}, f32[1,768,128]{2,1,0:T(8,128)S(1)}, u32[]{:S(2)}) copy-start(f32[1,768,128]{2,1,0:T(8,128)S(1)} %collective-permute-done.16.refs_0_) | copy-start | bytes 1179652
  161.6 15.3 %collective-permute-start.18 = (f32[1,128,128]{2,1,0:T(8,128)S(1)}, f32[1,128,128]{2,1,0:T(8,128)S(1)}, u32[]{:S(2)}, u32[]{:S(2)}) collective-permute-start(f32[1,128,128]{2,1,0:T(8,128)S(1)} %slice.118), channel_id=1, source_target_pairs={{4,0},{8,4},{12,8},{16,12},{20,16},{24,20},{28,24},{5,1},{9,5},{13... | collective-permute-start | bytes 196616 | tf_op jit(solution)/shard_map/ppermute | solution.py:27
  166.7 10.2 %copy-start.7 = (f32[1,128,768]{2,1,0:T(8,128)}, f32[1,128,768]{2,1,0:T(8,128)S(1)}, u32[]{:S(2)}) copy-start(f32[1,128,768]{2,1,0:T(8,128)S(1)} %collective-permute-done.20.refs_4_) | copy-start | bytes 1179652
  175.1 1.8 copy-start.8
  176.4 0.6 copy-start.10
  176.9 0.6 copy-start.11

commit v2 on v1

--- a/solution.py
+++ b/solution.py
@@ -1,3 +1,4 @@
+import functools
 import math
 
 import jax
@@ -27,8 +28,12 @@
     return lax.ppermute(block, axis, route)
 
 
-def swap(block, axis, mask):
-    return lax.ppermute(block, axis, [(i, i ^ mask) for i in range(lax.axis_size(axis))])
+def swap(block, row_mask, col_mask):
+    rows, cols = lax.axis_size("row"), lax.axis_size("col")
+    route = [
+        (r * cols + c, (r ^ row_mask) * cols + (c ^ col_mask)) for r in range(rows) for c in range(cols)
+    ]
+    return lax.ppermute(block, ("row", "col"), route)
 
 
 def split_two(value):
@@ -58,15 +63,6 @@
     return np.stack(pairs), perm.astype(jnp.bfloat16)
 
 
-def mark_block(place_ref, origin, part, shape):
-    lane = lane_of(shape)
-    row = lax.broadcasted_iota(jnp.int32, shape, 0)
-    block = jnp.zeros(shape, jnp.int32)
-    for frame in range(place_ref.shape[0]):
-        block = jnp.where((lane == frame) & (row == 0), place_ref[frame, part] + origin + 1, block)
-    return block.astype(jnp.float32)
-
-
 def lane_of(shape):
     return lax.broadcasted_iota(jnp.int32, shape, len(shape) - 1)
 
@@ -80,7 +76,7 @@
 def frames_kernel(
     place_ref, self_ref, amp_low_ref, amp_high_ref, patch_ref, dual_ref, probe_ref, pair_ref, perm_ref,
     obj_low_ref, obj_high_ref, obj_first_ref, obj_last_ref,
-    new_ref, keep_ref, give_ref, canvas_ref, lead_ref, trail_ref, down_ref, up_ref,
+    new_ref, keep_ref, give_ref, canvas_ref, lead_ref, link_ref, trail_ref, down0_ref, down1_ref, up_ref,
     even_ref, odd_ref, num_ref, right_ref, left_ref,
 ):
     frame = pl.program_id(0)
@@ -163,8 +159,9 @@
         ratio = amps[parity] / jnp.sqrt(power[parity] + amp_floor)
         ratios.append(jnp.concatenate([ratio, ratio], axis=0))
 
-    start_row = pl.multiple_of(place_ref[frame, 0], half)
-    start_col = pl.multiple_of(place_ref[frame, 1], half)
+    tile = canvas_ref.shape[1] - half
+    start_row = pl.multiple_of(place_ref[frame, 0] - self_ref[0] * tile, half)
+    start_col = pl.multiple_of(place_ref[frame, 1] - self_ref[1] * tile, half)
     obj_re = jnp.zeros((width, width), jnp.float32)
     obj_im = jnp.zeros((width, width), jnp.float32)
     for m in range(modes):
@@ -208,38 +205,42 @@
     @pl.when(frame == pl.num_programs(0) - 1)
     def _():
         grow = canvas_ref.shape[1]
-        tile = grow - half
         blocks = grow // half
-        kept = pl.multiple_of(self_ref[2] * half, half)
-        given = pl.multiple_of((1 - self_ref[2]) * half, half)
+        kept = pl.multiple_of((self_ref[1] & 1) * half, half)
+        given = pl.multiple_of((1 - (self_ref[1] & 1)) * half, half)
         keep_ref[...] = num_ref[:, pl.ds(kept, half), :]
         give_ref[...] = num_ref[:, pl.ds(given, half), :]
-        for part in range(2):
-            origin = self_ref[part] * tile
-            lead_ref[part, :grow, :] = canvas_ref[part, :, tile:]
-            down_ref[part, : half + HALO, :] = canvas_ref[part, tile - HALO :, :]
+        shape = (HALO, half)
+        lane = lane_of(shape)
+        row = lax.broadcasted_iota(jnp.int32, shape, 0)
+        marks = jnp.zeros(shape, jnp.int32)
+        for n in range(place_ref.shape[0]):
+            for part in range(2):
+                marks = jnp.where((lane == n) & (row == part), place_ref[n, part] + 1, marks)
+        marks = marks.astype(jnp.float32)
+        for part, down_ref in enumerate((down0_ref, down1_ref)):
+            down_ref[: half + HALO, :] = canvas_ref[part, tile - HALO :, :]
+            down_ref[half + HALO : half + 2 * HALO, :tile] = obj_last_ref[part]
+            down_ref[half + HALO : half + 2 * HALO, tile:] = jnp.zeros(shape, jnp.float32)
+            lead_ref[part] = canvas_ref[part, :, tile:]
+            link_ref[part, : half + HALO, :] = canvas_ref[part, tile - HALO :, tile:]
+            link_ref[part, half + HALO : half + 2 * HALO, :] = canvas_ref[part, :HALO, tile:]
+            past = half + 2 * HALO
             up_ref[part, :HALO, :] = canvas_ref[part, :HALO, :]
-            ends = edge_block(canvas_ref[part, :, :half], canvas_ref[part, :, tile - half : tile]).T
-            for n in range(blocks):
-                at = slice(n * half, (n + 1) * half)
-                trail_ref[part, n * HALO : (n + 1) * HALO, :] = ends[:HALO, at]
-                lead_ref[part, grow + n * HALO : grow + (n + 1) * HALO, :] = ends[half - HALO :, at]
-            ends = edge_block(obj_low_ref[part], obj_high_ref[part]).T
-            for n in range(blocks - 1):
-                at = slice(n * half, (n + 1) * half)
-                to = (blocks + n) * HALO
-                trail_ref[part, to : to + HALO, :] = ends[:HALO, at]
-                lead_ref[part, grow + to : grow + to + HALO, :] = ends[half - HALO :, at]
-            note = mark_block(place_ref, origin, part, (HALO, half))
+            up_ref[part, HALO:, :tile] = obj_first_ref[part]
+            up_ref[part, HALO:, tile:] = marks
+            sums = edge_block(canvas_ref[part, :, :half], canvas_ref[part, :, tile - half : tile]).T
+            objs = edge_block(obj_low_ref[part], obj_high_ref[part]).T
+            for ends, count, base in ((sums, blocks, 0), (objs, blocks - 1, blocks)):
+                for n in range(count):
+                    at = slice(n * half, (n + 1) * half)
+                    to = (base + n) * HALO
+                    trail_ref[part, to : to + HALO, :] = ends[:HALO, at]
+                    link_ref[part, past + to : past + to + HALO, :] = ends[half - HALO :, at]
             to = (2 * blocks - 1) * HALO
-            trail_ref[part, to:, :] = note
-            lead_ref[part, grow + to :, :] = note
-            down_ref[part, half + HALO : half + 2 * HALO, :tile] = obj_last_ref[part]
-            up_ref[part, HALO : 2 * HALO, :tile] = obj_first_ref[part]
-            for ref, at in ((down_ref, half + 2 * HALO), (up_ref, 2 * HALO)):
-                ref[part, at - HALO : at, tile:] = jnp.zeros((HALO, half), jnp.float32)
-                ref[part, at:, :half] = note
-                ref[part, at:, half:] = jnp.zeros((HALO, tile), jnp.float32)
+            trail_ref[part, to:, :] = marks
+            link_ref[part, past + to :, :] = marks
+        down0_ref[half + HALO : half + 2 * HALO, tile:] = marks
 
 
 def frames_update(amplitude, patches, dual, probe, obj, places, self_index):
@@ -249,16 +250,18 @@
     half = width // 2
     tile = obj.shape[1]
     grow = tile + half
-    notes = 2 * grow // half * HALO
+    thin = 2 * grow // half * HALO
     last = tile // half - 1
     messages = (
         (2 * modes + 1, half, width),
         (2 * modes + 1, half, width),
         (2, grow, grow),
-        (2, grow + notes, half),
-        (2, notes, half),
-        (2, half + 3 * HALO, grow),
-        (2, 3 * HALO, grow),
+        (2, grow, half),
+        (2, half + 2 * HALO + thin, half),
+        (2, thin, half),
+        (half + 2 * HALO, grow),
+        (half + 2 * HALO, grow),
+        (2, 2 * HALO, grow),
     )
 
     def whole(shape):
@@ -307,31 +310,64 @@
     )
 
 
-def weights_kernel(place_ref, bound_ref, probe_ref, out_ref, sums_ref):
+def weights_kernel(
+    self_ref, own_ref, lead_ref, trail_ref, above_ref, below_ref, corner_ref, probe_ref, out_ref,
+    sums_ref, marks_ref, sem, *, size, count,
+):
     modes = probe_ref.shape[0]
     width = probe_ref.shape[-1]
     half = width // 2
     rows = out_ref.shape[1]
     tile = rows - 2 * HALO
+    last = pl.ds(above_ref.shape[0] - HALO, HALO)
+    final = pl.ds(tile, half)
+    spots = (
+        lead_ref.at[0, pl.ds(lead_ref.shape[1] - HALO, HALO), :],
+        trail_ref.at[0, pl.ds(trail_ref.shape[1] - HALO, HALO), :],
+        above_ref.at[last, final],
+        below_ref.at[0, pl.ds(HALO, HALO), final],
+        corner_ref.at[0, pl.ds(corner_ref.shape[1] - 2 * HALO, HALO), :],
+        corner_ref.at[0, pl.ds(corner_ref.shape[1] - HALO, HALO), :],
+        below_ref.at[0, pl.ds(2 * HALO, HALO), pl.ds(tile - half, half)],
+        below_ref.at[0, pl.ds(2 * HALO, HALO), final],
+    )
+    copies = [pltpu.make_async_copy(spot, marks_ref.at[n], sem.at[n]) for n, spot in enumerate(spots)]
+    for copy in copies:
+        copy.start()
     power = jnp.zeros((width, width), jnp.float32)
     for m in range(modes):
         power += probe_ref[m, 0] * probe_ref[m, 0] + probe_ref[m, 1] * probe_ref[m, 1]
     sums_ref[...] = jnp.zeros_like(sums_ref)
 
-    def place(frame, carry):
-        row = place_ref[frame, 0]
-        col = place_ref[frame, 1]
-
-        @pl.when((row >= -width) & (row <= tile) & (col >= -width) & (col <= tile))
+    def place(row, col, present):
+        row = row - self_ref[0] * tile
+        col = col - self_ref[1] * tile
+        reached = (row >= -width) & (row <= tile) & (col >= -width) & (col <= tile)
+
+        @pl.when(present & reached)
         def _():
             at_row = pl.ds(pl.multiple_of(row + width, half), width)
             at_col = pl.ds(pl.multiple_of(col + width, half), width)
             sums_ref[at_row, at_col] += power
 
+    def place_own(frame, carry):
+        place(own_ref[frame, 0], own_ref[frame, 1], True)
         return carry
 
-    lax.fori_loop(0, place_ref.shape[0], place, 0)
-    low_row, high_row, low_col, high_col = (bound_ref[n] for n in range(4))
+    lax.fori_loop(0, count, place_own, 0)
+    for copy in copies:
+        copy.wait()
+
+    def place_marked(n, carry):
+        source, frame = n // count, n % count
+        row = marks_ref[source, 0, frame].astype(jnp.int32)
+        col = marks_ref[source, 1, frame].astype(jnp.int32)
+        place(row - 1, col - 1, row > 0)
+        return carry
+
+    lax.fori_loop(0, len(spots) * count, place_marked, 0)
+    low_row, high_row = -self_ref[0] * tile, (size[0] - self_ref[0]) * tile
+    low_col, high_col = -self_ref[1] * tile, (size[1] - self_ref[1]) * tile
 
     chunk = 56
 
@@ -357,30 +393,37 @@
     lax.fori_loop(0, rows // chunk, finish, 0)
 
 
-def object_weights(places, bounds, probe, tile):
+def object_weights(self_index, positions, messages, probe, tile):
     width = probe.shape[-1]
+    half = width // 2
     smem = pl.BlockSpec(memory_space=pltpu.SMEM)
+    size = (lax.axis_size("row"), lax.axis_size("col"))
     return pl.pallas_call(
-        weights_kernel,
-        out_shape=jax.ShapeDtypeStruct(
-            (2 * tile // width + 1, tile + 2 * HALO, width // 2), jnp.float32
-        ),
-        in_specs=[smem, smem, VMEM_SPEC],
+        functools.partial(weights_kernel, size=size, count=positions.shape[0]),
+        out_shape=jax.ShapeDtypeStruct((tile // half + 1, tile + 2 * HALO, half), jnp.float32),
+        in_specs=[smem] * 2 + [pl.BlockSpec(memory_space=pl.ANY)] * len(messages) + [VMEM_SPEC],
         out_specs=VMEM_SPEC,
-        scratch_shapes=[pltpu.VMEM((tile + 2 * width, tile + 2 * width), jnp.float32)],
-        compiler_params=pltpu.CompilerParams(vmem_limit_bytes=VMEM_LIMIT),
+        scratch_shapes=[
+            pltpu.VMEM((tile + 2 * width, tile + 2 * width), jnp.float32),
+            pltpu.SMEM((8, HALO, half), jnp.float32),
+            pltpu.SemaphoreType.DMA((8,)),
+        ],
+        compiler_params=pltpu.CompilerParams(vmem_limit_bytes=20 << 20),
         name="weights",
-    )(places, bounds, probe)
+    )(self_index, positions, *messages, probe)
 
 
 PAD = 8
 
 
 def sweeps_kernel(
-    canvas_ref, lead_ref, trail_ref, above_ref, below_ref, corner_above_ref, corner_below_ref,
-    obj_ref, weight_ref, *refs,
+    canvas_ref, trail_block, obj_ref, lead_block, link_block, below_block, corner_block, above_ref,
+    weight_ref, *refs,
 ):
     field_ref, edge_ref, head_ref, rhs_ref, first_ref, second_ref = refs[-6:]
+    trail, lead_ref, link, below_ref, corner_ref = (
+        ref.at[0] for ref in (trail_block, lead_block, link_block, below_block, corner_block)
+    )
     tile = obj_ref.shape[1]
     half = lead_ref.shape[-1]
     rows = tile + 2 * HALO
@@ -394,10 +437,11 @@
     lower = slice(PAD + HALO + tile, PAD + 2 * HALO + tile)
     near_top = slice(PAD + HALO, PAD + HALO + half)
     lane = lane_of((rows, half))
-
-    def thin(ref, start, count):
+    corner_below = [below_ref[2 * HALO : 3 * HALO, n * half : (n + 1) * half] for n in range(5)]
+
+    def thin(values, start, count):
         return jnp.concatenate(
-            [ref[0, start + n * HALO : start + (n + 1) * HALO, :] for n in range(count)], axis=1
+            [values[start + n * HALO : start + (n + 1) * HALO, :] for n in range(count)], axis=1
         )
 
     def halo(middle, above, below):
@@ -412,45 +456,37 @@
 
     nothing = jnp.zeros((HALO, half), jnp.float32)
     sides = columns(
+        halo(thin(trail, 0, blocks), thin(corner_ref, tall + 3 * HALO, 2), corner_below[3]),
+        halo(thin(link, tall + HALO, blocks), thin(corner_ref, tall, 2), corner_below[1]),
+    )
+    first_ref[wide, PAD : PAD + rows, :] = columns(
         halo(
-            thin(trail_ref, 0, blocks),
-            thin(corner_above_ref, tall + 4 * HALO, 2),
-            corner_below_ref[0, 4 * HALO : 5 * HALO, :],
+            jnp.concatenate([thin(trail, blocks * HALO, blocks - 1), nothing], axis=1),
+            jnp.concatenate([thin(corner_ref, tall + 5 * HALO, 1), nothing], axis=1),
+            corner_below[4],
         ),
         halo(
-            thin(lead_ref, grow, blocks),
-            thin(corner_above_ref, tall, 2),
-            corner_below_ref[0, HALO : 2 * HALO, :],
-        ),
-    )
-    first_ref[wide, PAD : PAD + rows, :] = columns(
-        halo(
-            jnp.concatenate([thin(trail_ref, blocks * HALO, blocks - 1), nothing], axis=1),
-            jnp.concatenate([corner_above_ref[0, tall + 6 * HALO : tall + 7 * HALO, :], nothing], axis=1),
-            corner_below_ref[0, 5 * HALO : 6 * HALO, :],
-        ),
-        halo(
-            jnp.concatenate([thin(lead_ref, grow + blocks * HALO, blocks - 1), nothing], axis=1),
-            jnp.concatenate([corner_above_ref[0, tall + 2 * HALO : tall + 3 * HALO, :], nothing], axis=1),
-            corner_below_ref[0, 2 * HALO : 3 * HALO, :],
+            jnp.concatenate([thin(link, tall + HALO + blocks * HALO, blocks - 1), nothing], axis=1),
+            jnp.concatenate([thin(corner_ref, tall + 2 * HALO, 1), nothing], axis=1),
+            corner_below[2],
         ),
     )
     for n in range(blocks):
         at = slice(n * half, (n + 1) * half)
         if n < wide:
-            first_ref[n, upper, :] = above_ref[0, tall : tall + HALO, at]
+            first_ref[n, upper, :] = above_ref[tall : tall + HALO, at]
             first_ref[n, own, :] = obj_ref[0, :, at]
-            first_ref[n, lower, :] = below_ref[0, HALO : 2 * HALO, at]
-        rhs_ref[n, upper, :] = above_ref[0, :HALO, at]
+            first_ref[n, lower, :] = below_ref[HALO : 2 * HALO, at]
+        rhs_ref[n, upper, :] = above_ref[:HALO, at]
         rhs_ref[n, own, :] = canvas_ref[0, :tile, at]
-        rhs_ref[n, lower, :] = canvas_ref[0, tile : tile + HALO, at] + below_ref[0, :HALO, at]
-        rhs_ref[n, near_top, :] += above_ref[0, HALO:tall, at]
+        rhs_ref[n, lower, :] = canvas_ref[0, tile : tile + HALO, at] + below_ref[:HALO, at]
+        rhs_ref[n, near_top, :] += above_ref[HALO:tall, at]
         for ref in (first_ref, second_ref):
             ref[n, :PAD, :] = jnp.zeros((PAD, half), jnp.float32)
             ref[n, PAD + rows :, :] = jnp.zeros((PAD, half), jnp.float32)
-    rhs_ref[0, PAD + HALO : PAD + 2 * HALO + tile, :] += lead_ref[0, : tile + HALO, :]
-    rhs_ref[0, PAD : PAD + tall, :] += corner_above_ref[0, :tall, :]
-    rhs_ref[0, lower, :] += corner_below_ref[0, :HALO, :]
+    rhs_ref[0, PAD + HALO : PAD + 2 * HALO + tile, :] += lead_ref[: tile + HALO, :]
+    rhs_ref[0, PAD : PAD + tall, :] += corner_ref[:tall, :]
+    rhs_ref[0, lower, :] += corner_below[0]
     rhs_ref[wide, PAD : PAD + rows, :] = sides + jnp.where(
         lane < HALO, rhs_ref[wide, PAD : PAD + rows, :], 0.0
     )
@@ -502,67 +538,106 @@
     for n in range(wide):
         at = slice(n * half, (n + 1) * half)
         field_ref[0, :, at] = source[n, own, :]
-        head_ref[0, :, at] = source[n, near_top, :]
-    edge_ref[0] = source[0, own, :]
-
-
-def object_sweeps(part, canvas, lead, trail, above, below, corner_above, corner_below, obj, weight, field):
+        head_ref[:, at] = source[n, near_top, :]
+    edge_ref[...] = source[0, own, :]
+
+
+def object_sweeps(part, canvas, trail, obj, lead, link, below, corner, above, weight, field):
     tile = obj.shape[1]
     half = lead.shape[-1]
     work = pltpu.VMEM((tile // half + 1, tile + 2 * HALO + 2 * PAD, half), jnp.float32)
-    sources = [canvas, lead, trail, above, below, corner_above, corner_below, obj]
 
     def one(shape):
         return pl.BlockSpec((1,) + tuple(shape[1:]), lambda g: (part, 0, 0))
 
+    def whole(shape):
+        return pl.BlockSpec(shape, lambda g: (0,) * len(shape))
+
+    blocked = [canvas, trail, obj, lead, link, below, corner]
     extra = [] if field is None else [field]
     return pl.pallas_call(
         sweeps_kernel,
         out_shape=(
             jax.ShapeDtypeStruct(obj.shape, jnp.float32),
-            jax.ShapeDtypeStruct((1, tile, half), jnp.float32),
-            jax.ShapeDtypeStruct((1, half, tile), jnp.float32),
+            jax.ShapeDtypeStruct((tile, half), jnp.float32),
+            jax.ShapeDtypeStruct((half, tile), jnp.float32),
         ),
         grid=(1,),
-        in_specs=[one(x.shape) for x in sources]
-        + [pl.BlockSpec(weight.shape, lambda g: (0, 0, 0))]
+        in_specs=[one(x.shape) for x in blocked]
+        + [whole(above.shape), whole(weight.shape)]
         + [pl.BlockSpec(memory_space=pl.ANY)] * len(extra),
-        out_specs=[
-            one(obj.shape),
-            pl.BlockSpec((1, tile, half), lambda g: (0, 0, 0)),
-            pl.BlockSpec((1, half, tile), lambda g: (0, 0, 0)),
-        ],
+        out_specs=[one(obj.shape), whole((tile, half)), whole((half, tile))],
         scratch_shapes=[work, work, work],
         input_output_aliases={9: 0} if extra else {},
-        compiler_params=pltpu.CompilerParams(vmem_limit_bytes=VMEM_LIMIT),
-    )(*sources, weight, *extra)
-
-
-def windows_kernel(place_ref, field_ref, *refs):
-    strips = refs[:6]
-    out_ref, whole_ref, load_sem, store_sem = refs[6:]
+        compiler_params=pltpu.CompilerParams(vmem_limit_bytes=56 << 20),
+    )(*blocked, above, weight, *extra)
+
+
+def corners_kernel(link_block, trail_block, up_ref, corner_ref, below_ref):
+    half = link_block.shape[-1]
+    grow = up_ref.shape[-1]
+    blocks = grow // half
+    tall = half + HALO
+    first, last = blocks * HALO, (2 * blocks - 2) * HALO
+    marks = last + HALO
+    past = tall + HALO
+    for part in range(2):
+        link_ref, trail_ref = link_block.at[part], trail_block.at[part]
+        corner_ref[part, :tall, :] = link_ref[:tall, :]
+        at = tall
+        for ref, base in ((link_ref, past), (trail_ref, 0)):
+            corner_ref[part, at : at + 2 * HALO, :] = ref[base + first - 2 * HALO : base + first, :]
+            corner_ref[part, at + 2 * HALO : at + 3 * HALO, :] = ref[base + last : base + last + HALO, :]
+            at += 3 * HALO
+        corner_ref[part, at : at + HALO, :] = link_ref[past + marks : past + marks + HALO, :]
+        corner_ref[part, at + HALO : at + 2 * HALO, :] = trail_ref[marks : marks + HALO, :]
+        below_ref[part, : 2 * HALO, :] = up_ref[part]
+        spots = (
+            (link_ref, tall), (link_ref, past), (link_ref, past + first), (trail_ref, 0), (trail_ref, first),
+            (link_ref, past + marks), (trail_ref, marks),
+        )
+        places = [*range(5), blocks - 2, blocks - 1]
+        for n, (ref, start) in zip(places, spots):
+            below_ref[part, 2 * HALO :, n * half : (n + 1) * half] = ref[start : start + HALO, :]
+
+
+def corners(link, trail, up):
+    grow = up.shape[-1]
+    half = link.shape[-1]
+    shapes = ((2, half + 9 * HALO, half), (2, 3 * HALO, grow))
+    return pl.pallas_call(
+        corners_kernel,
+        out_shape=tuple(jax.ShapeDtypeStruct(x, jnp.float32) for x in shapes),
+        grid=(1,),
+        in_specs=[pl.BlockSpec(x.shape, lambda g: (0, 0, 0)) for x in (link, trail, up)],
+        out_specs=[pl.BlockSpec(x, lambda g: (0, 0, 0)) for x in shapes],
+        compiler_params=pltpu.CompilerParams(vmem_limit_bytes=12 << 20),
+        name="corners",
+    )(link, trail, up)
+
+
+def windows_kernel(place_ref, self_ref, field_ref, *refs):
+    strips = refs[:-4]
+    out_ref, whole_ref, load_sem, store_sem = refs[-4:]
     tile = field_ref.shape[1]
     width = out_ref.shape[-1]
     half = width // 2
-    loads = [pltpu.make_async_copy(field_ref, whole_ref.at[:, :tile, :tile], load_sem.at[0])]
+    moves = [(field_ref, whole_ref.at[:, :tile, :tile])]
     for part in range(2):
-        spots = (
-            whole_ref.at[part, :tile, tile:],
-            whole_ref.at[part, tile:, :tile],
-            whole_ref.at[part, tile:, tile:],
-        )
-        for n, spot in enumerate(spots):
-            loads.append(
-                pltpu.make_async_copy(strips[3 * part + n].at[0], spot, load_sem.at[1 + 3 * part + n])
-            )
+        moves.append((strips[3 * part], whole_ref.at[part, :tile, tile:]))
+        moves.append((strips[3 * part + 1], whole_ref.at[part, tile:, tile:]))
+        moves.append((strips[3 * part + 2], whole_ref.at[part, tile:, :tile]))
+    loads = [
+        pltpu.make_async_copy(source, target, load_sem.at[n]) for n, (source, target) in enumerate(moves)
+    ]
     for copy in loads:
         copy.start()
     for copy in loads:
         copy.wait()
     stores = []
     for frame in range(out_ref.shape[0]):
-        row = pl.multiple_of(place_ref[frame, 0], half)
-        col = pl.multiple_of(place_ref[frame, 1], half)
+        row = pl.multiple_of(place_ref[frame, 0] - self_ref[0] * tile, half)
+        col = pl.multiple_of(place_ref[frame, 1] - self_ref[1] * tile, half)
         stores.append(
             pltpu.make_async_copy(
                 whole_ref.at[:, pl.ds(row, width), pl.ds(col, width)], out_ref.at[frame], store_sem.at[frame]
@@ -574,150 +649,117 @@
         copy.wait()
 
 
-def windows(places, field, strips, width):
+def windows(places, self_index, field, strips, width):
     count = places.shape[0]
     grow = field.shape[1] + width // 2
     anywhere = pl.BlockSpec(memory_space=pl.ANY)
     return pl.pallas_call(
         windows_kernel,
         out_shape=jax.ShapeDtypeStruct((count, 2, width, width), jnp.float32),
-        in_specs=[pl.BlockSpec(memory_space=pltpu.SMEM)] + [anywhere] * 7,
+        in_specs=[pl.BlockSpec(memory_space=pltpu.SMEM)] * 2 + [anywhere] * 7,
         out_specs=anywhere,
         scratch_shapes=[
             pltpu.VMEM((2, grow, grow), jnp.float32),
             pltpu.SemaphoreType.DMA((7,)),
             pltpu.SemaphoreType.DMA((count,)),
         ],
-        compiler_params=pltpu.CompilerParams(vmem_limit_bytes=VMEM_LIMIT),
+        compiler_params=pltpu.CompilerParams(vmem_limit_bytes=56 << 20),
         name="windows",
-    )(places, field, *strips)
-
-
-def halve(data, axis, mask):
-    rows = data.shape[1] // 2
-    upper = (lax.axis_index(axis) & mask) != 0
-    keep = jnp.where(upper, rows, 0)
-    give = jnp.where(upper, 0, rows)
-    got = swap(lax.dynamic_slice_in_dim(data, give, rows, axis=1), axis, mask)
-    return lax.dynamic_slice_in_dim(data, keep, rows, axis=1) + got
-
-
-def double(data, axis, mask):
-    upper = (lax.axis_index(axis) & mask) != 0
-    got = swap(data, axis, mask)
-    return jnp.concatenate([jnp.where(upper, got, data), jnp.where(upper, data, got)], axis=1)
-
-
-def probe_steps():
-    cols, rows = lax.axis_size("col"), lax.axis_size("row")
-    steps = [("col", 1 << n) for n in range(cols.bit_length() - 1)]
-    return steps + [("row", 1 << n) for n in (0, *reversed(range(1, rows.bit_length() - 1)))]
+    )(places, self_index, field, *strips)
+
+
+def join_kernel(spot_ref, *refs):
+    out_ref = refs[-1]
+    rows = refs[0].shape[1]
+    for n, ref in enumerate(refs[:-1]):
+        at = pl.multiple_of(spot_ref[n] * rows, 8)
+        out_ref[:, pl.ds(at, rows), :] = ref[...]
+
+
+def join(spots, pieces):
+    shape = pieces[0].shape
+    return pl.pallas_call(
+        join_kernel,
+        out_shape=jax.ShapeDtypeStruct((shape[0], len(pieces) * shape[1], shape[2]), jnp.float32),
+        in_specs=[pl.BlockSpec(memory_space=pltpu.SMEM)] + [VMEM_SPEC] * len(pieces),
+        out_specs=VMEM_SPEC,
+        compiler_params=pltpu.CompilerParams(vmem_limit_bytes=16 << 20),
+        name="join",
+    )(spots, *pieces)
 
 
 def update_probe(keep, give, probe):
     parts = keep.shape[0] - 1
     width = probe.shape[-1]
-    flat = probe.reshape(parts, width, width)
-    steps = probe_steps()
-    piece = keep + swap(give, *steps[0])
-    offset = jnp.zeros((), jnp.int32)
-    span = width
-    for n, (axis, mask) in enumerate(steps):
-        if n > 0:
-            piece = halve(piece, axis, mask)
-        span = span // 2
-        offset = offset + jnp.where((lax.axis_index(axis) & mask) != 0, span, 0)
-    mine = lax.dynamic_slice_in_dim(flat, offset, span, axis=1)
-    fresh = (piece[:parts] + probe_weight * mine) / (piece[parts:] + probe_weight)
-    for n, (axis, mask) in reversed(list(enumerate(steps))):
-        fresh = double(fresh, axis, mask)
-    return fresh.reshape(probe.shape)
+    rows, cols = lax.axis_size("row"), lax.axis_size("col")
+    row_index, col_index = lax.axis_index("row"), lax.axis_index("col")
+    core = col_index & 1
+    piece = keep + swap(give, 0, 1)
+    span = piece.shape[1] // 4
+    quarter = (col_index & 2) + (row_index & 1)
+    masks = ((0, 2), (1, 0), (1, 2))
+
+    def cut(n):
+        return lax.dynamic_slice_in_dim(piece, (quarter ^ n) * span, span, axis=1)
+
+    total = cut(0)
+    for row_mask, col_mask in masks:
+        n = row_mask + col_mask
+        total = total + swap(cut(n), row_mask, col_mask)
+    doublings = [(1 << n, 0) for n in range(1, rows.bit_length() - 1)]
+    doublings += [(0, 1 << n) for n in range(2, cols.bit_length() - 1)]
+    for n, (row_mask, col_mask) in enumerate(doublings):
+        total = total + swap(total, row_mask, col_mask)
+    offset = core * (width // 2) + quarter * span
+    mine = lax.dynamic_slice_in_dim(probe.reshape(parts, width, width), offset, span, axis=1)
+    fresh = (total[:parts] + probe_weight * mine) / (total[parts:] + probe_weight)
+    pieces = [fresh] + [swap(fresh, r, c) for r, c in masks]
+    spots = jnp.stack([quarter] + [quarter ^ (r + c) for r, c in masks]).astype(jnp.int32)
+    half = join(spots, pieces)
+    other = swap(half, 0, 1)
+    return join(jnp.stack([core, 1 - core]).astype(jnp.int32), [half, other]).reshape(probe.shape)
 
 
 def per_device(amplitude, patches, dual, probe, obj, positions):
     width = amplitude.shape[-1]
     half = width // 2
     tile = obj.shape[1]
-    count = positions.shape[0]
-    row_index = lax.axis_index("row")
-    col_index = lax.axis_index("col")
-    origin = jnp.stack([row_index * tile, col_index * tile]).astype(jnp.int32)
-    places = positions - origin
-    self_index = jnp.stack([row_index, col_index, col_index & 1]).astype(jnp.int32)
-
-    dual_new, keep, give, canvas, lead, trail, down, up = frames_update(
-        amplitude, patches, dual, probe, obj, places, self_index
-    )
+    self_index = jnp.stack([lax.axis_index("row"), lax.axis_index("col")]).astype(jnp.int32)
+
+    dual_new, keep, give, canvas, lead, link, trail, down0, down1, up = frames_update(
+        amplitude, patches, dual, probe, obj, positions, self_index
+    )
+    link = shift(link, "col", 1)
     lead = shift(lead, "col", 1)
     trail = shift(trail, "col", -1)
-    above = shift(down, "row", 1)
-    below = shift(up, "row", -1)
-    grow = tile + half
-    blocks = grow // half
-    notes = (2 * blocks - 1) * HALO
-    corner_down = jnp.concatenate(
-        [
-            lead[:, tile - HALO : grow],
-            lead[:, grow + (blocks - 2) * HALO : grow + blocks * HALO],
-            lead[:, grow + notes - HALO :],
-            trail[:, (blocks - 2) * HALO : blocks * HALO],
-            trail[:, notes - HALO :],
-        ],
-        axis=1,
-    )
-    corner_up = jnp.concatenate(
-        [
-            lead[:, :HALO],
-            lead[:, grow : grow + HALO],
-            lead[:, grow + blocks * HALO : grow + (blocks + 1) * HALO],
-            lead[:, grow + notes :],
-            trail[:, :HALO],
-            trail[:, blocks * HALO : (blocks + 1) * HALO],
-            trail[:, notes:],
-        ],
-        axis=1,
-    )
-    corner_above = shift(corner_down, "row", 1)
-    corner_below = shift(corner_up, "row", -1)
-    tall = half + HALO
-    own_marks = (positions + 1).astype(jnp.float32).T
-    marks = jnp.concatenate(
-        [
-            own_marks,
-            lead[:, grow + notes, :count],
-            trail[:, notes, :count],
-            above[:, tall + HALO, :count],
-            below[:, 2 * HALO, :count],
-            corner_above[:, tall + 3 * HALO, :count],
-            corner_above[:, tall + 7 * HALO, :count],
-            corner_below[:, 3 * HALO, :count],
-            corner_below[:, 6 * HALO, :count],
-        ],
-        axis=1,
-    )
-    marks = marks.T.astype(jnp.int32)
-    around = jnp.where(marks > 0, marks - 1 - origin, -tile * 4)
-    bounds = jnp.stack(
-        [
-            -row_index * tile,
-            (lax.axis_size("row") - row_index) * tile,
-            -col_index * tile,
-            (lax.axis_size("col") - col_index) * tile,
-        ]
-    ).astype(jnp.int32)
-    weight = object_weights(around, bounds, probe, tile)
-    field = None
-    strips = []
-    for part in range(2):
-        field, edge, head = object_sweeps(
-            part, canvas, lead, trail, above, below, corner_above, corner_below, obj, weight, field
-        )
-        far_below = shift(head, "row", -1)
-        far_right = shift(edge, "col", -1)
-        far_corner = shift(far_right[:, :half, :], "row", -1)
-        strips += [far_right, far_below, far_corner]
+    above0 = shift(down0, "row", 1)
+    above1 = shift(down1, "row", 1)
+    corner, below = corners(link, trail, up)
+    corner = shift(corner, "row", 1)
+    below = shift(below, "row", -1)
+    weight = object_weights(
+        self_index, positions, (link, trail, above0, below, corner), probe, tile
+    )
+    field, edge0, head0 = object_sweeps(
+        0, canvas, trail, obj, lead, link, below, corner, above0, weight, None
+    )
+    far_below0 = shift(head0, "row", -1)
+    field, edge1, head1 = object_sweeps(
+        1, canvas, trail, obj, lead, link, below, corner, above1, weight, field
+    )
+    far_below1 = shift(head1, "row", -1)
+    far_right0 = shift(edge0, "col", -1)
+    far_right1 = shift(edge1, "col", -1)
+    far_corner0 = shift(far_right0[:half, :], "row", -1)
+    far_corner1 = shift(far_right1[:half, :], "row", -1)
     probe_new = update_probe(keep, give, probe)
-    patches_new = windows(places, field, strips, width)
+    patches_new = windows(
+        positions,
+        self_index,
+        field,
+        (far_right0, far_corner0, far_below0, far_right1, far_corner1, far_below1),
+        width,
+    )
     return (dual_new, field, probe_new, patches_new)
 
 

time: 187 us -> 194 us (1.037)
  the two profiles are of different devices: /device:TPU:9 before, /device:TPU:22 now
where the time goes in v2:
time: 194 us; the launch traced here: 193 us
  Pallas kernels  69.9 us (36%)
  waiting for transfers between devices  67.9 us (35%)
  starting transfers between devices  46.3 us (24%)
  local copies, waits for them, and re-layouts  5.11 us (3%)
  other arithmetic  3.27 us (2%)
    ppermute x10, waiting for transfers between devices, swap(): return lax.ppermute(block, ('row', 'col'), route)  40.6 us
    ppermute x13, starting transfers between devices, shift(): return lax.ppermute(block, axis, route)  37.6 us
    pallas_call x2, Pallas kernels, object_sweeps(): pl.pallas_call(sweeps_kernel, out_shape=(jax.ShapeDtypeStruct(obj.shape,...  31.2 us
    pallas_call x1, Pallas kernels, frames_update(): pl.pallas_call(frames_kernel, out_shape=(jax.ShapeDtypeStruct(dual.shape,...  27.7 us
    ppermute x13, waiting for transfers between devices, shift(): return lax.ppermute(block, axis, route)  27.3 us
    ppermute x10, starting transfers between devices, swap(): return lax.ppermute(block, ('row', 'col'), route)  8.65 us
    pallas_call x1, Pallas kernels, windows(): pl.pallas_call(windows_kernel, out_shape=jax.ShapeDtypeStruct((count, 2,...  4.91 us
    unnamed x33, local copies, waits for them, and re-layouts  4.33 us
  transfers between devices with their start and end apart: 23, of which 14 were waited for; matrix products, arithmetic and copies ran while one was open for 0% of the time, Pallas kernels for 21%

profile of v2, /device:TPU:22, one launch (start us, length us, event | category | flops | bytes accessed | tf_op | source)
XLA Modules:
  0.0 193.5 jit_solution(15415705087708221455)
XLA Ops:
  0.6 1.3 copy.13.place_ref.own_ref
  1.9 0.6 pad_add_fusion.self_ref
  2.6 27.7 %frames.1 = (f32[4,3,2,256,256]{4,3,2,1,0:T(8,128)}, f32[7,128,256]{2,1,0:T(8,128)}, f32[7,128,256]{2,1,0:T(8,128)}, f32[2,896,896]{2,1,0:T(8,128)}, f32[2,896,1...) custom-call(s32[4,2]{1,0:T(4,128)} %copy.13.place_ref.own_ref, ...), custom_call_target="tpu_custom_call" | custom-call | flops 9663676416 | bytes 20971520 | tf_op jit(solution)/shard_map/frames/pallas_call | solution.py:270
  30.4 2.6 %collective-permute-done.7 = f32[7,128,256]{2,1,0:T(8,128)S(1)} collective-permute-done((f32[7,128,256]{2,1,0:T(8,128)}, f32[7,128,256]{2,1,0:T(8,128)S(1)}, u32[]{:S(2)}, u32[]{:S(2)}) %collective-permute-start.7) | collective-permute-done | bytes 917536 | tf_op jit(solution)/shard_map/ppermute | solution.py:36
  33.0 1.4 add.49
  34.4 0.8 constant_dynamic-slice_fusion.2
  35.2 0.5 collective-permute-start.8
  35.7 1.5 collective-permute-start.10
  37.1 1.5 collective-permute-start.9
  38.6 5.2 %collective-permute-done.8 = f32[7,32,256]{2,1,0:T(8,128)S(1)} collective-permute-done((f32[7,32,256]{2,1,0:T(8,128)}, f32[7,32,256]{2,1,0:T(8,128)S(1)}, u32[]{:S(2)}, u32[]{:S(2)}) %collective-permute-start.8) | collective-permute-done | bytes 229408 | tf_op jit(solution)/shard_map/ppermute | solution.py:36
  43.8 4.1 %collective-permute-done.10 = f32[7,32,256]{2,1,0:T(8,128)S(1)} collective-permute-done((f32[7,32,256]{2,1,0:T(8,128)S(1)}, f32[7,32,256]{2,1,0:T(8,128)S(1)}, u32[]{:S(2)}, u32[]{:S(2)}) %collective-permute-start.10) | collective-permute-done | bytes 229408 | tf_op jit(solution)/shard_map/ppermute | solution.py:36
  48.0 1.3 collective-permute-done.9
  49.2 1.0 add_add_fusion
  50.2 1.6 collective-permute-start.11
  51.9 5.1 %collective-permute-done.11 = f32[7,32,256]{2,1,0:T(8,128)S(1)} collective-permute-done((f32[7,32,256]{2,1,0:T(8,128)S(1)}, f32[7,32,256]{2,1,0:T(8,128)S(1)}, u32[]{:S(2)}, u32[]{:S(2)}) %collective-permute-start.11) | collective-permute-done | bytes 229408 | tf_op jit(solution)/shard_map/ppermute | solution.py:36
  57.1 1.9 collective-permute-start.2
  59.0 1.9 collective-permute-start.1
  60.9 3.1 %collective-permute-done.12 = f32[7,32,256]{2,1,0:T(8,128)S(1)} collective-permute-done((f32[7,32,256]{2,1,0:T(8,128)S(1)}, f32[7,32,256]{2,1,0:T(8,128)S(1)}, u32[]{:S(2)}, u32[]{:S(2)}) %collective-permute-start.12) | collective-permute-done | bytes 229408 | tf_op jit(solution)/shard_map/ppermute | solution.py:36
  64.2 1.5 collective-permute-start.15
  65.7 1.9 collective-permute-start
  67.6 1.4 collective-permute-start.14
  69.0 1.3 collective-permute-done.trail_block.trail_ref
  70.3 5.8 %collective-permute-start.6 = (f32[144,896]{1,0:T(8,128)}, f32[144,896]{1,0:T(8,128)S(1)}, u32[]{:S(2)}, u32[]{:S(2)}) collective-permute-start(f32[144,896]{1,0:T(8,128)} %get-tuple-element.31), channel_id=1, source_target_pairs={{0,4},{4,8},{8,12},{12,16},{16,20},{20,24},{24,28},{1,5},{5,9},{9,... | collective-permute-start | bytes 1548296 | tf_op jit(solution)/shard_map/ppermute | solution.py:28
  76.1 3.4 %collective-permute-start.5 = (f32[144,896]{1,0:T(8,128)}, f32[144,896]{1,0:T(8,128)S(1)}, u32[]{:S(2)}, u32[]{:S(2)}) collective-permute-start(f32[144,896]{1,0:T(8,128)} %get-tuple-element.30), channel_id=1, source_target_pairs={{0,4},{4,8},{8,12},{12,16},{16,20},{20,24},{24,28},{1,5},{5,9},{9,... | collective-permute-start | bytes 1548296 | tf_op jit(solution)/shard_map/ppermute | solution.py:28
  80.0 19.2 %collective-permute-done.14.refs_2_ = f32[6,32,256]{2,1,0:T(8,128)S(1)} collective-permute-done((f32[6,32,256]{2,1,0:T(8,128)S(1)}, f32[6,32,256]{2,1,0:T(8,128)S(1)}, u32[]{:S(2)}, u32[]{:S(2)}) %collective-permute-start.14) | collective-permute-done | bytes 196640 | tf_op jit(solution)/shard_map/ppermute | solution.py:36
  99.2 4.4 %collective-permute-start.3 = (f32[2,24,896]{2,1,0:T(8,128)S(1)}, f32[2,24,896]{2,1,0:T(8,128)S(1)}, u32[]{:S(2)}, u32[]{:S(2)}) collective-permute-start(f32[2,24,896]{2,1,0:T(8,128)S(1)} %get-tuple-element.28), channel_id=1, source_target_pairs={{4,0},{8,4},{12,8},{16,12},{20,16},{24,20},{28,24},{5,1},{9,5},{13... | collective-permute-start | bytes 516104 | tf_op jit(solution)/shard_map/ppermute | solution.py:28
  103.7 0.6 join.2.refs_0_
  104.4 6.6 %collective-permute-done.3.below_ref.below_block = f32[2,24,896]{2,1,0:T(8,128)S(1)} collective-permute-done((f32[2,24,896]{2,1,0:T(8,128)S(1)}, f32[2,24,896]{2,1,0:T(8,128)S(1)}, u32[]{:S(2)}, u32[]{:S(2)}) %collective-permute-start.3) | collective-permute-done | bytes 172064 | tf_op jit(solution)/shard_map/ppermute | solution.py:28
  111.0 3.8 %collective-permute-start.4 = (f32[2,200,128]{2,1,0:T(8,128)S(1)}, f32[2,200,128]{2,1,0:T(8,128)S(1)}, u32[]{:S(2)}, u32[]{:S(2)}) collective-permute-start(f32[2,200,128]{2,1,0:T(8,128)S(1)} %get-tuple-element.29), channel_id=1, source_target_pairs={{0,4},{4,8},{8,12},{12,16},{16,20},{20,24},{24,28},{1,5},{5,9},{9,... | collective-permute-start | bytes 614408 | tf_op jit(solution)/shard_map/ppermute | solution.py:28
  114.8 4.3 %collective-permute-done.4.corner_ref.corner_block = f32[2,200,128]{2,1,0:T(8,128)S(1)} collective-permute-done((f32[2,200,128]{2,1,0:T(8,128)S(1)}, f32[2,200,128]{2,1,0:T(8,128)S(1)}, u32[]{:S(2)}, u32[]{:S(2)}) %collective-permute-start.4) | collective-permute-done | bytes 204832 | tf_op jit(solution)/shard_map/ppermute | solution.py:28
  119.2 3.7 %weights.1.weight_ref = f32[7,784,128]{2,1,0:T(8,128)S(1)} custom-call(s32[2]{0:T(128)S(1)} %copy-done.9, s32[4,2]{1,0:T(4,128)S(1)} %copy-done.8, f32[2,256,128]{2,1,0:T(8,128)S(1)} %collective-permute-done.2.link_block.lead_ref, f32[2,112,128]{2,1,0:T(8,128)S(1)} %collective-permute-done.trail_block.trail_ref, ...), custom_call_target="tpu_custom_call" | custom-call | tf_op jit(solution)/shard_map/weights/pallas_call | solution.py:401
  122.9 1.6 copy-done
  124.5 15.6 %shard_map.111 = (f32[2,768,768]{2,1,0:T(8,128)}, f32[768,128]{1,0:T(8,128)}, f32[128,768]{1,0:T(8,128)}) custom-call(f32[2,896,896]{2,1,0:T(8,128)} %get-tuple-element.23.canvas_ref, f32[2,112,128]{2,1,0:T(8,128)} %copy-done.5, f32[2,768,768]{2,1,0:T(8,128)} %obj_ref.3, f32[2,896,128]{2,1,0:T(8,128)} %collective-permute-done.1.lead_block, ...), custom_call_target="tpu_custom_call" | custom-call | tf_op jit(solution)/shard_map/pallas_call | solution.py:558
  140.2 0.8 copy-done.12
  140.9 15.6 %shard_map.112 = (f32[2,768,768]{2,1,0:T(8,128)}, f32[768,128]{1,0:T(8,128)}, f32[128,768]{1,0:T(8,128)}) custom-call(f32[2,896,896]{2,1,0:T(8,128)} %get-tuple-element.23.canvas_ref, f32[2,112,128]{2,1,0:T(8,128)} %copy-done.5, f32[2,768,768]{2,1,0:T(8,128)} %obj_ref.3, ...), custom_call_target="tpu_custom_call", output_to_operand_aliasing={{0}: (9, {})} | custom-call | tf_op jit(solution)/shard_map/pallas_call | solution.py:558
  156.5 1.9 collective-permute-start.20
  158.5 1.9 collective-permute-start.17
  160.4 1.9 collective-permute-start.22
  162.3 1.9 collective-permute-start.19
  164.3 4.3 %collective-permute-start.21 = (f32[128,128]{1,0:T(8,128)S(1)}, f32[128,128]{1,0:T(8,128)S(1)}, u32[]{:S(2)}, u32[]{:S(2)}) collective-permute-start(f32[128,128]{1,0:T(8,128)S(1)} %slice.19), channel_id=1, source_target_pairs={{4,0},{8,4},{12,8},{16,12},{20,16},{24,20},{28,24},{5,1},{9,5},{13... | collective-permute-start | bytes 196616 | tf_op jit(solution)/shard_map/ppermute | solution.py:28
  168.6 2.5 %collective-permute-start.18 = (f32[128,128]{1,0:T(8,128)S(1)}, f32[128,128]{1,0:T(8,128)S(1)}, u32[]{:S(2)}, u32[]{:S(2)}) collective-permute-start(f32[128,128]{1,0:T(8,128)S(1)} %slice.18), channel_id=1, source_target_pairs={{4,0},{8,4},{12,8},{16,12},{20,16},{24,20},{28,24},{5,1},{9,5},{13... | collective-permute-start | bytes 196616 | tf_op jit(solution)/shard_map/ppermute | solution.py:28
  171.2 4.2 %collective-permute-done.22.refs_5_ = f32[128,768]{1,0:T(8,128)S(1)} collective-permute-done((f32[128,768]{1,0:T(8,128)}, f32[128,768]{1,0:T(8,128)S(1)}, u32[]{:S(2)}, u32[]{:S(2)}) %collective-permute-start.22) | collective-permute-done | bytes 393248 | tf_op jit(solution)/shard_map/ppermute | solution.py:28
  175.4 8.5 %collective-permute-done.19.refs_2_ = f32[128,768]{1,0:T(8,128)} collective-permute-done((f32[128,768]{1,0:T(8,128)}, f32[128,768]{1,0:T(8,128)}, u32[]{:S(2)}, u32[]{:S(2)}) %collective-permute-start.19) | collective-permute-done | bytes 393248 | tf_op jit(solution)/shard_map/ppermute | solution.py:28
  183.9 1.3 collective-permute-done.21.refs_4_
  185.2 1.0 collective-permute-done.18.refs_1_
  186.2 0.6 copy-done.15
  186.8 4.9 %windows.1 = f32[4,2,256,256]{3,2,1,0:T(8,128)} custom-call(s32[4,2]{1,0:T(4,128)} %copy.13.place_ref.own_ref, s32[2]{0:T(128)} %pad_add_fusion.self_ref, f32[2,768,768]{2,1,0:T(8,128)} %get-tuple-element.19.field_ref, f32[768,128]{1,0:T(8,128)} %copy-done.11, f32[128,128]{1,0:T(8,128)} %copy-done.15, f32[128,768]{1,0:T(8,128)} %collective-permute-done.19.refs_2_, ...), custom_call_target="tpu_custom_call" | custom-call | tf_op jit(solution)/shard_map/windows/pallas_call | solution.py:656
  191.7 1.8 join.3
  (51 shorter events, 1.0 us)
Async XLA Ops:
  30.3 33.8 %copy-start.3 = (f32[3,2,256,256]{3,2,1,0:T(8,128)S(1)}, f32[3,2,256,256]{3,2,1,0:T(8,128)}, u32[]{:S(2)}) copy-start(f32[3,2,256,256]{3,2,1,0:T(8,128)} %probe_ref.3) | copy-start | bytes 4718596
  30.3 49.7 %copy-start.7 = (f32[2,16,896]{2,1,0:T(8,128)S(1)}, f32[2,16,896]{2,1,0:T(8,128)}, u32[]{:S(2)}) copy-start(f32[2,16,896]{2,1,0:T(8,128)} %get-tuple-element.27.up_ref) | copy-start | bytes 344068
  30.3 2.7 %collective-permute-start.7 = (f32[7,128,256]{2,1,0:T(8,128)}, f32[7,128,256]{2,1,0:T(8,128)S(1)}, u32[]{:S(2)}, u32[]{:S(2)}) collective-permute-start(f32[7,128,256]{2,1,0:T(8,128)} %get-tuple-element.35), channel_id=1, source_target_pairs={{0,1},{1,0},{2,3},{3,2},{4,5},{5,4},{6,7},{7,6},{8,9},{9,8},{10,11... | collective-permute-start | bytes 2752520 | tf_op jit(solution)/shard_map/ppermute | solution.py:36
  33.0 86.2 %copy-start.8 = (s32[4,2]{1,0:T(4,128)S(1)}, s32[4,2]{1,0:T(4,128)}, u32[]{:S(2)}) copy-start(s32[4,2]{1,0:T(4,128)} %copy.13.place_ref.own_ref) | copy-start | bytes 100
  33.0 86.2 %copy-start.9 = (s32[2]{0:T(128)S(1)}, s32[2]{0:T(128)}, u32[]{:S(2)}) copy-start(s32[2]{0:T(128)} %pad_add_fusion.self_ref) | copy-start | bytes 28
  35.2 8.7 %collective-permute-start.8 = (f32[7,32,256]{2,1,0:T(8,128)}, f32[7,32,256]{2,1,0:T(8,128)S(1)}, u32[]{:S(2)}, u32[]{:S(2)}) collective-permute-start(f32[7,32,256]{2,1,0:T(8,128)} %get-tuple-element.40), channel_id=1, source_target_pairs={{0,2},{1,3},{2,0},{3,1},{4,6},{5,7},{6,4},{7,5},{8,10},{9,11},{10,... | collective-permute-start | bytes 688136 | tf_op jit(solution)/shard_map/ppermute | solution.py:36
  35.7 12.3 %collective-permute-start.10 = (f32[7,32,256]{2,1,0:T(8,128)S(1)}, f32[7,32,256]{2,1,0:T(8,128)S(1)}, u32[]{:S(2)}, u32[]{:S(2)}) collective-permute-start(f32[7,32,256]{2,1,0:T(8,128)S(1)} %get-tuple-element.41), channel_id=1, source_target_pairs={{0,6},{1,7},{2,4},{3,5},{4,2},{5,3},{6,0},{7,1},{8,14},{9,15},{10,... | collective-permute-start | bytes 688136 | tf_op jit(solution)/shard_map/ppermute | solution.py:36
  37.1 12.1 %collective-permute-start.9 = (f32[7,32,256]{2,1,0:T(8,128)S(1)}, f32[7,32,256]{2,1,0:T(8,128)}, u32[]{:S(2)}, u32[]{:S(2)}) collective-permute-start(f32[7,32,256]{2,1,0:T(8,128)S(1)} %get-tuple-element.42), channel_id=1, source_target_pairs={{0,4},{1,5},{2,6},{3,7},{4,0},{5,1},{6,2},{7,3},{8,12},{9,13},{10,... | collective-permute-start | bytes 688136 | tf_op jit(solution)/shard_map/ppermute | solution.py:36
  50.2 6.7 %collective-permute-start.11 = (f32[7,32,256]{2,1,0:T(8,128)S(1)}, f32[7,32,256]{2,1,0:T(8,128)S(1)}, u32[]{:S(2)}, u32[]{:S(2)}) collective-permute-start(f32[7,32,256]{2,1,0:T(8,128)S(1)} %add_add_fusion), channel_id=1, source_target_pairs={{0,8},{1,9},{2,10},{3,11},{4,12},{5,13},{6,14},{7,15},{8,0},{9,1},... | collective-permute-start | bytes 688136 | tf_op jit(solution)/shard_map/ppermute | solution.py:36
  57.0 7.1 %collective-permute-start.12 = (f32[7,32,256]{2,1,0:T(8,128)S(1)}, f32[7,32,256]{2,1,0:T(8,128)S(1)}, u32[]{:S(2)}, u32[]{:S(2)}) collective-permute-start(f32[7,32,256]{2,1,0:T(8,128)S(1)} %add.57), channel_id=1, source_target_pairs={{0,16},{1,17},{2,18},{3,19},{4,20},{5,21},{6,22},{7,23},{8,24},{9,... | collective-permute-start | bytes 688136 | tf_op jit(solution)/shard_map/ppermute | solution.py:36
  57.1 19.0 %collective-permute-start.2 = (f32[2,256,128]{2,1,0:T(8,128)}, f32[2,256,128]{2,1,0:T(8,128)S(1)}, u32[]{:S(2)}, u32[]{:S(2)}) collective-permute-start(f32[2,256,128]{2,1,0:T(8,128)} %get-tuple-element.26), channel_id=1, source_target_pairs={{0,1},{1,2},{2,3},{4,5},{5,6},{6,7},{8,9},{9,10},{10,11},{12,13},{... | collective-permute-start | bytes 786440 | tf_op jit(solution)/shard_map/ppermute | solution.py:28
  59.0 65.5 %collective-permute-start.1 = (f32[2,896,128]{2,1,0:T(8,128)}, f32[2,896,128]{2,1,0:T(8,128)}, u32[]{:S(2)}, u32[]{:S(2)}) collective-permute-start(f32[2,896,128]{2,1,0:T(8,128)} %get-tuple-element.25), channel_id=1, source_target_pairs={{0,1},{1,2},{2,3},{4,5},{5,6},{6,7},{8,9},{9,10},{10,11},{12,13},{... | collective-permute-start | bytes 2752520 | tf_op jit(solution)/shard_map/ppermute | solution.py:28
  64.2 15.4 %collective-permute-start.15 = (f32[6,32,256]{2,1,0:T(8,128)S(1)}, f32[6,32,256]{2,1,0:T(8,128)S(1)}, u32[]{:S(2)}, u32[]{:S(2)}) collective-permute-start(f32[6,32,256]{2,1,0:T(8,128)S(1)} %fusion.refs_0_), channel_id=1, source_target_pairs={{0,6},{1,7},{2,4},{3,5},{4,2},{5,3},{6,0},{7,1},{8,14},{9,15},{10,... | collective-permute-start | bytes 589832 | tf_op jit(solution)/shard_map/ppermute | solution.py:36
  65.7 4.6 %collective-permute-start = (f32[2,112,128]{2,1,0:T(8,128)}, f32[2,112,128]{2,1,0:T(8,128)S(1)}, u32[]{:S(2)}, u32[]{:S(2)}) collective-permute-start(f32[2,112,128]{2,1,0:T(8,128)} %get-tuple-element.24), channel_id=1, source_target_pairs={{1,0},{2,1},{3,2},{5,4},{6,5},{7,6},{9,8},{10,9},{11,10},{13,12},{... | collective-permute-start | bytes 344072 | tf_op jit(solution)/shard_map/ppermute | solution.py:28
  67.6 31.6 %collective-permute-start.14 = (f32[6,32,256]{2,1,0:T(8,128)S(1)}, f32[6,32,256]{2,1,0:T(8,128)S(1)}, u32[]{:S(2)}, u32[]{:S(2)}) collective-permute-start(f32[6,32,256]{2,1,0:T(8,128)S(1)} %fusion.refs_0_), channel_id=1, source_target_pairs={{0,4},{1,5},{2,6},{3,7},{4,0},{5,1},{6,2},{7,3},{8,12},{9,13},{10,... | collective-permute-start | bytes 589832 | tf_op jit(solution)/shard_map/ppermute | solution.py:36
  70.3 54.2 %copy-start.5 = (f32[2,112,128]{2,1,0:T(8,128)}, f32[2,112,128]{2,1,0:T(8,128)S(1)}, u32[]{:S(2)}) copy-start(f32[2,112,128]{2,1,0:T(8,128)S(1)} %collective-permute-done.trail_block.trail_ref) | copy-start | bytes 344068
  70.3 48.9 %collective-permute-start.6 = (f32[144,896]{1,0:T(8,128)}, f32[144,896]{1,0:T(8,128)S(1)}, u32[]{:S(2)}, u32[]{:S(2)}) collective-permute-start(f32[144,896]{1,0:T(8,128)} %get-tuple-element.31), channel_id=1, source_target_pairs={{0,4},{4,8},{8,12},{12,16},{16,20},{20,24},{24,28},{1,5},{5,9},{9,... | collective-permute-start | bytes 1548296 | tf_op jit(solution)/shard_map/ppermute | solution.py:28
  76.1 48.4 %copy-start.1 = (f32[2,256,128]{2,1,0:T(8,128)}, f32[2,256,128]{2,1,0:T(8,128)S(1)}, u32[]{:S(2)}) copy-start(f32[2,256,128]{2,1,0:T(8,128)S(1)} %collective-permute-done.2.link_block.lead_ref) | copy-start | bytes 786436
  76.1 64.0 %collective-permute-start.5 = (f32[144,896]{1,0:T(8,128)}, f32[144,896]{1,0:T(8,128)S(1)}, u32[]{:S(2)}, u32[]{:S(2)}) collective-permute-start(f32[144,896]{1,0:T(8,128)} %get-tuple-element.30), channel_id=1, source_target_pairs={{0,4},{4,8},{8,12},{12,16},{16,20},{20,24},{24,28},{1,5},{5,9},{9,... | collective-permute-start | bytes 1548296 | tf_op jit(solution)/shard_map/ppermute | solution.py:28
  79.6 24.1 %collective-permute-start.13 = (f32[6,32,256]{2,1,0:T(8,128)S(1)}, f32[6,32,256]{2,1,0:T(8,128)S(1)}, u32[]{:S(2)}, u32[]{:S(2)}) collective-permute-start(f32[6,32,256]{2,1,0:T(8,128)S(1)} %fusion.refs_0_), channel_id=1, source_target_pairs={{0,2},{1,3},{2,0},{3,1},{4,6},{5,7},{6,4},{7,5},{8,10},{9,11},{10,... | collective-permute-start | bytes 589832 | tf_op jit(solution)/shard_map/ppermute | solution.py:36
  99.2 11.8 %collective-permute-start.3 = (f32[2,24,896]{2,1,0:T(8,128)S(1)}, f32[2,24,896]{2,1,0:T(8,128)S(1)}, u32[]{:S(2)}, u32[]{:S(2)}) collective-permute-start(f32[2,24,896]{2,1,0:T(8,128)S(1)} %get-tuple-element.28), channel_id=1, source_target_pairs={{4,0},{8,4},{12,8},{16,12},{20,16},{24,20},{28,24},{5,1},{9,5},{13... | collective-permute-start | bytes 516104 | tf_op jit(solution)/shard_map/ppermute | solution.py:28
  104.3 87.4 %collective-permute-start.16 = (f32[6,128,256]{2,1,0:T(8,128)S(1)}, f32[6,128,256]{2,1,0:T(8,128)S(1)}, u32[]{:S(2)}, u32[]{:S(2)}) collective-permute-start(f32[6,128,256]{2,1,0:T(8,128)S(1)} %join.2.refs_0_), channel_id=1, source_target_pairs={{0,1},{1,0},{2,3},{3,2},{4,5},{5,4},{6,7},{7,6},{8,9},{9,8},{10,11... | collective-permute-start | bytes 2359304 | tf_op jit(solution)/shard_map/ppermute | solution.py:36
  111.0 13.5 %copy-start.6 = (f32[2,24,896]{2,1,0:T(8,128)}, f32[2,24,896]{2,1,0:T(8,128)S(1)}, u32[]{:S(2)}) copy-start(f32[2,24,896]{2,1,0:T(8,128)S(1)} %collective-permute-done.3.below_ref.below_block) | copy-start | bytes 516100
  111.0 8.2 %collective-permute-start.4 = (f32[2,200,128]{2,1,0:T(8,128)S(1)}, f32[2,200,128]{2,1,0:T(8,128)S(1)}, u32[]{:S(2)}, u32[]{:S(2)}) collective-permute-start(f32[2,200,128]{2,1,0:T(8,128)S(1)} %get-tuple-element.29), channel_id=1, source_target_pairs={{0,4},{4,8},{8,12},{12,16},{16,20},{20,24},{24,28},{1,5},{5,9},{9,... | collective-permute-start | bytes 614408 | tf_op jit(solution)/shard_map/ppermute | solution.py:28
  119.2 5.4 %copy-start.4 = (f32[2,200,128]{2,1,0:T(8,128)}, f32[2,200,128]{2,1,0:T(8,128)S(1)}, u32[]{:S(2)}) copy-start(f32[2,200,128]{2,1,0:T(8,128)S(1)} %collective-permute-done.4.corner_ref.corner_block) | copy-start | bytes 614404
  119.2 5.3 %copy-start.2 = (f32[144,896]{1,0:T(8,128)}, f32[144,896]{1,0:T(8,128)S(1)}, u32[]{:S(2)}) copy-start(f32[144,896]{1,0:T(8,128)S(1)} %collective-permute-done.6.above_ref) | copy-start | bytes 1548292
  122.9 1.6 copy-start
  140.2 0.8 copy-start.12
  156.5 7.7 %collective-permute-start.20 = (f32[768,128]{1,0:T(8,128)}, f32[768,128]{1,0:T(8,128)S(1)}, u32[]{:S(2)}, u32[]{:S(2)}) collective-permute-start(f32[768,128]{1,0:T(8,128)} %get-tuple-element.38), channel_id=1, source_target_pairs={{1,0},{2,1},{3,2},{5,4},{6,5},{7,6},{9,8},{10,9},{11,10},{13,12},{... | collective-permute-start | bytes 1179656 | tf_op jit(solution)/shard_map/ppermute | solution.py:28
  158.5 10.1 %collective-permute-start.17 = (f32[768,128]{1,0:T(8,128)}, f32[768,128]{1,0:T(8,128)S(1)}, u32[]{:S(2)}, u32[]{:S(2)}) collective-permute-start(f32[768,128]{1,0:T(8,128)} %get-tuple-element.36), channel_id=1, source_target_pairs={{1,0},{2,1},{3,2},{5,4},{6,5},{7,6},{9,8},{10,9},{11,10},{13,12},{... | collective-permute-start | bytes 1179656 | tf_op jit(solution)/shard_map/ppermute | solution.py:28
  160.4 15.0 %collective-permute-start.22 = (f32[128,768]{1,0:T(8,128)}, f32[128,768]{1,0:T(8,128)S(1)}, u32[]{:S(2)}, u32[]{:S(2)}) collective-permute-start(f32[128,768]{1,0:T(8,128)} %get-tuple-element.39), channel_id=1, source_target_pairs={{4,0},{8,4},{12,8},{16,12},{20,16},{24,20},{28,24},{5,1},{9,5},{13... | collective-permute-start | bytes 1179656 | tf_op jit(solution)/shard_map/ppermute | solution.py:28
  162.3 21.6 %collective-permute-start.19 = (f32[128,768]{1,0:T(8,128)}, f32[128,768]{1,0:T(8,128)}, u32[]{:S(2)}, u32[]{:S(2)}) collective-permute-start(f32[128,768]{1,0:T(8,128)} %get-tuple-element.37), channel_id=1, source_target_pairs={{4,0},{8,4},{12,8},{16,12},{20,16},{24,20},{28,24},{5,1},{9,5},{13... | collective-permute-start | bytes 1179656 | tf_op jit(solution)/shard_map/ppermute | solution.py:28
  164.3 21.9 %copy-start.10 = (f32[768,128]{1,0:T(8,128)}, f32[768,128]{1,0:T(8,128)S(1)}, u32[]{:S(2)}) copy-start(f32[768,128]{1,0:T(8,128)S(1)} %collective-permute-done.20.refs_3_) | copy-start | bytes 1179652
  164.3 20.9 %collective-permute-start.21 = (f32[128,128]{1,0:T(8,128)S(1)}, f32[128,128]{1,0:T(8,128)S(1)}, u32[]{:S(2)}, u32[]{:S(2)}) collective-permute-start(f32[128,128]{1,0:T(8,128)S(1)} %slice.19), channel_id=1, source_target_pairs={{4,0},{8,4},{12,8},{16,12},{20,16},{24,20},{28,24},{5,1},{9,5},{13... | collective-permute-start | bytes 196616 | tf_op jit(solution)/shard_map/ppermute | solution.py:28
  168.6 17.6 %copy-start.11 = (f32[768,128]{1,0:T(8,128)}, f32[768,128]{1,0:T(8,128)S(1)}, u32[]{:S(2)}) copy-start(f32[768,128]{1,0:T(8,128)S(1)} %collective-permute-done.17.refs_0_) | copy-start | bytes 1179652
  168.6 17.5 %collective-permute-start.18 = (f32[128,128]{1,0:T(8,128)S(1)}, f32[128,128]{1,0:T(8,128)S(1)}, u32[]{:S(2)}, u32[]{:S(2)}) collective-permute-start(f32[128,128]{1,0:T(8,128)S(1)} %slice.18), channel_id=1, source_target_pairs={{4,0},{8,4},{12,8},{16,12},{20,16},{24,20},{28,24},{5,1},{9,5},{13... | collective-permute-start | bytes 196616 | tf_op jit(solution)/shard_map/ppermute | solution.py:28
  175.4 10.8 %copy-start.13 = (f32[128,768]{1,0:T(8,128)}, f32[128,768]{1,0:T(8,128)S(1)}, u32[]{:S(2)}) copy-start(f32[128,768]{1,0:T(8,128)S(1)} %collective-permute-done.22.refs_5_) | copy-start | bytes 1179652
  185.2 1.0 copy-start.14
  186.2 0.6 copy-start.15

commit v3 on v2

--- a/solution.py
+++ b/solution.py
@@ -146,8 +146,12 @@
                 axis=0,
             )
 
-        far_even = times_left(0, stack(lambda a, b: a + b))
-        far_odd = times_left(1, stack(lambda a, b: a - b))
+        even_ref[m] = stack(lambda a, b: a + b)
+        odd_ref[m] = stack(lambda a, b: a - b)
+
+    for m in range(modes):
+        far_even = times_left(0, even_ref[m])
+        far_odd = times_left(1, odd_ref[m])
         even_ref[m] = far_even
         odd_ref[m] = far_odd
         for parity, far in enumerate((far_even, far_odd)):
@@ -179,8 +183,12 @@
                 axis=0,
             )
 
-        even = times_right(rows_of(slice(0, half)), 2)
-        odd = times_right(rows_of(slice(half, width)), 3)
+        even_ref[m] = rows_of(slice(0, half))
+        odd_ref[m] = rows_of(slice(half, width))
+
+    for m in range(modes):
+        even = times_right(even_ref[m], 2)
+        odd = times_right(odd_ref[m], 3)
         low = even + odd
         high = even - odd
         near_re = jnp.concatenate([low[:, :half], high[:, :half]], axis=1)
@@ -618,40 +626,60 @@
 
 def windows_kernel(place_ref, self_ref, field_ref, *refs):
     strips = refs[:-4]
-    out_ref, whole_ref, load_sem, store_sem = refs[-4:]
+    out_ref, block_ref, load_sem, store_sem = refs[-4:]
     tile = field_ref.shape[1]
     width = out_ref.shape[-1]
     half = width // 2
-    moves = [(field_ref, whole_ref.at[:, :tile, :tile])]
-    for part in range(2):
-        moves.append((strips[3 * part], whole_ref.at[part, :tile, tile:]))
-        moves.append((strips[3 * part + 1], whole_ref.at[part, tile:, tile:]))
-        moves.append((strips[3 * part + 2], whole_ref.at[part, tile:, :tile]))
-    loads = [
-        pltpu.make_async_copy(source, target, load_sem.at[n]) for n, (source, target) in enumerate(moves)
-    ]
-    for copy in loads:
-        copy.start()
-    for copy in loads:
-        copy.wait()
+    quadrants = [(down, right) for down in range(2) for right in range(2)]
+
+    def spot(frame, part, down, right):
+        return block_ref.at[
+            frame, part, down * half : (down + 1) * half, right * half : (right + 1) * half
+        ]
+
+    for frame in range(out_ref.shape[0]):
+        for n, (down, right) in enumerate(quadrants):
+            row = pl.multiple_of(place_ref[frame, 0] - self_ref[0] * tile + down * half, half)
+            col = pl.multiple_of(place_ref[frame, 1] - self_ref[1] * tile + right * half, half)
+            above, before = row < tile, col < tile
+            for part in range(2):
+                side_ref, corner_ref, below_ref = strips[3 * part : 3 * part + 3]
+                sem = load_sem.at[frame, n, part]
+
+                def fetch(source):
+                    pltpu.make_async_copy(source, spot(frame, part, down, right), sem).start()
+
+                @pl.when(above & before)
+                def _():
+                    fetch(field_ref.at[part, pl.ds(row, half), pl.ds(col, half)])
+
+                @pl.when(above & jnp.logical_not(before))
+                def _():
+                    fetch(side_ref.at[pl.ds(row, half), :])
+
+                @pl.when(jnp.logical_not(above) & before)
+                def _():
+                    fetch(below_ref.at[:, pl.ds(col, half)])
+
+                @pl.when(jnp.logical_not(above | before))
+                def _():
+                    fetch(corner_ref)
+
     stores = []
     for frame in range(out_ref.shape[0]):
-        row = pl.multiple_of(place_ref[frame, 0] - self_ref[0] * tile, half)
-        col = pl.multiple_of(place_ref[frame, 1] - self_ref[1] * tile, half)
-        stores.append(
-            pltpu.make_async_copy(
-                whole_ref.at[:, pl.ds(row, width), pl.ds(col, width)], out_ref.at[frame], store_sem.at[frame]
-            )
-        )
-    for copy in stores:
-        copy.start()
+        for n, (down, right) in enumerate(quadrants):
+            for part in range(2):
+                pltpu.make_async_copy(
+                    strips[1], spot(frame, part, down, right), load_sem.at[frame, n, part]
+                ).wait()
+        stores.append(pltpu.make_async_copy(block_ref.at[frame], out_ref.at[frame], store_sem.at[frame]))
+        stores[-1].start()
     for copy in stores:
         copy.wait()
 
 
 def windows(places, self_index, field, strips, width):
     count = places.shape[0]
-    grow = field.shape[1] + width // 2
     anywhere = pl.BlockSpec(memory_space=pl.ANY)
     return pl.pallas_call(
         windows_kernel,
@@ -659,8 +687,8 @@
         in_specs=[pl.BlockSpec(memory_space=pltpu.SMEM)] * 2 + [anywhere] * 7,
         out_specs=anywhere,
         scratch_shapes=[
-            pltpu.VMEM((2, grow, grow), jnp.float32),
-            pltpu.SemaphoreType.DMA((7,)),
+            pltpu.VMEM((count, 2, width, width), jnp.float32),
+            pltpu.SemaphoreType.DMA((count, 4, 2)),
             pltpu.SemaphoreType.DMA((count,)),
         ],
         compiler_params=pltpu.CompilerParams(vmem_limit_bytes=56 << 20),

time: 194 us -> 190 us (0.979)
  Pallas kernels: 69.9 us -> 65.7 us
    pallas_call x1, Pallas kernels: 27.7 us -> 25 us  [frames_update(): pl.pallas_call(frames_kernel, out_shape=(jax.ShapeDtypeStruct(dual.shape,...]
where the time goes in v3:
time: 190 us; the launch traced here: 189 us
  waiting for transfers between devices  67.9 us (36%)
  Pallas kernels  65.7 us (35%)
  starting transfers between devices  46.3 us (24%)
  local copies, waits for them, and re-layouts  5.11 us (3%)
  other arithmetic  3.27 us (2%)
    ppermute x10, waiting for transfers between devices, swap(): return lax.ppermute(block, ('row', 'col'), route)  40.6 us
    ppermute x13, starting transfers between devices, shift(): return lax.ppermute(block, axis, route)  37.6 us
    pallas_call x2, Pallas kernels, object_sweeps(): pl.pallas_call(sweeps_kernel, out_shape=(jax.ShapeDtypeStruct(obj.shape,...  31.2 us
    ppermute x13, waiting for transfers between devices, shift(): return lax.ppermute(block, axis, route)  27.3 us
    pallas_call x1, Pallas kernels, frames_update(): pl.pallas_call(frames_kernel, out_shape=(jax.ShapeDtypeStruct(dual.shape,...  25 us
    ppermute x10, starting transfers between devices, swap(): return lax.ppermute(block, ('row', 'col'), route)  8.65 us
    unnamed x33, local copies, waits for them, and re-layouts  4.33 us
  transfers between devices with their start and end apart: 23, of which 14 were waited for; matrix products, arithmetic and copies ran while one was open for 0% of the time, Pallas kernels for 21%

profile of v3, /device:TPU:22, one launch (start us, length us, event | category | flops | bytes accessed | tf_op | source)
XLA Modules:
  0.0 189.3 jit_solution(13564280941195739177)
XLA Ops:
  0.6 1.3 copy.13.place_ref.own_ref
  1.9 0.6 pad_add_fusion.self_ref
  2.6 25.0 %frames.1 = (f32[4,3,2,256,256]{4,3,2,1,0:T(8,128)}, f32[7,128,256]{2,1,0:T(8,128)}, f32[7,128,256]{2,1,0:T(8,128)}, f32[2,896,896]{2,1,0:T(8,128)}, f32[2,896,1...) custom-call(s32[4,2]{1,0:T(4,128)} %copy.13.place_ref.own_ref, ...), custom_call_target="tpu_custom_call" | custom-call | flops 9663676416 | bytes 20971520 | tf_op jit(solution)/shard_map/frames/pallas_call | solution.py:278
  27.7 2.6 %collective-permute-done.7 = f32[7,128,256]{2,1,0:T(8,128)S(1)} collective-permute-done((f32[7,128,256]{2,1,0:T(8,128)}, f32[7,128,256]{2,1,0:T(8,128)S(1)}, u32[]{:S(2)}, u32[]{:S(2)}) %collective-permute-start.7) | collective-permute-done | bytes 917536 | tf_op jit(solution)/shard_map/ppermute | solution.py:36
  30.3 1.4 add.49
  31.7 0.8 constant_dynamic-slice_fusion.2
  32.4 0.5 collective-permute-start.8
  33.0 1.5 collective-permute-start.10
  34.4 1.5 collective-permute-start.9
  35.9 5.2 %collective-permute-done.8 = f32[7,32,256]{2,1,0:T(8,128)S(1)} collective-permute-done((f32[7,32,256]{2,1,0:T(8,128)}, f32[7,32,256]{2,1,0:T(8,128)S(1)}, u32[]{:S(2)}, u32[]{:S(2)}) %collective-permute-start.8) | collective-permute-done | bytes 229408 | tf_op jit(solution)/shard_map/ppermute | solution.py:36
  41.1 4.1 %collective-permute-done.10 = f32[7,32,256]{2,1,0:T(8,128)S(1)} collective-permute-done((f32[7,32,256]{2,1,0:T(8,128)S(1)}, f32[7,32,256]{2,1,0:T(8,128)S(1)}, u32[]{:S(2)}, u32[]{:S(2)}) %collective-permute-start.10) | collective-permute-done | bytes 229408 | tf_op jit(solution)/shard_map/ppermute | solution.py:36
  45.3 1.3 collective-permute-done.9
  46.5 1.0 add_add_fusion
  47.5 1.6 collective-permute-start.11
  49.1 5.1 %collective-permute-done.11 = f32[7,32,256]{2,1,0:T(8,128)S(1)} collective-permute-done((f32[7,32,256]{2,1,0:T(8,128)S(1)}, f32[7,32,256]{2,1,0:T(8,128)S(1)}, u32[]{:S(2)}, u32[]{:S(2)}) %collective-permute-start.11) | collective-permute-done | bytes 229408 | tf_op jit(solution)/shard_map/ppermute | solution.py:36
  54.3 1.9 %collective-permute-start.2 = (f32[2,256,128]{2,1,0:T(8,128)}, f32[2,256,128]{2,1,0:T(8,128)S(1)}, u32[]{:S(2)}, u32[]{:S(2)}) collective-permute-start(f32[2,256,128]{2,1,0:T(8,128)} %get-tuple-element.26), channel_id=1, source_target_pairs={{0,1},{1,2},{2,3},{4,5},{5,6},{6,7},{8,9},{9,10},{10,11},{12,13},{... | collective-permute-start | bytes 786440 | tf_op jit(solution)/shard_map/ppermute | solution.py:28
  56.3 1.9 %collective-permute-start.1 = (f32[2,896,128]{2,1,0:T(8,128)}, f32[2,896,128]{2,1,0:T(8,128)}, u32[]{:S(2)}, u32[]{:S(2)}) collective-permute-start(f32[2,896,128]{2,1,0:T(8,128)} %get-tuple-element.25), channel_id=1, source_target_pairs={{0,1},{1,2},{2,3},{4,5},{5,6},{6,7},{8,9},{9,10},{10,11},{12,13},{... | collective-permute-start | bytes 2752520 | tf_op jit(solution)/shard_map/ppermute | solution.py:28
  58.2 3.1 %collective-permute-done.12 = f32[7,32,256]{2,1,0:T(8,128)S(1)} collective-permute-done((f32[7,32,256]{2,1,0:T(8,128)S(1)}, f32[7,32,256]{2,1,0:T(8,128)S(1)}, u32[]{:S(2)}, u32[]{:S(2)}) %collective-permute-start.12) | collective-permute-done | bytes 229408 | tf_op jit(solution)/shard_map/ppermute | solution.py:36
  61.4 1.6 collective-permute-start.15
  63.0 1.9 %collective-permute-start = (f32[2,112,128]{2,1,0:T(8,128)}, f32[2,112,128]{2,1,0:T(8,128)S(1)}, u32[]{:S(2)}, u32[]{:S(2)}) collective-permute-start(f32[2,112,128]{2,1,0:T(8,128)} %get-tuple-element.24), channel_id=1, source_target_pairs={{1,0},{2,1},{3,2},{5,4},{6,5},{7,6},{9,8},{10,9},{11,10},{13,12},{... | collective-permute-start | bytes 344072 | tf_op jit(solution)/shard_map/ppermute | solution.py:28
  64.9 1.4 collective-permute-start.14
  66.3 1.3 collective-permute-done.trail_block.trail_ref
  67.6 5.8 %collective-permute-start.6 = (f32[144,896]{1,0:T(8,128)}, f32[144,896]{1,0:T(8,128)S(1)}, u32[]{:S(2)}, u32[]{:S(2)}) collective-permute-start(f32[144,896]{1,0:T(8,128)} %get-tuple-element.31), channel_id=1, source_target_pairs={{0,4},{4,8},{8,12},{12,16},{16,20},{20,24},{24,28},{1,5},{5,9},{9,... | collective-permute-start | bytes 1548296 | tf_op jit(solution)/shard_map/ppermute | solution.py:28
  73.4 3.4 %collective-permute-start.5 = (f32[144,896]{1,0:T(8,128)}, f32[144,896]{1,0:T(8,128)S(1)}, u32[]{:S(2)}, u32[]{:S(2)}) collective-permute-start(f32[144,896]{1,0:T(8,128)} %get-tuple-element.30), channel_id=1, source_target_pairs={{0,4},{4,8},{8,12},{12,16},{16,20},{20,24},{24,28},{1,5},{5,9},{9,... | collective-permute-start | bytes 1548296 | tf_op jit(solution)/shard_map/ppermute | solution.py:28
  77.3 19.2 %collective-permute-done.14.refs_2_ = f32[6,32,256]{2,1,0:T(8,128)S(1)} collective-permute-done((f32[6,32,256]{2,1,0:T(8,128)S(1)}, f32[6,32,256]{2,1,0:T(8,128)S(1)}, u32[]{:S(2)}, u32[]{:S(2)}) %collective-permute-start.14) | collective-permute-done | bytes 196640 | tf_op jit(solution)/shard_map/ppermute | solution.py:36
  96.5 4.4 %collective-permute-start.3 = (f32[2,24,896]{2,1,0:T(8,128)S(1)}, f32[2,24,896]{2,1,0:T(8,128)S(1)}, u32[]{:S(2)}, u32[]{:S(2)}) collective-permute-start(f32[2,24,896]{2,1,0:T(8,128)S(1)} %get-tuple-element.28), channel_id=1, source_target_pairs={{4,0},{8,4},{12,8},{16,12},{20,16},{24,20},{28,24},{5,1},{9,5},{13... | collective-permute-start | bytes 516104 | tf_op jit(solution)/shard_map/ppermute | solution.py:28
  101.0 0.6 join.2.refs_0_
  101.7 6.6 %collective-permute-done.3.below_ref.below_block = f32[2,24,896]{2,1,0:T(8,128)S(1)} collective-permute-done((f32[2,24,896]{2,1,0:T(8,128)S(1)}, f32[2,24,896]{2,1,0:T(8,128)S(1)}, u32[]{:S(2)}, u32[]{:S(2)}) %collective-permute-start.3) | collective-permute-done | bytes 172064 | tf_op jit(solution)/shard_map/ppermute | solution.py:28
  108.3 3.8 %collective-permute-start.4 = (f32[2,200,128]{2,1,0:T(8,128)S(1)}, f32[2,200,128]{2,1,0:T(8,128)S(1)}, u32[]{:S(2)}, u32[]{:S(2)}) collective-permute-start(f32[2,200,128]{2,1,0:T(8,128)S(1)} %get-tuple-element.29), channel_id=1, source_target_pairs={{0,4},{4,8},{8,12},{12,16},{16,20},{20,24},{24,28},{1,5},{5,9},{9,... | collective-permute-start | bytes 614408 | tf_op jit(solution)/shard_map/ppermute | solution.py:28
  112.1 4.3 %collective-permute-done.4.corner_ref.corner_block = f32[2,200,128]{2,1,0:T(8,128)S(1)} collective-permute-done((f32[2,200,128]{2,1,0:T(8,128)S(1)}, f32[2,200,128]{2,1,0:T(8,128)S(1)}, u32[]{:S(2)}, u32[]{:S(2)}) %collective-permute-start.4) | collective-permute-done | bytes 204832 | tf_op jit(solution)/shard_map/ppermute | solution.py:28
  116.5 3.7 %weights.1.weight_ref = f32[7,784,128]{2,1,0:T(8,128)S(1)} custom-call(s32[2]{0:T(128)S(1)} %copy-done.9, s32[4,2]{1,0:T(4,128)S(1)} %copy-done.8, f32[2,256,128]{2,1,0:T(8,128)S(1)} %collective-permute-done.2.link_block.lead_ref, f32[2,112,128]{2,1,0:T(8,128)S(1)} %collective-permute-done.trail_block.trail_ref, ...), custom_call_target="tpu_custom_call" | custom-call | tf_op jit(solution)/shard_map/weights/pallas_call | solution.py:409
  120.2 1.6 copy-done
  121.8 15.6 %shard_map.111 = (f32[2,768,768]{2,1,0:T(8,128)}, f32[768,128]{1,0:T(8,128)}, f32[128,768]{1,0:T(8,128)}) custom-call(f32[2,896,896]{2,1,0:T(8,128)} %get-tuple-element.23.canvas_ref, f32[2,112,128]{2,1,0:T(8,128)} %copy-done.5, f32[2,768,768]{2,1,0:T(8,128)} %obj_ref.3, f32[2,896,128]{2,1,0:T(8,128)} %collective-permute-done.1.lead_block, ...), custom_call_target="tpu_custom_call" | custom-call | tf_op jit(solution)/shard_map/pallas_call | solution.py:566
  137.4 0.8 copy-done.12
  138.2 15.6 %shard_map.112 = (f32[2,768,768]{2,1,0:T(8,128)}, f32[768,128]{1,0:T(8,128)}, f32[128,768]{1,0:T(8,128)}) custom-call(f32[2,896,896]{2,1,0:T(8,128)} %get-tuple-element.23.canvas_ref, f32[2,112,128]{2,1,0:T(8,128)} %copy-done.5, f32[2,768,768]{2,1,0:T(8,128)} %obj_ref.3, ...), custom_call_target="tpu_custom_call", output_to_operand_aliasing={{0}: (9, {})} | custom-call | tf_op jit(solution)/shard_map/pallas_call | solution.py:566
  153.8 1.9 %collective-permute-start.20 = (f32[768,128]{1,0:T(8,128)}, f32[768,128]{1,0:T(8,128)S(1)}, u32[]{:S(2)}, u32[]{:S(2)}) collective-permute-start(f32[768,128]{1,0:T(8,128)} %get-tuple-element.38), channel_id=1, source_target_pairs={{1,0},{2,1},{3,2},{5,4},{6,5},{7,6},{9,8},{10,9},{11,10},{13,12},{... | collective-permute-start | bytes 1179656 | tf_op jit(solution)/shard_map/ppermute | solution.py:28
  155.7 1.9 %collective-permute-start.17 = (f32[768,128]{1,0:T(8,128)}, f32[768,128]{1,0:T(8,128)S(1)}, u32[]{:S(2)}, u32[]{:S(2)}) collective-permute-start(f32[768,128]{1,0:T(8,128)} %get-tuple-element.36), channel_id=1, source_target_pairs={{1,0},{2,1},{3,2},{5,4},{6,5},{7,6},{9,8},{10,9},{11,10},{13,12},{... | collective-permute-start | bytes 1179656 | tf_op jit(solution)/shard_map/ppermute | solution.py:28
  157.7 1.9 %collective-permute-start.22 = (f32[128,768]{1,0:T(8,128)}, f32[128,768]{1,0:T(8,128)S(1)}, u32[]{:S(2)}, u32[]{:S(2)}) collective-permute-start(f32[128,768]{1,0:T(8,128)} %get-tuple-element.39), channel_id=1, source_target_pairs={{4,0},{8,4},{12,8},{16,12},{20,16},{24,20},{28,24},{5,1},{9,5},{13... | collective-permute-start | bytes 1179656 | tf_op jit(solution)/shard_map/ppermute | solution.py:28
  159.6 1.9 %collective-permute-start.19 = (f32[128,768]{1,0:T(8,128)}, f32[128,768]{1,0:T(8,128)}, u32[]{:S(2)}, u32[]{:S(2)}) collective-permute-start(f32[128,768]{1,0:T(8,128)} %get-tuple-element.37), channel_id=1, source_target_pairs={{4,0},{8,4},{12,8},{16,12},{20,16},{24,20},{28,24},{5,1},{9,5},{13... | collective-permute-start | bytes 1179656 | tf_op jit(solution)/shard_map/ppermute | solution.py:28
  161.6 4.3 %collective-permute-start.21 = (f32[128,128]{1,0:T(8,128)S(1)}, f32[128,128]{1,0:T(8,128)S(1)}, u32[]{:S(2)}, u32[]{:S(2)}) collective-permute-start(f32[128,128]{1,0:T(8,128)S(1)} %slice.19), channel_id=1, source_target_pairs={{4,0},{8,4},{12,8},{16,12},{20,16},{24,20},{28,24},{5,1},{9,5},{13... | collective-permute-start | bytes 196616 | tf_op jit(solution)/shard_map/ppermute | solution.py:28
  165.9 2.5 %collective-permute-start.18 = (f32[128,128]{1,0:T(8,128)S(1)}, f32[128,128]{1,0:T(8,128)S(1)}, u32[]{:S(2)}, u32[]{:S(2)}) collective-permute-start(f32[128,128]{1,0:T(8,128)S(1)} %slice.18), channel_id=1, source_target_pairs={{4,0},{8,4},{12,8},{16,12},{20,16},{24,20},{28,24},{5,1},{9,5},{13... | collective-permute-start | bytes 196616 | tf_op jit(solution)/shard_map/ppermute | solution.py:28
  168.5 4.2 %collective-permute-done.22.refs_5_ = f32[128,768]{1,0:T(8,128)S(1)} collective-permute-done((f32[128,768]{1,0:T(8,128)}, f32[128,768]{1,0:T(8,128)S(1)}, u32[]{:S(2)}, u32[]{:S(2)}) %collective-permute-start.22) | collective-permute-done | bytes 393248 | tf_op jit(solution)/shard_map/ppermute | solution.py:28
  172.7 8.5 %collective-permute-done.19.refs_2_ = f32[128,768]{1,0:T(8,128)} collective-permute-done((f32[128,768]{1,0:T(8,128)}, f32[128,768]{1,0:T(8,128)}, u32[]{:S(2)}, u32[]{:S(2)}) %collective-permute-start.19) | collective-permute-done | bytes 393248 | tf_op jit(solution)/shard_map/ppermute | solution.py:28
  181.2 1.3 collective-permute-done.21.refs_4_
  182.5 1.0 collective-permute-done.18.refs_1_
  183.5 0.6 copy-done.15
  184.1 3.4 %windows.1 = f32[4,2,256,256]{3,2,1,0:T(8,128)} custom-call(s32[4,2]{1,0:T(4,128)} %copy.13.place_ref.own_ref, s32[2]{0:T(128)} %pad_add_fusion.self_ref, f32[2,768,768]{2,1,0:T(8,128)} %get-tuple-element.19.field_ref, f32[768,128]{1,0:T(8,128)} %copy-done.11, f32[128,128]{1,0:T(8,128)} %copy-done.15, f32[128,768]{1,0:T(8,128)} %collective-permute-done.19.refs_2_, ...), custom_call_target="tpu_custom_call" | custom-call | tf_op jit(solution)/shard_map/windows/pallas_call | solution.py:684
  187.5 1.8 join.3
  (51 shorter events, 1.0 us)
Async XLA Ops:
  27.5 33.8 %copy-start.3 = (f32[3,2,256,256]{3,2,1,0:T(8,128)S(1)}, f32[3,2,256,256]{3,2,1,0:T(8,128)}, u32[]{:S(2)}) copy-start(f32[3,2,256,256]{3,2,1,0:T(8,128)} %probe_ref.3) | copy-start | bytes 4718596
  27.6 49.7 %copy-start.7 = (f32[2,16,896]{2,1,0:T(8,128)S(1)}, f32[2,16,896]{2,1,0:T(8,128)}, u32[]{:S(2)}) copy-start(f32[2,16,896]{2,1,0:T(8,128)} %get-tuple-element.27.up_ref) | copy-start | bytes 344068
  27.6 2.7 %collective-permute-start.7 = (f32[7,128,256]{2,1,0:T(8,128)}, f32[7,128,256]{2,1,0:T(8,128)S(1)}, u32[]{:S(2)}, u32[]{:S(2)}) collective-permute-start(f32[7,128,256]{2,1,0:T(8,128)} %get-tuple-element.35), channel_id=1, source_target_pairs={{0,1},{1,0},{2,3},{3,2},{4,5},{5,4},{6,7},{7,6},{8,9},{9,8},{10,11... | collective-permute-start | bytes 2752520 | tf_op jit(solution)/shard_map/ppermute | solution.py:36
  30.3 86.2 %copy-start.8 = (s32[4,2]{1,0:T(4,128)S(1)}, s32[4,2]{1,0:T(4,128)}, u32[]{:S(2)}) copy-start(s32[4,2]{1,0:T(4,128)} %copy.13.place_ref.own_ref) | copy-start | bytes 100
  30.3 86.2 %copy-start.9 = (s32[2]{0:T(128)S(1)}, s32[2]{0:T(128)}, u32[]{:S(2)}) copy-start(s32[2]{0:T(128)} %pad_add_fusion.self_ref) | copy-start | bytes 28
  32.4 8.7 %collective-permute-start.8 = (f32[7,32,256]{2,1,0:T(8,128)}, f32[7,32,256]{2,1,0:T(8,128)S(1)}, u32[]{:S(2)}, u32[]{:S(2)}) collective-permute-start(f32[7,32,256]{2,1,0:T(8,128)} %get-tuple-element.40), channel_id=1, source_target_pairs={{0,2},{1,3},{2,0},{3,1},{4,6},{5,7},{6,4},{7,5},{8,10},{9,11},{10,... | collective-permute-start | bytes 688136 | tf_op jit(solution)/shard_map/ppermute | solution.py:36
  33.0 12.3 %collective-permute-start.10 = (f32[7,32,256]{2,1,0:T(8,128)S(1)}, f32[7,32,256]{2,1,0:T(8,128)S(1)}, u32[]{:S(2)}, u32[]{:S(2)}) collective-permute-start(f32[7,32,256]{2,1,0:T(8,128)S(1)} %get-tuple-element.41), channel_id=1, source_target_pairs={{0,6},{1,7},{2,4},{3,5},{4,2},{5,3},{6,0},{7,1},{8,14},{9,15},{10,... | collective-permute-start | bytes 688136 | tf_op jit(solution)/shard_map/ppermute | solution.py:36
  34.4 12.1 %collective-permute-start.9 = (f32[7,32,256]{2,1,0:T(8,128)S(1)}, f32[7,32,256]{2,1,0:T(8,128)}, u32[]{:S(2)}, u32[]{:S(2)}) collective-permute-start(f32[7,32,256]{2,1,0:T(8,128)S(1)} %get-tuple-element.42), channel_id=1, source_target_pairs={{0,4},{1,5},{2,6},{3,7},{4,0},{5,1},{6,2},{7,3},{8,12},{9,13},{10,... | collective-permute-start | bytes 688136 | tf_op jit(solution)/shard_map/ppermute | solution.py:36
  47.5 6.7 %collective-permute-start.11 = (f32[7,32,256]{2,1,0:T(8,128)S(1)}, f32[7,32,256]{2,1,0:T(8,128)S(1)}, u32[]{:S(2)}, u32[]{:S(2)}) collective-permute-start(f32[7,32,256]{2,1,0:T(8,128)S(1)} %add_add_fusion), channel_id=1, source_target_pairs={{0,8},{1,9},{2,10},{3,11},{4,12},{5,13},{6,14},{7,15},{8,0},{9,1},... | collective-permute-start | bytes 688136 | tf_op jit(solution)/shard_map/ppermute | solution.py:36
  54.2 7.1 %collective-permute-start.12 = (f32[7,32,256]{2,1,0:T(8,128)S(1)}, f32[7,32,256]{2,1,0:T(8,128)S(1)}, u32[]{:S(2)}, u32[]{:S(2)}) collective-permute-start(f32[7,32,256]{2,1,0:T(8,128)S(1)} %add.57), channel_id=1, source_target_pairs={{0,16},{1,17},{2,18},{3,19},{4,20},{5,21},{6,22},{7,23},{8,24},{9,... | collective-permute-start | bytes 688136 | tf_op jit(solution)/shard_map/ppermute | solution.py:36
  54.3 19.1 %collective-permute-start.2 = (f32[2,256,128]{2,1,0:T(8,128)}, f32[2,256,128]{2,1,0:T(8,128)S(1)}, u32[]{:S(2)}, u32[]{:S(2)}) collective-permute-start(f32[2,256,128]{2,1,0:T(8,128)} %get-tuple-element.26), channel_id=1, source_target_pairs={{0,1},{1,2},{2,3},{4,5},{5,6},{6,7},{8,9},{9,10},{10,11},{12,13},{... | collective-permute-start | bytes 786440 | tf_op jit(solution)/shard_map/ppermute | solution.py:28
  56.3 65.5 %collective-permute-start.1 = (f32[2,896,128]{2,1,0:T(8,128)}, f32[2,896,128]{2,1,0:T(8,128)}, u32[]{:S(2)}, u32[]{:S(2)}) collective-permute-start(f32[2,896,128]{2,1,0:T(8,128)} %get-tuple-element.25), channel_id=1, source_target_pairs={{0,1},{1,2},{2,3},{4,5},{5,6},{6,7},{8,9},{9,10},{10,11},{12,13},{... | collective-permute-start | bytes 2752520 | tf_op jit(solution)/shard_map/ppermute | solution.py:28
  61.4 15.4 %collective-permute-start.15 = (f32[6,32,256]{2,1,0:T(8,128)S(1)}, f32[6,32,256]{2,1,0:T(8,128)S(1)}, u32[]{:S(2)}, u32[]{:S(2)}) collective-permute-start(f32[6,32,256]{2,1,0:T(8,128)S(1)} %fusion.refs_0_), channel_id=1, source_target_pairs={{0,6},{1,7},{2,4},{3,5},{4,2},{5,3},{6,0},{7,1},{8,14},{9,15},{10,... | collective-permute-start | bytes 589832 | tf_op jit(solution)/shard_map/ppermute | solution.py:36
  63.0 4.6 %collective-permute-start = (f32[2,112,128]{2,1,0:T(8,128)}, f32[2,112,128]{2,1,0:T(8,128)S(1)}, u32[]{:S(2)}, u32[]{:S(2)}) collective-permute-start(f32[2,112,128]{2,1,0:T(8,128)} %get-tuple-element.24), channel_id=1, source_target_pairs={{1,0},{2,1},{3,2},{5,4},{6,5},{7,6},{9,8},{10,9},{11,10},{13,12},{... | collective-permute-start | bytes 344072 | tf_op jit(solution)/shard_map/ppermute | solution.py:28
  64.9 31.6 %collective-permute-start.14 = (f32[6,32,256]{2,1,0:T(8,128)S(1)}, f32[6,32,256]{2,1,0:T(8,128)S(1)}, u32[]{:S(2)}, u32[]{:S(2)}) collective-permute-start(f32[6,32,256]{2,1,0:T(8,128)S(1)} %fusion.refs_0_), channel_id=1, source_target_pairs={{0,4},{1,5},{2,6},{3,7},{4,0},{5,1},{6,2},{7,3},{8,12},{9,13},{10,... | collective-permute-start | bytes 589832 | tf_op jit(solution)/shard_map/ppermute | solution.py:36
  67.6 54.2 %copy-start.5 = (f32[2,112,128]{2,1,0:T(8,128)}, f32[2,112,128]{2,1,0:T(8,128)S(1)}, u32[]{:S(2)}) copy-start(f32[2,112,128]{2,1,0:T(8,128)S(1)} %collective-permute-done.trail_block.trail_ref) | copy-start | bytes 344068
  67.6 48.9 %collective-permute-start.6 = (f32[144,896]{1,0:T(8,128)}, f32[144,896]{1,0:T(8,128)S(1)}, u32[]{:S(2)}, u32[]{:S(2)}) collective-permute-start(f32[144,896]{1,0:T(8,128)} %get-tuple-element.31), channel_id=1, source_target_pairs={{0,4},{4,8},{8,12},{12,16},{16,20},{20,24},{24,28},{1,5},{5,9},{9,... | collective-permute-start | bytes 1548296 | tf_op jit(solution)/shard_map/ppermute | solution.py:28
  73.4 48.4 %copy-start.1 = (f32[2,256,128]{2,1,0:T(8,128)}, f32[2,256,128]{2,1,0:T(8,128)S(1)}, u32[]{:S(2)}) copy-start(f32[2,256,128]{2,1,0:T(8,128)S(1)} %collective-permute-done.2.link_block.lead_ref) | copy-start | bytes 786436
  73.4 64.0 %collective-permute-start.5 = (f32[144,896]{1,0:T(8,128)}, f32[144,896]{1,0:T(8,128)S(1)}, u32[]{:S(2)}, u32[]{:S(2)}) collective-permute-start(f32[144,896]{1,0:T(8,128)} %get-tuple-element.30), channel_id=1, source_target_pairs={{0,4},{4,8},{8,12},{12,16},{16,20},{20,24},{24,28},{1,5},{5,9},{9,... | collective-permute-start | bytes 1548296 | tf_op jit(solution)/shard_map/ppermute | solution.py:28
  76.9 24.1 %collective-permute-start.13 = (f32[6,32,256]{2,1,0:T(8,128)S(1)}, f32[6,32,256]{2,1,0:T(8,128)S(1)}, u32[]{:S(2)}, u32[]{:S(2)}) collective-permute-start(f32[6,32,256]{2,1,0:T(8,128)S(1)} %fusion.refs_0_), channel_id=1, source_target_pairs={{0,2},{1,3},{2,0},{3,1},{4,6},{5,7},{6,4},{7,5},{8,10},{9,11},{10,... | collective-permute-start | bytes 589832 | tf_op jit(solution)/shard_map/ppermute | solution.py:36
  96.5 11.8 %collective-permute-start.3 = (f32[2,24,896]{2,1,0:T(8,128)S(1)}, f32[2,24,896]{2,1,0:T(8,128)S(1)}, u32[]{:S(2)}, u32[]{:S(2)}) collective-permute-start(f32[2,24,896]{2,1,0:T(8,128)S(1)} %get-tuple-element.28), channel_id=1, source_target_pairs={{4,0},{8,4},{12,8},{16,12},{20,16},{24,20},{28,24},{5,1},{9,5},{13... | collective-permute-start | bytes 516104 | tf_op jit(solution)/shard_map/ppermute | solution.py:28
  101.6 85.9 %collective-permute-start.16 = (f32[6,128,256]{2,1,0:T(8,128)S(1)}, f32[6,128,256]{2,1,0:T(8,128)S(1)}, u32[]{:S(2)}, u32[]{:S(2)}) collective-permute-start(f32[6,128,256]{2,1,0:T(8,128)S(1)} %join.2.refs_0_), channel_id=1, source_target_pairs={{0,1},{1,0},{2,3},{3,2},{4,5},{5,4},{6,7},{7,6},{8,9},{9,8},{10,11... | collective-permute-start | bytes 2359304 | tf_op jit(solution)/shard_map/ppermute | solution.py:36
  108.3 13.5 %copy-start.6 = (f32[2,24,896]{2,1,0:T(8,128)}, f32[2,24,896]{2,1,0:T(8,128)S(1)}, u32[]{:S(2)}) copy-start(f32[2,24,896]{2,1,0:T(8,128)S(1)} %collective-permute-done.3.below_ref.below_block) | copy-start | bytes 516100
  108.3 8.2 %collective-permute-start.4 = (f32[2,200,128]{2,1,0:T(8,128)S(1)}, f32[2,200,128]{2,1,0:T(8,128)S(1)}, u32[]{:S(2)}, u32[]{:S(2)}) collective-permute-start(f32[2,200,128]{2,1,0:T(8,128)S(1)} %get-tuple-element.29), channel_id=1, source_target_pairs={{0,4},{4,8},{8,12},{12,16},{16,20},{20,24},{24,28},{1,5},{5,9},{9,... | collective-permute-start | bytes 614408 | tf_op jit(solution)/shard_map/ppermute | solution.py:28
  116.5 5.4 %copy-start.4 = (f32[2,200,128]{2,1,0:T(8,128)}, f32[2,200,128]{2,1,0:T(8,128)S(1)}, u32[]{:S(2)}) copy-start(f32[2,200,128]{2,1,0:T(8,128)S(1)} %collective-permute-done.4.corner_ref.corner_block) | copy-start | bytes 614404
  116.5 5.3 %copy-start.2 = (f32[144,896]{1,0:T(8,128)}, f32[144,896]{1,0:T(8,128)S(1)}, u32[]{:S(2)}) copy-start(f32[144,896]{1,0:T(8,128)S(1)} %collective-permute-done.6.above_ref) | copy-start | bytes 1548292
  120.2 1.6 copy-start
  137.4 0.8 copy-start.12
  153.8 7.7 %collective-permute-start.20 = (f32[768,128]{1,0:T(8,128)}, f32[768,128]{1,0:T(8,128)S(1)}, u32[]{:S(2)}, u32[]{:S(2)}) collective-permute-start(f32[768,128]{1,0:T(8,128)} %get-tuple-element.38), channel_id=1, source_target_pairs={{1,0},{2,1},{3,2},{5,4},{6,5},{7,6},{9,8},{10,9},{11,10},{13,12},{... | collective-permute-start | bytes 1179656 | tf_op jit(solution)/shard_map/ppermute | solution.py:28
  155.7 10.1 %collective-permute-start.17 = (f32[768,128]{1,0:T(8,128)}, f32[768,128]{1,0:T(8,128)S(1)}, u32[]{:S(2)}, u32[]{:S(2)}) collective-permute-start(f32[768,128]{1,0:T(8,128)} %get-tuple-element.36), channel_id=1, source_target_pairs={{1,0},{2,1},{3,2},{5,4},{6,5},{7,6},{9,8},{10,9},{11,10},{13,12},{... | collective-permute-start | bytes 1179656 | tf_op jit(solution)/shard_map/ppermute | solution.py:28
  157.7 15.0 %collective-permute-start.22 = (f32[128,768]{1,0:T(8,128)}, f32[128,768]{1,0:T(8,128)S(1)}, u32[]{:S(2)}, u32[]{:S(2)}) collective-permute-start(f32[128,768]{1,0:T(8,128)} %get-tuple-element.39), channel_id=1, source_target_pairs={{4,0},{8,4},{12,8},{16,12},{20,16},{24,20},{28,24},{5,1},{9,5},{13... | collective-permute-start | bytes 1179656 | tf_op jit(solution)/shard_map/ppermute | solution.py:28
  159.6 21.6 %collective-permute-start.19 = (f32[128,768]{1,0:T(8,128)}, f32[128,768]{1,0:T(8,128)}, u32[]{:S(2)}, u32[]{:S(2)}) collective-permute-start(f32[128,768]{1,0:T(8,128)} %get-tuple-element.37), channel_id=1, source_target_pairs={{4,0},{8,4},{12,8},{16,12},{20,16},{24,20},{28,24},{5,1},{9,5},{13... | collective-permute-start | bytes 1179656 | tf_op jit(solution)/shard_map/ppermute | solution.py:28
  161.5 21.9 %copy-start.10 = (f32[768,128]{1,0:T(8,128)}, f32[768,128]{1,0:T(8,128)S(1)}, u32[]{:S(2)}) copy-start(f32[768,128]{1,0:T(8,128)S(1)} %collective-permute-done.20.refs_3_) | copy-start | bytes 1179652
  161.6 20.9 %collective-permute-start.21 = (f32[128,128]{1,0:T(8,128)S(1)}, f32[128,128]{1,0:T(8,128)S(1)}, u32[]{:S(2)}, u32[]{:S(2)}) collective-permute-start(f32[128,128]{1,0:T(8,128)S(1)} %slice.19), channel_id=1, source_target_pairs={{4,0},{8,4},{12,8},{16,12},{20,16},{24,20},{28,24},{5,1},{9,5},{13... | collective-permute-start | bytes 196616 | tf_op jit(solution)/shard_map/ppermute | solution.py:28
  165.9 17.6 %copy-start.11 = (f32[768,128]{1,0:T(8,128)}, f32[768,128]{1,0:T(8,128)S(1)}, u32[]{:S(2)}) copy-start(f32[768,128]{1,0:T(8,128)S(1)} %collective-permute-done.17.refs_0_) | copy-start | bytes 1179652
  165.9 17.5 %collective-permute-start.18 = (f32[128,128]{1,0:T(8,128)S(1)}, f32[128,128]{1,0:T(8,128)S(1)}, u32[]{:S(2)}, u32[]{:S(2)}) collective-permute-start(f32[128,128]{1,0:T(8,128)S(1)} %slice.18), channel_id=1, source_target_pairs={{4,0},{8,4},{12,8},{16,12},{20,16},{24,20},{28,24},{5,1},{9,5},{13... | collective-permute-start | bytes 196616 | tf_op jit(solution)/shard_map/ppermute | solution.py:28
  172.7 10.8 %copy-start.13 = (f32[128,768]{1,0:T(8,128)}, f32[128,768]{1,0:T(8,128)S(1)}, u32[]{:S(2)}) copy-start(f32[128,768]{1,0:T(8,128)S(1)} %collective-permute-done.22.refs_5_) | copy-start | bytes 1179652
  182.5 1.0 copy-start.14
  183.4 0.6 copy-start.15
